TPU v7x, 32 devices: a whole 2x2x4 slice. The times are simulated.
32 devices in a mesh: atom: 4 (over y, x), row: 2 (over core), col: 4 (over z).
Axes of the slice: x: 2, y: 2, z: 4, core: 2. Of those that a mesh axis runs over, the one named last changes fastest.
Arguments:
- codes: bfloat16 [32, 64, 2048], P('row', 'col', 'atom'), may hold values from -1.5 to 1.5
- image: bfloat16 [32, 64, 128], P('row', 'col'), may hold values from -6 to 6
- master: float32 [128, 7, 7, 2048], P(('row', 'col'), None, None, 'atom'), may hold values from -0.078125 to 0.078125
- moment: float32 [128, 7, 7, 2048], P(('row', 'col'), None, None, 'atom'), may hold values from -120 to 120
- second: float32 [128, 7, 7, 2048], P(('row', 'col'), None, None, 'atom'), may hold values from 100 to 4000
Outputs:
- new_codes: bfloat16 [32, 64, 2048], P('row', 'col', 'atom')
- new_dictionary: float32 [128, 7, 7, 2048], P(('row', 'col'), None, None, 'atom')
- new_moment: float32 [128, 7, 7, 2048], P(('row', 'col'), None, None, 'atom')
- new_second: float32 [128, 7, 7, 2048], P(('row', 'col'), None, None, 'atom')
All inputs are finite; a program needn't handle non-finite values.
Results may differ from a plain program's by a relative error of at most 0.007.
Values may be sent and summed in bfloat16 or wider, within the bound.
No kernel may reach another device: no remote copies, remote signals or barrier semaphores. Data moves between devices by JAX's collectives and lax.ppermute only.
A program may use at most 128 MiB of HBM per device.

v0:
```python
import jax
import jax.numpy as jnp
from jax import lax
from jax.sharding import PartitionSpec as P

first_fix = 0.9999734386011124
second_fix = 0.09520785288629038


def extended(cells, sides, width):
    for axis, dim in sides:
        count = lax.axis_size(axis)
        ends = count - 1
        head = lax.slice_in_dim(cells, 0, width, axis=dim)
        tail = lax.slice_in_dim(cells, cells.shape[dim] - width, cells.shape[dim], axis=dim)
        cells = jnp.concatenate(
            [
                lax.ppermute(tail, axis, [(i, (i + 1) % count) for i in range(ends)]),
                cells,
                lax.ppermute(head, axis, [((i + 1) % count, i) for i in range(ends)]),
            ],
            axis=dim,
        )
    return cells


def windows(padded, first, height, width, taps):
    rows = padded[first : first + height]
    return jnp.stack([rows[:, shift : shift + width] for shift in range(taps)], axis=2)


def adam_update(master, moment, second, grad):
    new_moment = 0.9 * moment + 0.1 * grad
    new_second = 0.999 * second + 0.001 * grad * grad
    new_dictionary = master - 0.05 * (new_moment / first_fix) / (
        jnp.sqrt(new_second / second_fix) + 1e-08
    )
    return (new_dictionary, new_moment, new_second)


def adjoint(resid_pad, filters, codes, height, width, taps):
    back = jnp.zeros(codes.shape, jnp.float32)
    for tap_row in range(taps):
        rows = resid_pad[6 - tap_row : 6 - tap_row + height]
        block = jnp.stack([rows[:, 6 - shift : 6 - shift + width] for shift in range(taps)], axis=2)
        back = back + jnp.einsum(
            "ijbc,cbk->ijk", block, filters[:, tap_row], preferred_element_type=jnp.float32
        )
    moved = codes.astype(jnp.float32) - 0.05 * back
    return (moved - jnp.clip(moved, -0.02, 0.02)).astype(jnp.bfloat16)


def correlation(resid, code_pad, height, width, taps):
    tap_terms = []
    for tap_row in range(taps):
        block = windows(code_pad, tap_row, height, width, taps)
        tap_terms.append(
            jnp.einsum("ijc,ijbk->cbk", resid, block, preferred_element_type=jnp.float32)
        )
    return jnp.stack(tap_terms, axis=1)


def local(codes, image, master, moment, second):
    height, width = (codes.shape[0], codes.shape[1])
    taps = master.shape[1]
    filters = lax.all_gather(master.astype(jnp.bfloat16), ("row", "col"), axis=0, tiled=True)
    bands = filters.shape[0]
    code_pad = extended(codes, (("row", 0), ("col", 1)), 3)
    total = jnp.zeros((height, width, bands), jnp.float32)
    for tap_row in range(taps):
        block = windows(code_pad, tap_row, height, width, taps)
        total = total + jnp.einsum(
            "ijbk,cbk->ijc", block, filters[:, tap_row], preferred_element_type=jnp.float32
        )
    total = lax.psum(total.astype(jnp.bfloat16), "atom").astype(jnp.float32)
    resid = (total - image.astype(jnp.float32)).astype(jnp.bfloat16)
    resid_pad = extended(resid, (("row", 0), ("col", 1)), 3)
    new_codes = adjoint(resid_pad, filters, codes, height, width, taps)
    tile_term = correlation(resid, code_pad, height, width, taps)
    half = lax.psum_scatter(tile_term.astype(jnp.bfloat16), "row", scatter_dimension=0, tiled=True)
    grad = lax.psum_scatter(half, "col", scatter_dimension=0, tiled=True).astype(jnp.float32)
    new_dictionary, new_moment, new_second = adam_update(master, moment, second, grad)
    return (new_codes, new_dictionary, new_moment, new_second)


def solution(mesh):
    return jax.shard_map(
        local,
        mesh=mesh,
        in_specs=(
            P("row", "col", "atom"),
            P("row", "col", None),
            P(("row", "col"), None, None, "atom"),
            P(("row", "col"), None, None, "atom"),
            P(("row", "col"), None, None, "atom"),
        ),
        out_specs=(
            P("row", "col", "atom"),
            P(("row", "col"), None, None, "atom"),
            P(("row", "col"), None, None, "atom"),
            P(("row", "col"), None, None, "atom"),
        ),
        check_vma=False,
    )
```

profile of v0, /device:TPU:9, one launch (start us, length us, event | category | flops | bytes accessed | tf_op | source)
XLA Modules:
  0.0 244.5 jit_solution(17898045982416998722)
XLA Ops:
  7.2 2.5 %convert_element_type.26 = bf16[16,7,7,512]{3,0,2,1:T(8,128)(2,1)} convert(f32[16,7,7,512]{3,0,2,1:T(8,128)} %param.7) | non-fusion elementwise | flops 401408 | bytes 2408448 | tf_op jit(solution)/shard_map/convert_element_type | solution.py:66
  11.1 3.0 %collective-permute-start.1 = (bf16[3,16,512]{2,1,0:T(8,128)(2,1)S(1)}, bf16[3,16,512]{2,1,0:T(8,128)(2,1)S(1)}, u32[]{:S(2)}, u32[]{:S(2)}) collective-permute-start(bf16[3,16,512]{2,1,0:T(8,128)(2,1)S(1)} %get-tuple-element.48), channel_id=1, source_target_pairs={{4,0},{5,1},{6,2},{7,3},{12,8},{13,9},{14,10},{15,11},{20,16},{21,... | collective-permute-start | bytes 147464 | tf_op jit(solution)/shard_map/ppermute | solution.py:20
  15.1 3.2 %collective-permute-start.2 = (bf16[22,3,512]{2,1,0:T(4,128)(2,1)S(1)}, bf16[22,3,512]{2,1,0:T(4,128)(2,1)S(1)}, u32[]{:S(2)}, u32[]{:S(2)}) collective-permute-start(bf16[22,3,512]{2,1,0:T(4,128)(2,1)S(1)} %get-tuple-element.41), channel_id=1, source_target_pairs={{0,1},{1,2},{2,3},{4,5},{5,6},{6,7},{8,9},{9,10},{10,11},{12,13},{... | collective-permute-start | bytes 202760 | tf_op jit(solution)/shard_map/ppermute | solution.py:18
  18.3 2.1 collective-permute-start.3
  24.9 3.7 %collective-permute-done.3 = bf16[22,3,512]{2,1,0:T(4,128)(2,1)S(1)} collective-permute-done((bf16[22,3,512]{2,1,0:T(4,128)(2,1)S(1)}, bf16[22,3,512]{2,1,0:T(4,128)(2,1)S(1)}, u32[]{:S(2)}, u32[]{:S(2)}) %collective-permute-start.3) | collective-permute-done | bytes 67616 | tf_op jit(solution)/shard_map/ppermute | solution.py:20
  39.9 37.4 %all-gather.2.cloned.1.call-done = bf16[128,7,7,512]{3,0,2,1:T(8,128)(2,1)} async-done(((bf16[16,7,7,512]{3,0,2,1:T(8,128)(2,1)}), bf16[128,7,7,512]{3,0,2,1:T(8,128)(2,1)}) %all-gather.2.cloned.1.call-update) | async-done | bytes 6422544 | tf_op jit(solution)/shard_map/all_gather | solution.py:66
  77.3 2.5 %convolution_bitcast_fusion.7 = f32[16,16,128]{2,1,0:T(8,128)S(1)} fusion(bf16[16,16,7,512]{3,1,0,2:T(8,128)(2,1)} %get-tuple-element.23, bf16[128,7,7,512]{3,0,2,1:T(8,128)(2,1)} %all-gather.2.cloned.1.call-done), kind=kOutput, calls=%fused_computation.81 | convolution fusion | flops 234881024 | bytes 2883584 | tf_op jit(solution)/shard_map/ijbk,cbk->ijc/dot_general | solution.py:72
  79.8 2.5 %convolution_bitcast_fusion.8 = f32[16,16,128]{2,1,0:T(8,128)S(1)} fusion(bf16[16,16,7,512]{3,1,0,2:T(8,128)(2,1)} %get-tuple-element.35, bf16[128,7,7,512]{3,0,2,1:T(8,128)(2,1)} %all-gather.2.cloned.1.call-done), kind=kOutput, calls=%fused_computation.82 | convolution fusion | flops 234881024 | bytes 2883584 | tf_op jit(solution)/shard_map/ijbk,cbk->ijc/dot_general | solution.py:72
  82.3 2.4 convolution_bitcast_fusion.9
  84.7 2.1 convolution_bitcast_fusion.10
  86.8 2.1 convolution_bitcast_fusion.11
  89.0 2.1 convolution_bitcast_fusion.12
  92.5 41.9 %all-reduce.2.cloned.1.call-done = bf16[16,16,128]{2,1,0:T(8,128)(2,1)} async-done(((bf16[16,16,128]{2,1,0:T(8,128)(2,1)}), bf16[16,16,128]{2,1,0:T(8,128)(2,1)}) %all-reduce.2.cloned.1.call-update) | async-done | bytes 65552 | tf_op jit(solution)/shard_map/psum | solution.py:75
  136.6 3.0 %fusion.3 = bf16[128,7,7,512]{3,0,2,1:T(8,128)(2,1)} fusion(bf16[128,7,7,512]{3,0,2,1:T(8,128)(2,1)} %fusion.15, bf16[16,16,7,512]{3,1,0,2:T(8,128)(2,1)} %get-tuple-element.7, bf16[16,16,128]{2,1,0:T(8,128)(2,1)S(1)} %subtract_convert_fusion), kind=kOutput, calls=%fused_computation.53 | convolution fusion | flops 235339776 | bytes 2818048 | tf_op jit(solution)/shard_map/ijc,ijbk->cbk/dot_general | solution.py:58
  139.5 2.9 %fusion.5 = bf16[128,7,7,512]{3,0,2,1:T(8,128)(2,1)} fusion(bf16[128,7,7,512]{3,0,2,1:T(8,128)(2,1)} %fusion.3, bf16[16,16,7,512]{3,1,0,2:T(8,128)(2,1)} %get-tuple-element.19, bf16[16,16,128]{2,1,0:T(8,128)(2,1)S(1)} %subtract_convert_fusion), kind=kOutput, calls=%fused_computation.55 | convolution fusion | flops 235339776 | bytes 2818048 | tf_op jit(solution)/shard_map/ijc,ijbk->cbk/dot_general | solution.py:58
  142.5 2.9 %fusion.7 = bf16[128,7,7,512]{3,0,2,1:T(8,128)(2,1)} fusion(bf16[128,7,7,512]{3,0,2,1:T(8,128)(2,1)} %fusion.5, bf16[16,16,7,512]{3,1,0,2:T(8,128)(2,1)} %get-tuple-element.33, bf16[16,16,128]{2,1,0:T(8,128)(2,1)S(1)} %subtract_convert_fusion), kind=kOutput, calls=%fused_computation.57 | convolution fusion | flops 235339776 | bytes 2818048 | tf_op jit(solution)/shard_map/ijc,ijbk->cbk/dot_general | solution.py:58
  145.4 2.9 %fusion.9 = bf16[128,7,7,512]{3,0,2,1:T(8,128)(2,1)} fusion(bf16[128,7,7,512]{3,0,2,1:T(8,128)(2,1)} %fusion.7, bf16[16,16,7,512]{3,1,0,2:T(8,128)(2,1)} %get-tuple-element.34, bf16[16,16,128]{2,1,0:T(8,128)(2,1)S(1)} %subtract_convert_fusion), kind=kOutput, calls=%fused_computation.59 | convolution fusion | flops 235339776 | bytes 2818048 | tf_op jit(solution)/shard_map/ijc,ijbk->cbk/dot_general | solution.py:58
  148.2 2.9 %fusion.11 = bf16[128,7,7,512]{3,0,2,1:T(8,128)(2,1)} fusion(bf16[128,7,7,512]{3,0,2,1:T(8,128)(2,1)} %fusion.9, bf16[16,16,7,512]{3,1,0,2:T(8,128)(2,1)} %get-tuple-element.35, bf16[16,16,128]{2,1,0:T(8,128)(2,1)S(1)} %subtract_convert_fusion), kind=kOutput, calls=%fused_computation.61 | convolution fusion | flops 235339776 | bytes 2818048 | tf_op jit(solution)/shard_map/ijc,ijbk->cbk/dot_general | solution.py:58
  151.1 2.9 %fusion.13 = bf16[128,7,7,512]{3,0,2,1:T(8,128)(2,1)} fusion(bf16[128,7,7,512]{3,0,2,1:T(8,128)(2,1)} %fusion.11, bf16[16,16,7,512]{3,1,0,2:T(8,128)(2,1)} %get-tuple-element.23, bf16[16,16,128]{2,1,0:T(8,128)(2,1)S(1)} %subtract_convert_fusion), kind=kOutput, calls=%fused_computation.63 | convolution fusion | flops 235339776 | bytes 2818048 | tf_op jit(solution)/shard_map/ijc,ijbk->cbk/dot_general | solution.py:58
  154.1 15.1 %reduce-scatter.3.cloned.1.call-done = bf16[64,7,7,512]{3,0,2,1:T(8,128)(2,1)} async-done(((bf16[128,7,7,512]{3,0,2,1:T(8,128)(2,1)}), bf16[64,7,7,512]{3,0,2,1:T(8,128)(2,1)}) %reduce-scatter.3.cloned.1.call-update) | async-done | bytes 3211280 | tf_op jit(solution)/shard_map/reduce_scatter | solution.py:80
  169.3 2.3 collective-permute-start.5
  172.8 1.8 collective-permute-done.4
  174.6 3.1 %collective-permute-start.7 = (bf16[22,3,128]{2,1,0:T(4,128)(2,1)S(1)}, bf16[22,3,128]{2,1,0:T(4,128)(2,1)S(1)}, u32[]{:S(2)}, u32[]{:S(2)}) collective-permute-start(bf16[22,3,128]{2,1,0:T(4,128)(2,1)S(1)} %get-tuple-element.94), channel_id=1, source_target_pairs={{0,1},{1,2},{2,3},{4,5},{5,6},{6,7},{8,9},{9,10},{10,11},{12,13},{... | collective-permute-start | bytes 50696 | tf_op jit(solution)/shard_map/ppermute | solution.py:18
  177.7 2.3 collective-permute-start.6
  180.1 4.5 %collective-permute-done.6 = bf16[22,3,128]{2,1,0:T(4,128)(2,1)S(1)} collective-permute-done((bf16[22,3,128]{2,1,0:T(4,128)(2,1)S(1)}, bf16[22,3,128]{2,1,0:T(4,128)(2,1)S(1)}, u32[]{:S(2)}, u32[]{:S(2)}) %collective-permute-start.6) | collective-permute-done | bytes 16928 | tf_op jit(solution)/shard_map/ppermute | solution.py:20
  185.5 1.6 convolution_bitcast_fusion
  187.1 1.6 convolution_bitcast_fusion.1
  190.3 1.6 convolution_bitcast_fusion.3
  193.6 1.6 convolution_bitcast_fusion.5
  195.2 2.6 %fusion.37 = bf16[16,16,512]{2,1,0:T(8,128)(2,1)} fusion(f32[16,16,512]{2,1,0:T(8,128)S(1)} %convolution_bitcast_fusion, f32[16,16,512]{2,1,0:T(8,128)S(1)} %convolution_bitcast_fusion.1, f32[16,16,512]{2,1,0:T(8,128)S(1)} %convolution_bitcast_fusion.2, f32[16,16,512]{2,1,0:T(8,128)S(1)} %convolution_bitcast_fusion.3, ...), kind=kOutput, calls=%fused_computation.146 | convolution fusion | flops 236453888 | bytes 5046272 | tf_op jit(solution)/shard_map/ijbc,cbk->ijk/dot_general | solution.py:46
  197.9 35.4 %reduce-scatter.5.cloned.1.call-done = bf16[16,7,7,512]{3,0,2,1:T(8,128)(2,1)} async-done(((bf16[64,7,7,512]{3,0,2,1:T(8,128)(2,1)}), bf16[16,7,7,512]{3,0,2,1:T(8,128)(2,1)}) %reduce-scatter.5.cloned.1.call-update) | async-done | bytes 802832 | tf_op jit(solution)/shard_map/reduce_scatter | solution.py:81
  233.3 4.7 %divide_subtract_fusion = (f32[16,7,7,512]{3,0,2,1:T(8,128)}, f32[16,7,7,512]{3,0,2,1:T(8,128)}, f32[16,7,7,512]{3,0,2,1:T(8,128)}) fusion(f32[16,7,7,512]{3,0,2,1:T(8,128)S(1)} %copy-done, bf16[16,7,7,512]{3,0,2,1:T(8,128)(2,1)} %reduce-scatter.5.cloned.1.call-done, f32[16,7,7,512]{3,0,2,1:T(8,128)S(1)} %copy-done.2, f32[16,7,7,512]{3,0,2,1:T(8,128)} %param.9), kind=kLoop, calls=%fused_computation.51 | loop fusion | flops 5218304 | bytes 10436608 | tf_op jit(solution)/shard_map/sub | solution.py:35
  (67 shorter events, 27.1 us)
Async XLA Ops:
  7.2 2.6 %copy-start.1 = (bf16[16,16,512]{2,1,0:T(8,128)(2,1)S(1)}, bf16[16,16,512]{2,1,0:T(8,128)(2,1)}, u32[]{:S(2)}) copy-start(bf16[16,16,512]{2,1,0:T(8,128)(2,1)} %param.5) | copy-start | bytes 786436
  7.2 70.1 %all-gather.2.cloned.1.call-start = ((), (), s32[]{:S(2)}) async-start(), calls=%async_computation.2 | async-start | bytes 7225344 | tf_op jit(solution)/shard_map/all_gather | solution.py:66
  9.7 124.6 %all-reduce.2.cloned.1.call-start = ((), (), s32[]{:S(2)}) async-start(), calls=%async_computation.3 | async-start | bytes 131072 | tf_op jit(solution)/shard_map/psum | solution.py:75
  9.8 4.3 %collective-permute-start = (bf16[3,16,512]{2,1,0:T(8,128)(2,1)S(1)}, bf16[3,16,512]{2,1,0:T(8,128)(2,1)S(1)}, u32[]{:S(2)}, u32[]{:S(2)}) collective-permute-start(bf16[3,16,512]{2,1,0:T(8,128)(2,1)S(1)} %get-tuple-element.49), channel_id=1, source_target_pairs={{0,4},{1,5},{2,6},{3,7},{8,12},{9,13},{10,14},{11,15},{16,20},{17,... | collective-permute-start | bytes 147464 | tf_op jit(solution)/shard_map/ppermute | solution.py:18
  11.1 3.9 %collective-permute-start.1 = (bf16[3,16,512]{2,1,0:T(8,128)(2,1)S(1)}, bf16[3,16,512]{2,1,0:T(8,128)(2,1)S(1)}, u32[]{:S(2)}, u32[]{:S(2)}) collective-permute-start(bf16[3,16,512]{2,1,0:T(8,128)(2,1)S(1)} %get-tuple-element.48), channel_id=1, source_target_pairs={{4,0},{5,1},{6,2},{7,3},{12,8},{13,9},{14,10},{15,11},{20,16},{21,... | collective-permute-start | bytes 147464 | tf_op jit(solution)/shard_map/ppermute | solution.py:20
  15.1 5.7 %collective-permute-start.2 = (bf16[22,3,512]{2,1,0:T(4,128)(2,1)S(1)}, bf16[22,3,512]{2,1,0:T(4,128)(2,1)S(1)}, u32[]{:S(2)}, u32[]{:S(2)}) collective-permute-start(bf16[22,3,512]{2,1,0:T(4,128)(2,1)S(1)} %get-tuple-element.41), channel_id=1, source_target_pairs={{0,1},{1,2},{2,3},{4,5},{5,6},{6,7},{8,9},{9,10},{10,11},{12,13},{... | collective-permute-start | bytes 202760 | tf_op jit(solution)/shard_map/ppermute | solution.py:18
  18.3 10.3 %collective-permute-start.3 = (bf16[22,3,512]{2,1,0:T(4,128)(2,1)S(1)}, bf16[22,3,512]{2,1,0:T(4,128)(2,1)S(1)}, u32[]{:S(2)}, u32[]{:S(2)}) collective-permute-start(bf16[22,3,512]{2,1,0:T(4,128)(2,1)S(1)} %get-tuple-element.40), channel_id=1, source_target_pairs={{1,0},{2,1},{3,2},{5,4},{6,5},{7,6},{9,8},{10,9},{11,10},{13,12},{... | collective-permute-start | bytes 202760 | tf_op jit(solution)/shard_map/ppermute | solution.py:20
  77.3 7.4 %copy-start.3 = (bf16[128,7,7,512]{3,0,2,1:T(8,128)(2,1)S(1)}, bf16[128,7,7,512]{3,0,2,1:T(8,128)(2,1)}, u32[]{:S(2)}) copy-start(bf16[128,7,7,512]{3,0,2,1:T(8,128)(2,1)} %all-gather.2.cloned.1.call-done) | copy-start | bytes 19267588
  91.1 43.2 %copy-start.4 = (bf16[16,16,128]{2,1,0:T(8,128)(2,1)S(1)}, bf16[16,16,128]{2,1,0:T(8,128)(2,1)}, u32[]{:S(2)}) copy-start(bf16[16,16,128]{2,1,0:T(8,128)(2,1)} %param.6) | copy-start | bytes 196612
  92.4 76.8 %reduce-scatter.3.cloned.1.call-start = ((), (), s32[]{:S(2)}) async-start(), calls=%async_computation.4 | async-start | bytes 9633792 | tf_op jit(solution)/shard_map/reduce_scatter | solution.py:80
  154.0 79.2 %reduce-scatter.5.cloned.1.call-start = ((), (), s32[]{:S(2)}) async-start(), calls=%async_computation.5 | async-start | bytes 4014080 | tf_op jit(solution)/shard_map/reduce_scatter | solution.py:81
  169.3 3.6 %collective-permute-start.5 = (bf16[3,16,128]{2,1,0:T(8,128)(2,1)S(1)}, bf16[3,16,128]{2,1,0:T(8,128)(2,1)S(1)}, u32[]{:S(2)}, u32[]{:S(2)}) collective-permute-start(bf16[3,16,128]{2,1,0:T(8,128)(2,1)S(1)} %get-tuple-element.106), channel_id=1, source_target_pairs={{4,0},{5,1},{6,2},{7,3},{12,8},{13,9},{14,10},{15,11},{20,16},{21,... | collective-permute-start | bytes 36872 | tf_op jit(solution)/shard_map/ppermute | solution.py:20
  171.5 3.1 %collective-permute-start.4 = (bf16[3,16,128]{2,1,0:T(8,128)(2,1)S(1)}, bf16[3,16,128]{2,1,0:T(8,128)(2,1)S(1)}, u32[]{:S(2)}, u32[]{:S(2)}) collective-permute-start(bf16[3,16,128]{2,1,0:T(8,128)(2,1)S(1)} %get-tuple-element.105), channel_id=1, source_target_pairs={{0,4},{1,5},{2,6},{3,7},{8,12},{9,13},{10,14},{11,15},{16,20},{17,... | collective-permute-start | bytes 36872 | tf_op jit(solution)/shard_map/ppermute | solution.py:18
  174.6 5.5 %collective-permute-start.7 = (bf16[22,3,128]{2,1,0:T(4,128)(2,1)S(1)}, bf16[22,3,128]{2,1,0:T(4,128)(2,1)S(1)}, u32[]{:S(2)}, u32[]{:S(2)}) collective-permute-start(bf16[22,3,128]{2,1,0:T(4,128)(2,1)S(1)} %get-tuple-element.94), channel_id=1, source_target_pairs={{0,1},{1,2},{2,3},{4,5},{5,6},{6,7},{8,9},{9,10},{10,11},{12,13},{... | collective-permute-start | bytes 50696 | tf_op jit(solution)/shard_map/ppermute | solution.py:18
  177.7 6.9 %collective-permute-start.6 = (bf16[22,3,128]{2,1,0:T(4,128)(2,1)S(1)}, bf16[22,3,128]{2,1,0:T(4,128)(2,1)S(1)}, u32[]{:S(2)}, u32[]{:S(2)}) collective-permute-start(bf16[22,3,128]{2,1,0:T(4,128)(2,1)S(1)} %get-tuple-element.95), channel_id=1, source_target_pairs={{1,0},{2,1},{3,2},{5,4},{6,5},{7,6},{9,8},{10,9},{11,10},{13,12},{... | collective-permute-start | bytes 50696 | tf_op jit(solution)/shard_map/ppermute | solution.py:20
  195.2 38.1 %copy-start = (f32[16,7,7,512]{3,0,2,1:T(8,128)S(1)}, f32[16,7,7,512]{3,0,2,1:T(8,128)}, u32[]{:S(2)}) copy-start(f32[16,7,7,512]{3,0,2,1:T(8,128)} %param.7) | copy-start | bytes 4816900
  195.2 38.0 %copy-start.2 = (f32[16,7,7,512]{3,0,2,1:T(8,128)S(1)}, f32[16,7,7,512]{3,0,2,1:T(8,128)}, u32[]{:S(2)}) copy-start(f32[16,7,7,512]{3,0,2,1:T(8,128)} %param.8) | copy-start | bytes 4816900
Sparse Core Ops, SparseCore 0:
  10.2 67.1 all-gather.1
  92.5 41.7 all-reduce.1
  154.2 15.0 reduce-scatter.2
  171.4 61.8 reduce-scatter.4
where the time goes:
time: 248 us; the launch traced here: 244 us
  waiting for transfers between devices  141 us (57%)
  matrix products  46.2 us (19%)
  other arithmetic  21.1 us (9%)
  starting transfers between devices  18.8 us (8%)
  between operations  14.1 us (6%)
  local copies, waits for them, and re-layouts  3.29 us (1%)
    psum x1, waiting for transfers between devices, local(): total = lax.psum(total.astype(jnp.bfloat16), 'atom').astype(jnp.float32)  41.9 us
    all_gather x1, waiting for transfers between devices, local(): lax.all_gather(master.astype(jnp.bfloat16), ('row', 'col'), axis=0, tiled...  37.4 us
    reduce_scatter x1, waiting for transfers between devices, local(): lax.psum_scatter(half, 'col', scatter_dimension=0, tiled=True)  35.4 us
    dot_general x7, matrix products, correlation(): jnp.einsum('ijc,ijbk->cbk', resid, block, preferred_element_type=jnp.floa...  18.8 us
    reduce_scatter x1, waiting for transfers between devices, local(): lax.psum_scatter(tile_term.astype(jnp.bfloat16), 'row', scatter_dimension...  15.1 us
    dot_general x7, matrix products, local(): jnp.einsum('ijbk,cbk->ijc', block, filters[:, tap_row], preferred_element...  15 us
    dot_general x7, matrix products, adjoint(): jnp.einsum('ijbc,cbk->ijk', block, filters[:, tap_row], preferred_element...  12.4 us
    ppermute x4, starting transfers between devices, extended(): lax.ppermute(head, axis, [((i + 1) % count, i) for i in range(ends)])  9.71 us
  transfers between devices with their start and end apart: 12, of which 9 were waited for; matrix products, arithmetic and copies ran while one was open for 12% of the time, Pallas kernels for 0%

commit v1 on v0

v1 whole, which is shorter than its diff:
```python
import functools

import jax
import jax.numpy as jnp
from jax import lax
from jax.experimental import pallas as pl
from jax.experimental.pallas import tpu as pltpu
from jax.sharding import PartitionSpec as P

first_fix = 0.9999734386011124
second_fix = 0.09520785288629038


def shifted(x, axis, step):
    count = lax.axis_size(axis)
    return lax.ppermute(x, axis, [(i, (i + step) % count) for i in range(count)])


def moved_on(x, axis, step):
    count = lax.axis_size(axis)
    return lax.ppermute(x, axis, [(i, i + step) for i in range(count) if 0 <= i + step < count])


def whole(count, *extra):
    return [pl.BlockSpec(memory_space=pltpu.VMEM)] * count + list(extra)


def call(body, outs, args, flops=0, scratch=(), name=None):
    moved = sum(a.size * a.dtype.itemsize for a in args) + sum(o.size * o.dtype.itemsize for o in outs)
    return pl.pallas_call(
        body,
        out_shape=outs,
        in_specs=whole(len(args)),
        out_specs=whole(len(outs)),
        scratch_shapes=list(scratch),
        cost_estimate=pl.CostEstimate(flops=flops, bytes_accessed=moved, transcendentals=0),
        compiler_params=pltpu.CompilerParams(vmem_limit_bytes=60 << 20),
        name=name,
    )(*args)


def roll(x, amount):
    amount %= x.shape[1]
    return pltpu.roll(x, amount, 1) if amount else x


def struct(shape, dtype):
    return jax.ShapeDtypeStruct(shape, dtype)


def column_of(ext, cols):
    return lax.broadcasted_iota(jnp.int32, (1, ext), 1) % cols


def tile_parts(filters, tile, y_ref, taps, bands, ext, cols):
    reach = taps // 2
    y_ref[...] = lax.dot_general(filters, tile, (((1,), (1,)), ((), ())), preferred_element_type=jnp.float32)
    pixels = tile.shape[0]
    column = column_of(ext, cols)
    main = jnp.zeros((bands, ext), jnp.float32)
    to_right = jnp.zeros((bands, ext), jnp.float32)
    to_left = jnp.zeros((bands, ext), jnp.float32)
    tail = jnp.zeros((bands, ext - pixels), jnp.float32)
    for b in range(taps):
        total = None
        for a in range(taps):
            term = jnp.concatenate([y_ref[pl.ds((a * taps + b) * bands, bands), :], tail], axis=1)
            total = term if total is None else roll(total, cols) + term
        step = reach - b
        turned = roll(total, step)
        if step > 0:
            inside = column >= step
            to_right = to_right + jnp.where(inside, 0.0, turned)
        elif step < 0:
            inside = column < cols + step
            to_left = to_left + jnp.where(inside, 0.0, turned)
        main = main + (turned if step == 0 else jnp.where(inside, turned, 0.0))
    return main, roll(to_right, -cols) + roll(to_left, cols)


def early_body(taps, bands, ext, cols, filters_ref, tile_ref, main_ref, spill_ref, y_ref):
    main, spill = tile_parts(filters_ref[...], tile_ref[...], y_ref, taps, bands, ext, cols)
    main_ref[...] = main
    spill_ref[...] = spill


def tile_flags(axis, s):
    count = lax.axis_size(axis)
    place = lax.rem(lax.axis_index(axis) + count - s, count)
    return place > 0, place < count - 1


def late_body(taps, bands, ext, cols, order, share, *refs):
    count = len(order) + 1
    filters_ref, tile_ref = refs[:2]
    mains, spills = refs[2 : 2 + count - 1], refs[1 + count : 2 * count]
    images = refs[2 * count : 3 * count]
    out_ref, y_ref = refs[3 * count], refs[3 * count + 1]
    reach = taps // 2
    main, spill = tile_parts(filters_ref[...], tile_ref[...], y_ref, taps, bands, ext, cols)
    last = (set(range(count)) - set(order)).pop()
    main_of, spill_of = {last: main}, {last: spill}
    for place, s in enumerate(order):
        main_of[s] = mains[place][...]
        spill_of[s] = spills[place][...]
    column = column_of(ext, cols)
    for s in range(count):
        left, right = tile_flags("col", s)
        from_left = jnp.where((column < reach) & left, spill_of[(s + 1) % count], 0.0)
        from_right = jnp.where((column >= cols - reach) & right, spill_of[(s - 1) % count], 0.0)
        picture = images[s][...].astype(jnp.float32) * share
        pad = jnp.zeros((bands, ext - picture.shape[1]), jnp.float32)
        picture = roll(jnp.concatenate([picture, pad], axis=1), reach * cols)
        out_ref[:, s * ext : (s + 1) * ext] = main_of[s] + from_left + from_right - picture


def edges_body(count, ext, pixels, edge, z_ref, up_ref, down_ref):
    lane = lax.broadcasted_iota(jnp.int32, (1, 128), 1)
    for s in range(count):
        up_ref[:, s * 128 : (s + 1) * 128] = jnp.where(lane < edge, z_ref[:, s * ext : s * ext + 128], 0.0)
        down_ref[:, s * 128 : (s + 1) * 128] = z_ref[:, s * ext + pixels : s * ext + pixels + 128]


def join_body(count, ext, pixels, turn, z_ref, below_ref, above_ref, out_ref, send_ref):
    bands = z_ref.shape[0]

    def turned(x, step):
        step %= bands
        return x if step == 0 else jnp.concatenate([x[bands - step :], x[: bands - step]], axis=0)

    for s in range(count):
        at = s * ext
        own = z_ref[:, at : at + ext]
        above = turned(above_ref[:, s * 128 : (s + 1) * 128], turn)
        below = turned(below_ref[:, s * 128 : (s + 1) * 128], -turn)
        out_ref[:, at : at + 128] = own[:, :128] + above
        out_ref[:, at + 128 : at + pixels] = own[:, 128:pixels]
        out_ref[:, at + pixels : at + pixels + 128] = own[:, pixels : pixels + 128] + below
        if pixels + 128 < ext:
            out_ref[:, at + pixels + 128 : at + ext] = own[:, pixels + 128 :]
    send_ref[...] = out_ref[...].astype(jnp.bfloat16)


def resid_windows(taps, bands, ext, rows, cols, count, total, windows_ref):
    reach = taps // 2
    pixels = rows * cols
    line = lax.broadcasted_iota(jnp.int32, (1, ext), 1) // cols
    column = column_of(ext, cols)
    place, places = lax.axis_index("row"), lax.axis_size("row")
    real = ((line >= reach) | (place > 0)) & ((line < rows + reach) | (place < places - 1)) & (line < rows + 2 * reach)
    tiles = [jnp.where(real, total(s), 0.0).astype(jnp.bfloat16).astype(jnp.float32) for s in range(count)]
    for s in range(count):
        left, right = tile_flags("col", s)
        own = tiles[s]
        to_left = jnp.where(left, tiles[(s + 1) % count], 0.0)
        to_right = jnp.where(right, tiles[(s - 1) % count], 0.0)
        for b in range(taps):
            step = b - reach
            if step == 0:
                view = own
            elif step > 0:
                view = jnp.where(column >= step, roll(own, step), roll(to_left, step - cols))
            else:
                view = jnp.where(column < cols + step, roll(own, step), roll(to_right, step + cols))
            for a in range(taps):
                part = roll(view, -cols * (2 * reach - a))[:, :pixels]
                at = (a * taps + b) * bands
                windows_ref[at : at + bands, s * pixels : (s + 1) * pixels] = part.astype(jnp.bfloat16)


def back_body(taps, bands, ext, rows, cols, count, peers, *refs):
    turned_ref, own_ref = refs[:2]
    others = refs[2 : 2 + peers]
    windows_ref = refs[2 + peers]
    outs = refs[3 + peers :]
    pixels = rows * cols

    def total(s):
        value = own_ref[:, s * ext : (s + 1) * ext]
        for other in others:
            value = value + other[:, s * ext : (s + 1) * ext].astype(jnp.float32)
        return value

    resid_windows(taps, bands, ext, rows, cols, count, total, windows_ref)
    for s in range(1, count):
        outs[s - 1][...] = jnp.dot(
            turned_ref[...], windows_ref[:, s * pixels : (s + 1) * pixels], preferred_element_type=jnp.float32
        ).astype(jnp.bfloat16)


def grad_body(count, pixels, *refs):
    windows_ref, turned_ref = refs[:2]
    tiles = refs[2 : 2 + count]
    back_ref, grad_ref = refs[2 + count :]
    total = None
    for s in range(count):
        term = jnp.dot(windows_ref[:, s * pixels : (s + 1) * pixels], tiles[s][...], preferred_element_type=jnp.float32)
        total = term if total is None else total + term
    grad_ref[...] = total
    back_ref[...] = jnp.dot(turned_ref[...], windows_ref[:, :pixels], preferred_element_type=jnp.float32)


def codes_body(*refs):
    codes_ref, back_ref = refs[:2]
    others, out_ref = refs[2:-1], refs[-1]
    back = back_ref[...]
    for other in others:
        back = back + other[...].astype(jnp.float32)
    moved = codes_ref[...].astype(jnp.float32) - 0.05 * back.T
    out_ref[...] = (moved - jnp.clip(moved, -0.02, 0.02)).astype(jnp.bfloat16)


def adam_update(master, moment, second, grad):
    new_moment = 0.9 * moment + 0.1 * grad
    new_second = 0.999 * second + 0.001 * grad * grad
    new_dictionary = master - 0.05 * (new_moment / first_fix) / (
        jnp.sqrt(new_second / second_fix) + 1e-08
    )
    return (new_dictionary, new_moment, new_second)


def local(codes, image, master, moment, second):
    rows, cols, atoms = codes.shape
    own_bands, taps = master.shape[0], master.shape[1]
    groups, count, peers = lax.axis_size("row"), lax.axis_size("col"), lax.axis_size("atom")
    bands = groups * own_bands
    reach = taps // 2
    pixels = rows * cols
    ext = -(-(rows + 2 * reach) * cols // 128) * 128
    row_at, col_at = lax.axis_index("row"), lax.axis_index("col")

    order = sorted(range(1, count), key=lambda s: (abs(count - 2 * s), s))
    tiles = {0: codes.reshape(pixels, atoms)}
    for s in order:
        tiles[s] = shifted(codes, "col", s).reshape(pixels, atoms)

    own_filters = jnp.transpose(master, (1, 2, 0, 3)).reshape(taps * taps, own_bands, atoms).astype(jnp.bfloat16)
    filters = jnp.concatenate([own_filters] + [shifted(own_filters, "row", s) for s in range(1, groups)], axis=1)
    filters = filters.reshape(taps * taps * bands, atoms)
    turned = filters.T

    picture = image.reshape(pixels, groups, count, own_bands).transpose(1, 2, 3, 0)
    picture = jnp.stack([lax.dynamic_index_in_dim(picture, (row_at + groups - s) % groups, 0, False) for s in range(groups)])
    images = []
    for s in range(count):
        piece = lax.dynamic_index_in_dim(picture, (col_at + s) % count, 1, False).reshape(bands, pixels)
        images.append(piece if s == 0 else shifted(piece, "col", s))

    size = (bands, ext)
    y_scratch = [pltpu.VMEM((taps * taps * bands, pixels), jnp.float32)]
    tile_flops = 2 * taps * taps * bands * pixels * atoms
    mains, spills = [], []
    early = [0] + order[:-1]
    for s in early:
        main, spill = call(
            functools.partial(early_body, taps, bands, ext, cols),
            [struct(size, jnp.float32)] * 2,
            [filters, tiles[s]],
            tile_flops,
            y_scratch,
            "synth_early",
        )
        mains.append(main)
        spills.append(spill)
    share = 1.0 / peers
    (part,) = call(
        functools.partial(late_body, taps, bands, ext, cols, tuple(early), share),
        [struct((bands, count * ext), jnp.float32)],
        [filters, tiles[order[-1]], *mains, *spills, *images],
        tile_flops,
        y_scratch,
        "synth_late",
    )
    edge = struct((bands, count * 128), jnp.float32)
    up, down = call(functools.partial(edges_body, count, ext, pixels, 2 * reach * cols), [edge, edge], [part], name="edges")
    below = moved_on(up, "row", -1)
    above = moved_on(down, "row", 1)
    part, send = call(
        functools.partial(join_body, count, ext, pixels, own_bands),
        [struct(part.shape, jnp.float32), struct(part.shape, jnp.bfloat16)],
        [part, below, above],
        name="join",
    )
    if peers <= 4:
        others = [lax.ppermute(send, "atom", [(i, i ^ m) for i in range(peers)]) for m in range(peers - 1, 0, -1)]
    else:
        others = [(lax.psum(send, "atom").astype(jnp.float32) - send.astype(jnp.float32)).astype(jnp.bfloat16)]

    back_shape = struct((atoms, pixels), jnp.bfloat16)
    windows, *backs = call(
        functools.partial(back_body, taps, bands, ext, rows, cols, count, len(others)),
        [struct((taps * taps * bands, count * pixels), jnp.bfloat16)] + [back_shape] * (count - 1),
        [turned, part, *others],
        tile_flops * (count - 1),
        name="back",
    )
    received = [shifted(backs[s - 1], "col", -s) for s in order]
    own_back, grad = call(
        functools.partial(grad_body, count, pixels),
        [struct((atoms, pixels), jnp.float32), struct((taps * taps * bands, atoms), jnp.float32)],
        [windows, turned] + [tiles[s] for s in range(count)],
        tile_flops * (count + 1),
        name="grad",
    )
    grad = grad.reshape(taps * taps, groups, own_bands, atoms)
    own_grad = grad[:, 0]
    for s in range(1, groups):
        own_grad = own_grad + shifted(grad[:, s].astype(jnp.bfloat16), "row", -s).astype(jnp.float32)
    own_grad = jnp.transpose(own_grad.reshape(taps, taps, own_bands, atoms), (2, 0, 1, 3))
    new_dictionary, new_moment, new_second = adam_update(master, moment, second, own_grad)
    (new_codes,) = call(
        codes_body,
        [struct((pixels, atoms), jnp.bfloat16)],
        [codes.reshape(pixels, atoms), own_back, *received],
        name="shrink",
    )
    return (new_codes.reshape(rows, cols, atoms), new_dictionary, new_moment, new_second)


def solution(mesh):
    return jax.shard_map(
        local,
        mesh=mesh,
        in_specs=(
            P("row", "col", "atom"),
            P("row", "col", None),
            P(("row", "col"), None, None, "atom"),
            P(("row", "col"), None, None, "atom"),
            P(("row", "col"), None, None, "atom"),
        ),
        out_specs=(
            P("row", "col", "atom"),
            P(("row", "col"), None, None, "atom"),
            P(("row", "col"), None, None, "atom"),
            P(("row", "col"), None, None, "atom"),
        ),
        check_vma=False,
    )
```

time: 248 us -> 109 us (0.44); the launches traced: 244 us -> 109 us
  waiting for transfers between devices: 141 us -> 36.3 us
  matrix products: 46.2 us -> 0 us
  Pallas kernels: 0 us -> 30.5 us
  between operations: 14.1 us -> 0.83 us
  other arithmetic: 21.1 us -> 10.6 us
  local copies, waits for them, and re-layouts: 3.29 us -> 8.67 us
  starting transfers between devices: 18.8 us -> 21.9 us
    reduce_scatter x2 -> x0, waiting for transfers between devices: 50.5 us -> none  [the longest x1 35.4 us: local(): lax.psum_scatter(half, 'col', scatter_dimension=0, tiled=True)]
    dot_general x21 -> x0, matrix products: 46.2 us -> none  [the longest x7 18.8 us: correlation(): jnp.einsum('ijc,ijbk->cbk', resid, block, preferred_element_type=jnp.floa...]
    psum x1 -> x0, waiting for transfers between devices: 41.9 us -> none  [local(): total = lax.psum(total.astype(jnp.bfloat16), 'atom').astype(jnp.float32)]
    all_gather x1 -> x0, waiting for transfers between devices: 37.4 us -> none  [local(): lax.all_gather(master.astype(jnp.bfloat16), ('row', 'col'), axis=0, tiled...]
    pallas_call x0 -> x9, Pallas kernels: none -> 30.5 us  [call(): pl.pallas_call(body, out_shape=outs, in_specs=whole(len(args)), out_specs...]
    ppermute x8 -> x16, waiting for transfers between devices: 11.2 us -> 36.3 us  [the longest x11 32.2 us: shifted(): lax.ppermute(x, axis, [(i, (i + step) % count) for i in range(count)])]
    unnamed x14 -> x0, other arithmetic: 9.05 us -> none
    another operation x4 -> x1, other arithmetic: 3.95 us -> 0.62 us  [local(): jnp.stack([lax.dynamic_index_in_dim(picture, (row_at + groups - s) % grou...]
  transfers between devices with their start and end apart: 12 -> 16, of which waited for: 9 -> 7; matrix products, arithmetic and copies ran while one was open for 12% -> 6% of each run, Pallas kernels for 0% -> 10%
where the time goes in v1:
time: 109 us
  waiting for transfers between devices  36.3 us (33%)
  Pallas kernels  30.5 us (28%)
  starting transfers between devices  21.9 us (20%)
  other arithmetic  10.6 us (10%)
  local copies, waits for them, and re-layouts  8.67 us (8%)
    ppermute x11, waiting for transfers between devices, shifted(): lax.ppermute(x, axis, [(i, (i + step) % count) for i in range(count)])  32.2 us
    pallas_call x9, Pallas kernels, call(): pl.pallas_call(body, out_shape=outs, in_specs=whole(len(args)), out_specs...  30.5 us
    ppermute x11, starting transfers between devices, shifted(): lax.ppermute(x, axis, [(i, (i + step) % count) for i in range(count)])  14.5 us
    ppermute x2, starting transfers between devices, moved_on(): lax.ppermute(x, axis, [(i, i + step) for i in range(count) if 0 <= i + st...  4.75 us
    sub x1, other arithmetic, adam_update(): master - 0.05 * (new_moment / first_fix) / (jnp.sqrt(new_second / second_...  4.39 us
    unnamed x36, local copies, waits for them, and re-layouts  4.02 us
    ppermute x3, starting transfers between devices, local(): lax.ppermute(send, 'atom', [(i, i ^ m) for i in range(peers)])  2.65 us
    concatenate x1, other arithmetic, local(): jnp.concatenate([own_filters] + [shifted(own_filters, 'row', s) for s in...  2.45 us
  transfers between devices with their start and end apart: 16, of which 7 were waited for; matrix products, arithmetic and copies ran while one was open for 6% of the time, Pallas kernels for 10%

profile of v1, /device:TPU:9, one launch (start us, length us, event | category | flops | bytes accessed | tf_op | source)
XLA Modules:
  0.0 108.7 jit_solution(902819852686549709)
XLA Ops:
  0.7 1.6 %convert_element_type.16 = bf16[16,7,7,512]{3,0,2,1:T(8,128)(2,1)S(1)} convert(f32[16,7,7,512]{3,0,2,1:T(8,128)} %param.7) | non-fusion elementwise | flops 401408 | bytes 2408448 | tf_op jit(solution)/shard_map/convert_element_type | solution.py:237
  2.2 0.7 collective-permute-start
  3.0 1.5 %collective-permute-start.3 = (bf16[16,16,512]{2,1,0:T(8,128)(2,1)S(1)}, bf16[16,16,512]{2,1,0:T(8,128)(2,1)S(1)}, u32[]{:S(2)}, u32[]{:S(2)}) collective-permute-start(bf16[16,16,512]{2,1,0:T(8,128)(2,1)S(1)} %copy-done.4), channel_id=1, source_target_pairs={{0,1},{1,2},{2,3},{3,0},{4,5},{5,6},{6,7},{7,4},{8,9},{9,10},{10,1... | collective-permute-start | bytes 786440 | tf_op jit(solution)/shard_map/ppermute | solution.py:16
  4.5 4.1 %collective-permute-start.2 = (bf16[16,16,512]{2,1,0:T(8,128)(2,1)S(1)}, bf16[16,16,512]{2,1,0:T(8,128)(2,1)S(1)}, u32[]{:S(2)}, u32[]{:S(2)}) collective-permute-start(bf16[16,16,512]{2,1,0:T(8,128)(2,1)S(1)} %copy-done.4), channel_id=1, source_target_pairs={{0,2},{1,3},{2,0},{3,1},{4,6},{5,7},{6,4},{7,5},{8,10},{9,11},{10,... | collective-permute-start | bytes 786440 | tf_op jit(solution)/shard_map/ppermute | solution.py:16
  10.1 1.5 %collective-permute-start.4 = (bf16[32,256]{1,0:T(8,128)(2,1)S(1)}, bf16[32,256]{1,0:T(8,128)(2,1)S(1)}, u32[]{:S(2)}, u32[]{:S(2)}) collective-permute-start(bf16[32,256]{1,0:T(8,128)(2,1)S(1)} %bitcast.54), channel_id=1, source_target_pairs={{0,1},{1,2},{2,3},{3,0},{4,5},{5,6},{6,7},{7,4},{8,9},{9,10},{10,1... | collective-permute-start | bytes 49160 | tf_op jit(solution)/shard_map/ppermute | solution.py:16
  11.5 2.4 %pad_maximum_fusion = bf16[49,32,512]{2,1,0:T(8,128)(2,1)} fusion(bf16[49,16,512]{2,1,0:T(8,128)(2,1)} %collective-permute-done, bf16[49,16,512]{2,1,0:T(8,128)(2,1)S(1)} %bitcast.35), kind=kLoop, calls=%fused_computation.5 | loop fusion | flops 3211264 | bytes 3211264 | tf_op jit(solution)/shard_map/concatenate | solution.py:238
  14.0 4.5 %collective-permute-done.3 = bf16[16,16,512]{2,1,0:T(8,128)(2,1)S(1)} collective-permute-done((bf16[16,16,512]{2,1,0:T(8,128)(2,1)S(1)}, bf16[16,16,512]{2,1,0:T(8,128)(2,1)S(1)}, u32[]{:S(2)}, u32[]{:S(2)}) %collective-permute-start.3) | collective-permute-done | bytes 262176 | tf_op jit(solution)/shard_map/ppermute | solution.py:16
  19.2 3.0 %synth_early.5 = (f32[32,384]{1,0:T(8,128)}, f32[32,384]{1,0:T(8,128)}) custom-call(bf16[1568,512]{1,0:T(8,128)(2,1)} %bitcast.28, bf16[256,512]{1,0:T(8,128)(2,1)} %bitcast.45), custom_call_target="tpu_custom_call" | custom-call | flops 411041792 | bytes 1966080 | tf_op jit(solution)/shard_map/synth_early/pallas_call | solution.py:30
  22.1 5.2 %collective-permute-done.2 = bf16[16,16,512]{2,1,0:T(8,128)(2,1)S(1)} collective-permute-done((bf16[16,16,512]{2,1,0:T(8,128)(2,1)S(1)}, bf16[16,16,512]{2,1,0:T(8,128)(2,1)S(1)}, u32[]{:S(2)}, u32[]{:S(2)}) %collective-permute-start.2) | collective-permute-done | bytes 262176 | tf_op jit(solution)/shard_map/ppermute | solution.py:16
  28.0 3.0 %synth_early.4 = (f32[32,384]{1,0:T(8,128)}, f32[32,384]{1,0:T(8,128)}) custom-call(bf16[1568,512]{1,0:T(8,128)(2,1)} %bitcast.29, bf16[256,512]{1,0:T(8,128)(2,1)} %bitcast.47), custom_call_target="tpu_custom_call" | custom-call | flops 411041792 | bytes 1966080 | tf_op jit(solution)/shard_map/synth_early/pallas_call | solution.py:30
  31.0 3.0 %synth_early.3 = (f32[32,384]{1,0:T(8,128)}, f32[32,384]{1,0:T(8,128)}) custom-call(bf16[1568,512]{1,0:T(8,128)(2,1)} %bitcast.30, bf16[256,512]{1,0:T(8,128)(2,1)} %bitcast.40), custom_call_target="tpu_custom_call" | custom-call | flops 411041792 | bytes 1966080 | tf_op jit(solution)/shard_map/synth_early/pallas_call | solution.py:30
  34.7 3.3 %synth_late.1.z_ref = f32[32,1536]{1,0:T(8,128)} custom-call(bf16[1568,512]{1,0:T(8,128)(2,1)} %bitcast.31, bf16[256,512]{1,0:T(8,128)(2,1)} %bitcast.43, f32[32,384]{1,0:T(8,128)} %get-tuple-element.20.refs_2_, f32[32,384]{1,0:T(8,128)} %get-tuple-element.21.refs_3_, f32[32,384]{1,0:T(8,128)} %get-tuple-element.22.refs_4_, ...), custom_call_target="tpu_custom_call" | custom-call | flops 411041792 | bytes 2424832 | tf_op jit(solution)/shard_map/synth_late/pallas_call | solution.py:30
  38.0 1.6 %edges.1 = (f32[32,512]{1,0:T(8,128)}, f32[32,512]{1,0:T(8,128)}) custom-call(f32[32,1536]{1,0:T(8,128)} %synth_late.1.z_ref), custom_call_target="tpu_custom_call" | custom-call | bytes 327680 | tf_op jit(solution)/shard_map/edges/pallas_call | solution.py:30
  39.6 3.5 %collective-permute-start.7 = (f32[32,512]{1,0:T(8,128)}, f32[32,512]{1,0:T(8,128)S(1)}, u32[]{:S(2)}, u32[]{:S(2)}) collective-permute-start(f32[32,512]{1,0:T(8,128)} %get-tuple-element.26), channel_id=1, source_target_pairs={{4,0},{5,1},{6,2},{7,3},{12,8},{13,9},{14,10},{15,11},{20,16},{21,... | collective-permute-start | bytes 196616 | tf_op jit(solution)/shard_map/ppermute | solution.py:21
  43.0 1.3 %collective-permute-start.8 = (f32[32,512]{1,0:T(8,128)}, f32[32,512]{1,0:T(8,128)S(1)}, u32[]{:S(2)}, u32[]{:S(2)}) collective-permute-start(f32[32,512]{1,0:T(8,128)} %get-tuple-element.27), channel_id=1, source_target_pairs={{0,4},{1,5},{2,6},{3,7},{8,12},{9,13},{10,14},{11,15},{16,20},{17,... | collective-permute-start | bytes 196616 | tf_op jit(solution)/shard_map/ppermute | solution.py:21
  44.4 2.0 %collective-permute-done.8.above_ref = f32[32,512]{1,0:T(8,128)S(1)} collective-permute-done((f32[32,512]{1,0:T(8,128)}, f32[32,512]{1,0:T(8,128)S(1)}, u32[]{:S(2)}, u32[]{:S(2)}) %collective-permute-start.8) | collective-permute-done | bytes 65568 | tf_op jit(solution)/shard_map/ppermute | solution.py:21
  47.0 1.7 %join.1 = (f32[32,1536]{1,0:T(8,128)}, bf16[32,1536]{1,0:T(8,128)(2,1)}) custom-call(f32[32,1536]{1,0:T(8,128)} %synth_late.1.z_ref, f32[32,512]{1,0:T(8,128)} %copy-done.9, f32[32,512]{1,0:T(8,128)} %copy-done.10), custom_call_target="tpu_custom_call" | custom-call | bytes 622592 | tf_op jit(solution)/shard_map/join/pallas_call | solution.py:30
  48.7 1.2 %collective-permute-start.11 = (bf16[32,1536]{1,0:T(8,128)(2,1)}, bf16[32,1536]{1,0:T(8,128)(2,1)S(1)}, u32[]{:S(2)}, u32[]{:S(2)}) collective-permute-start(bf16[32,1536]{1,0:T(8,128)(2,1)} %get-tuple-element.29), channel_id=1, source_target_pairs={{0,8},{8,0},{16,24},{24,16},{1,9},{9,1},{17,25},{25,17},{2,10},{10... | collective-permute-start | bytes 294920 | tf_op jit(solution)/shard_map/ppermute | solution.py:285
  50.0 1.2 %collective-permute-start.10 = (bf16[32,1536]{1,0:T(8,128)(2,1)}, bf16[32,1536]{1,0:T(8,128)(2,1)S(1)}, u32[]{:S(2)}, u32[]{:S(2)}) collective-permute-start(bf16[32,1536]{1,0:T(8,128)(2,1)} %get-tuple-element.29), channel_id=1, source_target_pairs={{0,16},{8,24},{16,0},{24,8},{1,17},{9,25},{17,1},{25,9},{2,18},{10... | collective-permute-start | bytes 294920 | tf_op jit(solution)/shard_map/ppermute | solution.py:285
  51.4 2.4 %copy.18 = bf16[1568,512]{0,1:T(8,128)(2,1)} copy(bf16[1568,512]{1,0:T(8,128)(2,1)S(1)} %bitcast.32) | data formatting | bytes 3211264 | tf_op jit(solution)/shard_map/reshape | solution.py:239
  54.1 1.7 %collective-permute-done.9.refs_2_ = bf16[32,1536]{1,0:T(8,128)(2,1)S(1)} collective-permute-done((bf16[32,1536]{1,0:T(8,128)(2,1)}, bf16[32,1536]{1,0:T(8,128)(2,1)S(1)}, u32[]{:S(2)}, u32[]{:S(2)}) %collective-permute-start.9) | collective-permute-done | bytes 98336 | tf_op jit(solution)/shard_map/ppermute | solution.py:285
  56.4 5.9 %back.1 = (bf16[1568,1024]{1,0:T(8,128)(2,1)}, bf16[512,256]{1,0:T(8,128)(2,1)}, bf16[512,256]{1,0:T(8,128)(2,1)}, bf16[512,256]{1,0:T(8,128)(2,1)}) custom-call(bf16[512,1568]{1,0:T(8,128)(2,1)} %bitcast.38, f32[32,1536]{1,0:T(8,128)} %get-tuple-element.28.refs_1_, bf16[32,1536]{1,0:T(8,128)(2,1)} %copy-done.16, bf16[32,1536]{1,0:T(8,128)(2,1)} %copy-done.15, ...), custom_call_target="tpu_custom_call" | custom-call | flops 1233125376 | bytes 6094848 | tf_op jit(solution)/shard_map/back/pallas_call | solution.py:30
  62.4 6.8 %grad.1 = (f32[512,256]{1,0:T(8,128)}, f32[1568,512]{1,0:T(8,128)}) custom-call(bf16[1568,1024]{1,0:T(8,128)(2,1)} %get-tuple-element.30.refs_0_, bf16[512,1568]{1,0:T(8,128)(2,1)} %bitcast.39, bf16[256,512]{1,0:T(8,128)(2,1)} %bitcast.41, bf16[256,512]{1,0:T(8,128)(2,1)} %bitcast.46, bf16[256,512]{1,0:T(8,128)(2,1)} %bitcast.48, bf16[256,512]{1,0:T(8,128)(2,1)} %bitcast.44), custom_call_target="tpu_custom_call" | custom-call | flops 2055208960 | bytes 9601024 | tf_op jit(solution)/shard_map/grad/pallas_call | solution.py:30
  69.2 1.7 %fusion.2 = bf16[49,16,512]{2,1,0:T(8,128)(2,1)S(1)} fusion(f32[49,2,16,512]{3,2,1,0:T(8,128)} %bitcast.36), kind=kLoop, calls=%fused_computation.8 | loop fusion | bytes 1605632 | tf_op jit(solution)/shard_map/convert_element_type | solution.py:308
  70.9 1.9 %collective-permute-start.15 = (bf16[49,16,512]{2,1,0:T(8,128)(2,1)S(1)}, bf16[49,16,512]{2,1,0:T(8,128)(2,1)}, u32[]{:S(2)}, u32[]{:S(2)}) collective-permute-start(bf16[49,16,512]{2,1,0:T(8,128)(2,1)S(1)} %fusion.2), channel_id=1, source_target_pairs={{0,4},{4,0},{1,5},{5,1},{2,6},{6,2},{3,7},{7,3},{8,12},{12,8},{9,1... | collective-permute-start | bytes 2408456 | tf_op jit(solution)/shard_map/ppermute | solution.py:16
  72.8 3.1 %collective-permute-start.12 = (bf16[512,256]{1,0:T(8,128)(2,1)}, bf16[512,256]{1,0:T(8,128)(2,1)}, u32[]{:S(2)}, u32[]{:S(2)}) collective-permute-start(bf16[512,256]{1,0:T(8,128)(2,1)} %get-tuple-element.32), channel_id=1, source_target_pairs={{0,2},{1,3},{2,0},{3,1},{4,6},{5,7},{6,4},{7,5},{8,10},{9,11},{10,... | collective-permute-start | bytes 786440 | tf_op jit(solution)/shard_map/ppermute | solution.py:16
  75.9 1.5 %collective-permute-start.14 = (bf16[512,256]{1,0:T(8,128)(2,1)}, bf16[512,256]{1,0:T(8,128)(2,1)}, u32[]{:S(2)}, u32[]{:S(2)}) collective-permute-start(bf16[512,256]{1,0:T(8,128)(2,1)} %get-tuple-element.34), channel_id=1, source_target_pairs={{0,1},{1,2},{2,3},{3,0},{4,5},{5,6},{6,7},{7,4},{8,9},{9,10},{10,1... | collective-permute-start | bytes 786440 | tf_op jit(solution)/shard_map/ppermute | solution.py:16
  77.4 14.8 %collective-permute-done.12.refs_2_ = bf16[512,256]{1,0:T(8,128)(2,1)} collective-permute-done((bf16[512,256]{1,0:T(8,128)(2,1)}, bf16[512,256]{1,0:T(8,128)(2,1)}, u32[]{:S(2)}, u32[]{:S(2)}) %collective-permute-start.12) | collective-permute-done | bytes 262176 | tf_op jit(solution)/shard_map/ppermute | solution.py:16
  92.1 7.8 %collective-permute-done.13.refs_3_ = bf16[512,256]{1,0:T(8,128)(2,1)} collective-permute-done((bf16[512,256]{1,0:T(8,128)(2,1)}, bf16[512,256]{1,0:T(8,128)(2,1)}, u32[]{:S(2)}, u32[]{:S(2)}) %collective-permute-start.13) | collective-permute-done | bytes 262176 | tf_op jit(solution)/shard_map/ppermute | solution.py:16
  99.9 2.3 %shrink.1 = bf16[256,512]{1,0:T(8,128)(2,1)} custom-call(bf16[256,512]{1,0:T(8,128)(2,1)} %bitcast.42, f32[512,256]{1,0:T(8,128)} %get-tuple-element.31.refs_1_, bf16[512,256]{1,0:T(8,128)(2,1)} %collective-permute-done.12.refs_2_, bf16[512,256]{1,0:T(8,128)(2,1)} %collective-permute-done.13.refs_3_, bf16[512,256]{1,0:T(8,128)(2,1)} %collective-permute-done.14.refs_4_), custom_call_target="tpu_custom_call" | custom-call | bytes 1835008 | tf_op jit(solution)/shard_map/shrink/pallas_call | solution.py:30
  102.2 1.5 %fusion.1 = f32[49,16,512]{2,1,0:T(8,128)S(1)} fusion(f32[49,2,16,512]{3,2,1,0:T(8,128)S(1)} %bitcast.37, bf16[49,16,512]{2,1,0:T(8,128)(2,1)} %collective-permute-done.15), kind=kLoop, calls=%fused_computation.4 | loop fusion | flops 802816 | bytes 4014080 | tf_op jit(solution)/shard_map/add | solution.py:308
  104.4 4.4 %divide_subtract_fusion = (f32[16,7,7,512]{3,0,2,1:T(8,128)}, f32[16,7,7,512]{3,0,2,1:T(8,128)}, f32[16,7,7,512]{3,0,2,1:T(8,128)}) fusion(f32[16,7,7,512]{3,0,2,1:T(8,128)S(1)} %copy-done.1, f32[16,7,7,512]{3,0,2,1:T(8,128)S(1)} %bitcast.33, f32[16,7,7,512]{3,0,2,1:T(8,128)S(1)} %copy-done.3, f32[16,7,7,512]{3,0,2,1:T(8,128)} %param.9), kind=kLoop, calls=%fused_computation.6 | loop fusion | flops 4816896 | bytes 11239424 | tf_op jit(solution)/shard_map/sub | solution.py:216
  (54 shorter events, 5.9 us)
Async XLA Ops:
  0.6 2.4 %copy-start.4 = (bf16[16,16,512]{2,1,0:T(8,128)(2,1)S(1)}, bf16[16,16,512]{2,1,0:T(8,128)(2,1)}, u32[]{:S(2)}) copy-start(bf16[16,16,512]{2,1,0:T(8,128)(2,1)} %param.5) | copy-start | bytes 786436
  0.6 7.9 %copy-start.8 = (bf16[16,16,128]{2,1,0:T(8,128)(2,1)S(1)}, bf16[16,16,128]{2,1,0:T(8,128)(2,1)}, u32[]{:S(2)}) copy-start(bf16[16,16,128]{2,1,0:T(8,128)(2,1)} %param.6) | copy-start | bytes 196612
  2.2 7.8 %collective-permute-start = (bf16[49,16,512]{2,1,0:T(8,128)(2,1)S(1)}, bf16[49,16,512]{2,1,0:T(8,128)(2,1)}, u32[]{:S(2)}, u32[]{:S(2)}) collective-permute-start(bf16[49,16,512]{2,1,0:T(8,128)(2,1)S(1)} %bitcast.34), channel_id=1, source_target_pairs={{0,4},{4,0},{1,5},{5,1},{2,6},{6,2},{3,7},{7,3},{8,12},{12,8},{9,1... | collective-permute-start | bytes 2408456 | tf_op jit(solution)/shard_map/ppermute | solution.py:16
  3.0 31.0 %collective-permute-start.1 = (bf16[16,16,512]{2,1,0:T(8,128)(2,1)S(1)}, bf16[16,16,512]{2,1,0:T(8,128)(2,1)S(1)}, u32[]{:S(2)}, u32[]{:S(2)}) collective-permute-start(bf16[16,16,512]{2,1,0:T(8,128)(2,1)S(1)} %copy-done.4), channel_id=1, source_target_pairs={{0,3},{1,0},{2,1},{3,2},{4,7},{5,4},{6,5},{7,6},{8,11},{9,8},{10,9... | collective-permute-start | bytes 786440 | tf_op jit(solution)/shard_map/ppermute | solution.py:16
  3.0 15.5 %collective-permute-start.3 = (bf16[16,16,512]{2,1,0:T(8,128)(2,1)S(1)}, bf16[16,16,512]{2,1,0:T(8,128)(2,1)S(1)}, u32[]{:S(2)}, u32[]{:S(2)}) collective-permute-start(bf16[16,16,512]{2,1,0:T(8,128)(2,1)S(1)} %copy-done.4), channel_id=1, source_target_pairs={{0,1},{1,2},{2,3},{3,0},{4,5},{5,6},{6,7},{7,4},{8,9},{9,10},{10,1... | collective-permute-start | bytes 786440 | tf_op jit(solution)/shard_map/ppermute | solution.py:16
  4.5 22.9 %collective-permute-start.2 = (bf16[16,16,512]{2,1,0:T(8,128)(2,1)S(1)}, bf16[16,16,512]{2,1,0:T(8,128)(2,1)S(1)}, u32[]{:S(2)}, u32[]{:S(2)}) collective-permute-start(bf16[16,16,512]{2,1,0:T(8,128)(2,1)S(1)} %copy-done.4), channel_id=1, source_target_pairs={{0,2},{1,3},{2,0},{3,1},{4,6},{5,7},{6,4},{7,5},{8,10},{9,11},{10,... | collective-permute-start | bytes 786440 | tf_op jit(solution)/shard_map/ppermute | solution.py:16
  10.0 23.9 %collective-permute-start.6 = (bf16[32,256]{1,0:T(8,128)(2,1)S(1)}, bf16[32,256]{1,0:T(8,128)(2,1)S(1)}, u32[]{:S(2)}, u32[]{:S(2)}) collective-permute-start(bf16[32,256]{1,0:T(8,128)(2,1)S(1)} %bitcast.55), channel_id=1, source_target_pairs={{0,3},{1,0},{2,1},{3,2},{4,7},{5,4},{6,5},{7,6},{8,11},{9,8},{10,9... | collective-permute-start | bytes 49160 | tf_op jit(solution)/shard_map/ppermute | solution.py:16
  10.1 23.9 %collective-permute-start.4 = (bf16[32,256]{1,0:T(8,128)(2,1)S(1)}, bf16[32,256]{1,0:T(8,128)(2,1)S(1)}, u32[]{:S(2)}, u32[]{:S(2)}) collective-permute-start(bf16[32,256]{1,0:T(8,128)(2,1)S(1)} %bitcast.54), channel_id=1, source_target_pairs={{0,1},{1,2},{2,3},{3,0},{4,5},{5,6},{6,7},{7,4},{8,9},{9,10},{10,1... | collective-permute-start | bytes 49160 | tf_op jit(solution)/shard_map/ppermute | solution.py:16
  18.5 0.7 copy-start.6
  18.5 15.5 %collective-permute-start.5 = (bf16[32,256]{1,0:T(8,128)(2,1)S(1)}, bf16[32,256]{1,0:T(8,128)(2,1)S(1)}, u32[]{:S(2)}, u32[]{:S(2)}) collective-permute-start(bf16[32,256]{1,0:T(8,128)(2,1)S(1)} %bitcast.53), channel_id=1, source_target_pairs={{0,2},{1,3},{2,0},{3,1},{4,6},{5,7},{6,4},{7,5},{8,10},{9,11},{10,... | collective-permute-start | bytes 49160 | tf_op jit(solution)/shard_map/ppermute | solution.py:16
  27.3 0.7 copy-start.7
  34.0 17.4 %copy-start = (bf16[49,32,512]{2,1,0:T(8,128)(2,1)S(1)}, bf16[49,32,512]{2,1,0:T(8,128)(2,1)}, u32[]{:S(2)}) copy-start(bf16[49,32,512]{2,1,0:T(8,128)(2,1)} %pad_maximum_fusion) | copy-start | bytes 4816900
  34.0 0.6 copy-start.11
  34.0 0.6 copy-start.13
  34.0 0.7 copy-start.5
  39.6 4.8 %collective-permute-start.7 = (f32[32,512]{1,0:T(8,128)}, f32[32,512]{1,0:T(8,128)S(1)}, u32[]{:S(2)}, u32[]{:S(2)}) collective-permute-start(f32[32,512]{1,0:T(8,128)} %get-tuple-element.26), channel_id=1, source_target_pairs={{4,0},{5,1},{6,2},{7,3},{12,8},{13,9},{14,10},{15,11},{20,16},{21,... | collective-permute-start | bytes 196616 | tf_op jit(solution)/shard_map/ppermute | solution.py:21
  43.0 3.4 %collective-permute-start.8 = (f32[32,512]{1,0:T(8,128)}, f32[32,512]{1,0:T(8,128)S(1)}, u32[]{:S(2)}, u32[]{:S(2)}) collective-permute-start(f32[32,512]{1,0:T(8,128)} %get-tuple-element.27), channel_id=1, source_target_pairs={{0,4},{1,5},{2,6},{3,7},{8,12},{9,13},{10,14},{11,15},{16,20},{17,... | collective-permute-start | bytes 196616 | tf_op jit(solution)/shard_map/ppermute | solution.py:21
  44.4 2.1 %copy-start.9 = (f32[32,512]{1,0:T(8,128)}, f32[32,512]{1,0:T(8,128)S(1)}, u32[]{:S(2)}) copy-start(f32[32,512]{1,0:T(8,128)S(1)} %collective-permute-done.7.below_ref) | copy-start | bytes 196612
  46.4 0.6 copy-start.10
  48.7 5.1 %collective-permute-start.11 = (bf16[32,1536]{1,0:T(8,128)(2,1)}, bf16[32,1536]{1,0:T(8,128)(2,1)S(1)}, u32[]{:S(2)}, u32[]{:S(2)}) collective-permute-start(bf16[32,1536]{1,0:T(8,128)(2,1)} %get-tuple-element.29), channel_id=1, source_target_pairs={{0,8},{8,0},{16,24},{24,16},{1,9},{9,1},{17,25},{25,17},{2,10},{10... | collective-permute-start | bytes 294920 | tf_op jit(solution)/shard_map/ppermute | solution.py:285
  50.0 4.1 %collective-permute-start.10 = (bf16[32,1536]{1,0:T(8,128)(2,1)}, bf16[32,1536]{1,0:T(8,128)(2,1)S(1)}, u32[]{:S(2)}, u32[]{:S(2)}) collective-permute-start(bf16[32,1536]{1,0:T(8,128)(2,1)} %get-tuple-element.29), channel_id=1, source_target_pairs={{0,16},{8,24},{16,0},{24,8},{1,17},{9,25},{17,1},{25,9},{2,18},{10... | collective-permute-start | bytes 294920 | tf_op jit(solution)/shard_map/ppermute | solution.py:285
  51.2 4.6 %collective-permute-start.9 = (bf16[32,1536]{1,0:T(8,128)(2,1)}, bf16[32,1536]{1,0:T(8,128)(2,1)S(1)}, u32[]{:S(2)}, u32[]{:S(2)}) collective-permute-start(bf16[32,1536]{1,0:T(8,128)(2,1)} %get-tuple-element.29), channel_id=1, source_target_pairs={{0,24},{8,16},{16,8},{24,0},{1,25},{9,17},{17,9},{25,1},{2,26},{10... | collective-permute-start | bytes 294920 | tf_op jit(solution)/shard_map/ppermute | solution.py:285
  53.8 2.0 %copy-start.14 = (bf16[32,1536]{1,0:T(8,128)(2,1)}, bf16[32,1536]{1,0:T(8,128)(2,1)S(1)}, u32[]{:S(2)}) copy-start(bf16[32,1536]{1,0:T(8,128)(2,1)S(1)} %collective-permute-done.11.refs_4_) | copy-start | bytes 294916
  54.1 1.7 %copy-start.15 = (bf16[32,1536]{1,0:T(8,128)(2,1)}, bf16[32,1536]{1,0:T(8,128)(2,1)S(1)}, u32[]{:S(2)}) copy-start(bf16[32,1536]{1,0:T(8,128)(2,1)S(1)} %collective-permute-done.10.refs_3_) | copy-start | bytes 294916
  55.8 0.6 copy-start.16
  69.2 33.1 %copy-start.2 = (f32[1568,512]{1,0:T(8,128)S(1)}, f32[1568,512]{1,0:T(8,128)}, u32[]{:S(2)}) copy-start(f32[1568,512]{1,0:T(8,128)} %get-tuple-element.35) | copy-start | bytes 9633796
  70.9 31.3 %collective-permute-start.15 = (bf16[49,16,512]{2,1,0:T(8,128)(2,1)S(1)}, bf16[49,16,512]{2,1,0:T(8,128)(2,1)}, u32[]{:S(2)}, u32[]{:S(2)}) collective-permute-start(bf16[49,16,512]{2,1,0:T(8,128)(2,1)S(1)} %fusion.2), channel_id=1, source_target_pairs={{0,4},{4,0},{1,5},{5,1},{2,6},{6,2},{3,7},{7,3},{8,12},{12,8},{9,1... | collective-permute-start | bytes 2408456 | tf_op jit(solution)/shard_map/ppermute | solution.py:16
  72.8 19.3 %collective-permute-start.12 = (bf16[512,256]{1,0:T(8,128)(2,1)}, bf16[512,256]{1,0:T(8,128)(2,1)}, u32[]{:S(2)}, u32[]{:S(2)}) collective-permute-start(bf16[512,256]{1,0:T(8,128)(2,1)} %get-tuple-element.32), channel_id=1, source_target_pairs={{0,2},{1,3},{2,0},{3,1},{4,6},{5,7},{6,4},{7,5},{8,10},{9,11},{10,... | collective-permute-start | bytes 786440 | tf_op jit(solution)/shard_map/ppermute | solution.py:16
  75.9 24.0 %collective-permute-start.13 = (bf16[512,256]{1,0:T(8,128)(2,1)}, bf16[512,256]{1,0:T(8,128)(2,1)}, u32[]{:S(2)}, u32[]{:S(2)}) collective-permute-start(bf16[512,256]{1,0:T(8,128)(2,1)} %get-tuple-element.33), channel_id=1, source_target_pairs={{0,3},{1,0},{2,1},{3,2},{4,7},{5,4},{6,5},{7,6},{8,11},{9,8},{10,9... | collective-permute-start | bytes 786440 | tf_op jit(solution)/shard_map/ppermute | solution.py:16
  75.9 24.0 %collective-permute-start.14 = (bf16[512,256]{1,0:T(8,128)(2,1)}, bf16[512,256]{1,0:T(8,128)(2,1)}, u32[]{:S(2)}, u32[]{:S(2)}) collective-permute-start(bf16[512,256]{1,0:T(8,128)(2,1)} %get-tuple-element.34), channel_id=1, source_target_pairs={{0,1},{1,2},{2,3},{3,0},{4,5},{5,6},{6,7},{7,4},{8,9},{9,10},{10,1... | collective-permute-start | bytes 786440 | tf_op jit(solution)/shard_map/ppermute | solution.py:16
  102.2 1.7 %copy-start.1 = (f32[16,7,7,512]{3,0,2,1:T(8,128)S(1)}, f32[16,7,7,512]{3,0,2,1:T(8,128)}, u32[]{:S(2)}) copy-start(f32[16,7,7,512]{3,0,2,1:T(8,128)} %param.7) | copy-start | bytes 4816900
  102.2 2.1 %copy-start.3 = (f32[16,7,7,512]{3,0,2,1:T(8,128)S(1)}, f32[16,7,7,512]{3,0,2,1:T(8,128)}, u32[]{:S(2)}) copy-start(f32[16,7,7,512]{3,0,2,1:T(8,128)} %param.8) | copy-start | bytes 4816900
  (1 other events, 0.6 us)

commit v2 on v1

v2 whole, which is shorter than its diff:
```python
import functools

import jax
import jax.numpy as jnp
from jax import lax
from jax.experimental import pallas as pl
from jax.experimental.pallas import tpu as pltpu
from jax.sharding import PartitionSpec as P


first_fix = 0.9999734386011124
second_fix = 0.09520785288629038


def shifted(x, axis, step):
    count = lax.axis_size(axis)
    return lax.ppermute(x, axis, [(i, (i + step) % count) for i in range(count)])


def moved_on(x, axis, step):
    count = lax.axis_size(axis)
    return lax.ppermute(x, axis, [(i, i + step) for i in range(count) if 0 <= i + step < count])


def call(body, outs, args, flops=0, scratch=()):
    moved = sum(a.size * a.dtype.itemsize for a in args) + sum(o.size * o.dtype.itemsize for o in outs)
    return pl.pallas_call(
        body,
        out_shape=outs,
        in_specs=[pl.BlockSpec(memory_space=pltpu.VMEM)] * len(args),
        out_specs=[pl.BlockSpec(memory_space=pltpu.VMEM)] * len(outs),
        scratch_shapes=list(scratch),
        cost_estimate=pl.CostEstimate(flops=flops, bytes_accessed=moved, transcendentals=0),
        compiler_params=pltpu.CompilerParams(vmem_limit_bytes=24 << 20),
    )(*args)


def roll(x, amount):
    amount %= x.shape[1]
    return pltpu.roll(x, amount, 1) if amount else x


def struct(shape, dtype):
    return jax.ShapeDtypeStruct(shape, dtype)


def column_of(ext, cols):
    return lax.broadcasted_iota(jnp.int32, (1, ext), 1) % cols


def tile_parts(filters, tile, y_ref, taps, bands, ext, cols):
    reach = taps // 2
    y_ref[...] = lax.dot_general(filters, tile, (((1,), (1,)), ((), ())), preferred_element_type=jnp.float32)
    pixels = tile.shape[0]
    column = column_of(ext, cols)
    main = jnp.zeros((bands, ext), jnp.float32)
    to_right = jnp.zeros((bands, ext), jnp.float32)
    to_left = jnp.zeros((bands, ext), jnp.float32)
    tail = jnp.zeros((bands, ext - pixels), jnp.float32)
    for b in range(taps):
        total = None
        for a in range(taps):
            term = jnp.concatenate([y_ref[pl.ds((a * taps + b) * bands, bands), :], tail], axis=1)
            total = term if total is None else roll(total, cols) + term
        step = reach - b
        turned = roll(total, step)
        if step > 0:
            inside = column >= step
            to_right = to_right + jnp.where(inside, 0.0, turned)
        elif step < 0:
            inside = column < cols + step
            to_left = to_left + jnp.where(inside, 0.0, turned)
        main = main + (turned if step == 0 else jnp.where(inside, turned, 0.0))
    return main, roll(to_right, -cols) + roll(to_left, cols)


def early_body(taps, bands, ext, cols, filters_ref, tile_ref, main_ref, spill_ref, y_ref):
    main, spill = tile_parts(filters_ref[...], tile_ref[...], y_ref, taps, bands, ext, cols)
    main_ref[...] = main
    spill_ref[...] = spill


def tile_flags(axis, s):
    count = lax.axis_size(axis)
    place = lax.rem(lax.axis_index(axis) + count - s, count)
    return place > 0, place < count - 1


def late_body(taps, bands, ext, cols, pixels, order, share, *refs):
    count = len(order) + 1
    filters_ref, tile_ref = refs[:2]
    mains, spills = refs[2 : 1 + count], refs[1 + count : 2 * count]
    images = refs[2 * count : 3 * count]
    out_ref, *edge_refs, y_ref = refs[3 * count :]
    reach = taps // 2
    main, spill = tile_parts(filters_ref[...], tile_ref[...], y_ref, taps, bands, ext, cols)
    last = (set(range(count)) - set(order)).pop()
    main_of, spill_of = {last: main}, {last: spill}
    for place, s in enumerate(order):
        main_of[s] = mains[place][...]
        spill_of[s] = spills[place][...]
    column = column_of(ext, cols)
    lane = lax.broadcasted_iota(jnp.int32, (1, 128), 1)
    for s in range(count):
        left, right = tile_flags("col", s)
        from_left = jnp.where((column < reach) & left, spill_of[(s + 1) % count], 0.0)
        from_right = jnp.where((column >= cols - reach) & right, spill_of[(s - 1) % count], 0.0)
        picture = images[s][...].astype(jnp.float32) * share
        pad = jnp.zeros((bands, ext - picture.shape[1]), jnp.float32)
        picture = roll(jnp.concatenate([picture, pad], axis=1), reach * cols)
        value = main_of[s] + from_left + from_right - picture
        out_ref[:, s * ext : (s + 1) * ext] = value
        up = jnp.where(lane < 2 * reach * cols, value[:, :128], 0.0)
        down = value[:, pixels : pixels + 128]
        if len(edge_refs) == 1:
            edges = [jnp.where(lax.axis_index("row") == 0, down, up)]
        else:
            edges = [up, down]
        for ref, edge in zip(edge_refs, edges):
            ref[:, s * 128 : (s + 1) * 128] = edge


def join_body(count, ext, pixels, turn, *refs):
    part_ref, *edge_refs, out_ref, send_ref = refs
    bands = part_ref.shape[0]

    def turned(x, step):
        step %= bands
        return x if step == 0 else jnp.concatenate([x[bands - step :], x[: bands - step]], axis=0)

    for s in range(count):
        at = s * ext
        pieces = [turned(ref[:, s * 128 : (s + 1) * 128], turn * sign) for ref, sign in zip(edge_refs, (-1, 1))]
        if len(pieces) == 1:
            first = lax.axis_index("row") == 0
            pieces = [jnp.where(first, pieces[0], 0.0), jnp.where(first, 0.0, pieces[0])]
        below, above = pieces
        own = part_ref[:, at : at + ext]
        parts = [own[:, :128] + above, own[:, 128:pixels], own[:, pixels : pixels + 128] + below, own[:, pixels + 128 :]]
        value = jnp.concatenate([part for part in parts if part.shape[1]], axis=1)
        out_ref[:, at : at + ext] = value
        send_ref[:, at : at + ext] = value.astype(jnp.bfloat16)


def resid_body(ext, rows, cols, count, reach, peers, *refs):
    own_ref, others, out_ref = refs[0], refs[1 : 1 + peers], refs[1 + peers]
    line = lax.broadcasted_iota(jnp.int32, (1, ext), 1) // cols
    place, places = lax.axis_index("row"), lax.axis_size("row")
    real = ((line >= reach) | (place > 0)) & ((line < rows + reach) | (place < places - 1)) & (line < rows + 2 * reach)
    for s in range(count):
        value = own_ref[:, s * ext : (s + 1) * ext]
        for other in others:
            value = value + other[:, s * ext : (s + 1) * ext].astype(jnp.float32)
        out_ref[:, s * ext : (s + 1) * ext] = jnp.where(real, value, 0.0).astype(jnp.bfloat16).astype(jnp.float32)


def windows_of(taps, bands, ext, rows, cols, count, s, resid_ref, windows_ref):
    reach = taps // 2
    pixels = rows * cols
    column = column_of(ext, cols)

    def tile(s):
        return resid_ref[:, s * ext : (s + 1) * ext]

    left, right = tile_flags("col", s)
    own = tile(s)
    to_left = jnp.where(left, tile((s + 1) % count), 0.0)
    to_right = jnp.where(right, tile((s - 1) % count), 0.0)
    for b in range(taps):
        step = b - reach
        if step == 0:
            view = own
        elif step > 0:
            view = jnp.where(column >= step, roll(own, step), roll(to_left, step - cols))
        else:
            view = jnp.where(column < cols + step, roll(own, step), roll(to_right, step + cols))
        for a in range(taps):
            part = roll(view, -cols * (2 * reach - a))[:, :pixels]
            at = (a * taps + b) * bands
            windows_ref[at : at + bands, :] = part.astype(jnp.bfloat16)


def back_body(taps, bands, ext, rows, cols, count, s, peers, *refs):
    turned_ref = refs[0]
    if peers is None:
        resid_ref, (windows_ref, back_ref) = refs[1], refs[2:]
    else:
        windows_ref, back_ref, resid_ref = refs[-3:]
        resid_body(ext, rows, cols, count, taps // 2, peers, *refs[1:-3], resid_ref)
    windows_of(taps, bands, ext, rows, cols, count, s, resid_ref, windows_ref)
    back = jnp.dot(turned_ref[...], windows_ref[...], preferred_element_type=jnp.float32)
    back_ref[...] = back.astype(back_ref.dtype)


def grad_body(count, *refs):
    windows, tiles, grad_ref = refs[:count], refs[count : 2 * count], refs[2 * count]
    total = None
    for s in range(count):
        term = jnp.dot(windows[s][...], tiles[s][...], preferred_element_type=jnp.float32)
        total = term if total is None else total + term
    grad_ref[...] = total


def codes_body(*refs):
    codes_ref, back_ref = refs[:2]
    others, out_ref = refs[2:-1], refs[-1]
    back = back_ref[...]
    for other in others:
        back = back + other[...].astype(jnp.float32)
    moved = codes_ref[...].astype(jnp.float32) - 0.05 * back.T
    out_ref[...] = (moved - jnp.clip(moved, -0.02, 0.02)).astype(jnp.bfloat16)


def adam_update(master, moment, second, grad):
    new_moment = 0.9 * moment + 0.1 * grad
    new_second = 0.999 * second + 0.001 * grad * grad
    new_dictionary = master - 0.05 * (new_moment / first_fix) / (
        jnp.sqrt(new_second / second_fix) + 1e-08
    )
    return (new_dictionary, new_moment, new_second)


def iteration(codes, image, master, moment, second):
    rows, cols, atoms = codes.shape
    own_bands, taps = master.shape[0], master.shape[1]
    groups, count, peers = lax.axis_size("row"), lax.axis_size("col"), lax.axis_size("atom")
    bands = groups * own_bands
    reach = taps // 2
    pixels = rows * cols
    ext = -(-(rows + 2 * reach) * cols // 128) * 128
    row_at, col_at = lax.axis_index("row"), lax.axis_index("col")

    order = column_order(count)
    tiles = {0: codes.reshape(pixels, atoms)}
    for s in order:
        tiles[s] = shifted(codes, "col", s).reshape(pixels, atoms)

    own_filters = jnp.transpose(master, (1, 2, 0, 3)).reshape(taps * taps, own_bands, atoms).astype(jnp.bfloat16)
    filters = [own_filters]
    for s in range(1, groups):
        filters.append(shifted(own_filters, "row", s))
    filters = jnp.concatenate(filters, axis=1).reshape(taps * taps * bands, atoms)
    turned = filters.T

    picture = image.reshape(pixels, groups, count, own_bands).transpose(1, 2, 3, 0)
    picture = jnp.stack([lax.dynamic_index_in_dim(picture, (row_at + groups - s) % groups, 0, False) for s in range(groups)])
    pieces = [lax.dynamic_index_in_dim(picture, (col_at + s) % count, 1, False).reshape(bands, pixels) for s in range(count)]
    images = []
    for s in range(count):
        images.append(pieces[s] if s == 0 else shifted(pieces[s], "col", s))

    size = struct((bands, ext), jnp.float32)
    y_scratch = [pltpu.VMEM((taps * taps * bands, pixels), jnp.float32)]
    tile_flops = 2 * taps * taps * bands * pixels * atoms
    mains, spills = [], []
    early = [0] + order[:-1]
    for s in early:
        body = functools.partial(early_body, taps, bands, ext, cols)
        main, spill = call(body, [size, size], [filters, tiles[s]], tile_flops, y_scratch)
        mains.append(main)
        spills.append(spill)
    edge = struct((bands, count * 128), jnp.float32)
    part, *edges = call(
        functools.partial(late_body, taps, bands, ext, cols, pixels, tuple(early), 1.0 / peers),
        [struct((bands, count * ext), jnp.float32)] + [edge] * (1 if groups == 2 else 2),
        [filters, tiles[order[-1]], *mains, *spills, *images],
        tile_flops,
        y_scratch,
    )
    if groups == 2:
        edges = [shifted(edges[0], "row", 1)]
    else:
        edges = [moved_on(edges[0], "row", -1), moved_on(edges[1], "row", 1)]
    part, send = call(
        functools.partial(join_body, count, ext, pixels, own_bands),
        [struct(part.shape, jnp.float32), struct(part.shape, jnp.bfloat16)],
        [part, *edges],
    )
    if peers <= 4:
        others = []
        for m in range(peers - 1, 0, -1):
            others.append(lax.ppermute(send, "atom", [(i, i ^ m) for i in range(peers)]))
    else:
        others = [(lax.psum(send, "atom").astype(jnp.float32) - send.astype(jnp.float32)).astype(jnp.bfloat16)]

    windows, received = {}, []
    for place, s in enumerate(order + [0]):
        body = functools.partial(
            back_body, taps, bands, ext, rows, cols, count, s, len(others) if place == 0 else None
        )
        outs = [
            struct((taps * taps * bands, pixels), jnp.bfloat16),
            struct((atoms, pixels), jnp.bfloat16 if s else jnp.float32),
        ]
        if place == 0:
            windows[s], back, resid = call(
                body, outs + [struct(part.shape, jnp.float32)], [turned, part, *others], tile_flops
            )
        else:
            windows[s], back = call(body, outs, [turned, resid], tile_flops)
        if s:
            received.append(shifted(back, "col", -s))
    own_back = back
    (grad,) = call(
        functools.partial(grad_body, count),
        [struct((taps * taps * bands, atoms), jnp.float32)],
        [windows[s] for s in range(count)] + [tiles[s] for s in range(count)],
        tile_flops * count,
    )
    grad = grad.reshape(taps * taps, groups, own_bands, atoms)
    own_grad = grad[:, 0]
    for s in range(1, groups):
        piece = grad[:, s].astype(jnp.bfloat16)
        piece = shifted(piece, "row", -s)
        own_grad = own_grad + piece.astype(jnp.float32)
    own_grad = jnp.transpose(own_grad.reshape(taps, taps, own_bands, atoms), (2, 0, 1, 3))
    new_dictionary, new_moment, new_second = adam_update(master, moment, second, own_grad)
    (new_codes,) = call(
        codes_body, [struct((pixels, atoms), jnp.bfloat16)], [codes.reshape(pixels, atoms), own_back, *received]
    )
    return (new_codes.reshape(rows, cols, atoms), new_dictionary, new_moment, new_second)


def column_order(count):
    return sorted(range(1, count), key=lambda s: (abs(count - 2 * s), s))


def solution(mesh):
    return jax.shard_map(
        iteration,
        mesh=mesh,
        in_specs=(
            P("row", "col", "atom"),
            P("row", "col", None),
            P(("row", "col"), None, None, "atom"),
            P(("row", "col"), None, None, "atom"),
            P(("row", "col"), None, None, "atom"),
        ),
        out_specs=(
            P("row", "col", "atom"),
            P(("row", "col"), None, None, "atom"),
            P(("row", "col"), None, None, "atom"),
            P(("row", "col"), None, None, "atom"),
        ),
        check_vma=False,
    )
```

time: 109 us -> 83.2 us (0.76)
  Pallas kernels: 30.5 us -> 11.7 us
  local copies, waits for them, and re-layouts: 8.67 us -> 4.08 us
  other arithmetic: 10.6 us -> 6.09 us
  waiting for transfers between devices: 36.3 us -> 37.5 us
    pallas_call x9 -> x11, Pallas kernels: 30.5 us -> 11.7 us  [call(): pl.pallas_call(body, out_shape=outs, in_specs=[pl.BlockSpec(memory_space=...]
    ppermute x11 -> x12, starting transfers between devices: 14.5 us -> 19.9 us  [shifted(): lax.ppermute(x, axis, [(i, (i + step) % count) for i in range(count)])]
    ppermute x5 -> x3, starting transfers between devices: 7.4 us -> 2.65 us  [iteration(): lax.ppermute(send, 'atom', [(i, i ^ m) for i in range(peers)])]
    unnamed x36 -> x26, local copies, waits for them, and re-layouts: 4.02 us -> 2.1 us
    convert_element_type x1, local copies, waits for them, and re-layouts: 1.7 us -> 0.12 us  [iteration(): piece = grad[:, s].astype(jnp.bfloat16)]
    sub x1, other arithmetic: 4.39 us -> 2.97 us  [adam_update(): master - 0.05 * (new_moment / first_fix) / (jnp.sqrt(new_second / second_...]
    ppermute x11 -> x12, waiting for transfers between devices: 32.2 us -> 33.6 us  [shifted(): lax.ppermute(x, axis, [(i, (i + step) % count) for i in range(count)])]
    add x1, other arithmetic: 1.54 us -> 0.25 us  [iteration(): own_grad = own_grad + piece.astype(jnp.float32)]
  transfers between devices with their start and end apart: 16 -> 15, of which waited for: 7 -> 6; matrix products, arithmetic and copies ran while one was open for 6% -> 4% of each run, Pallas kernels for 10% -> 4%
where the time goes in v2:
time: 83.2 us; the launch traced here: 82.9 us
  waiting for transfers between devices  37.5 us (45%)
  starting transfers between devices  22.6 us (27%)
  Pallas kernels  11.7 us (14%)
  other arithmetic  6.09 us (7%)
  local copies, waits for them, and re-layouts  4.08 us (5%)
  between operations  0.96 us (1%)
    ppermute x12, waiting for transfers between devices, shifted(): lax.ppermute(x, axis, [(i, (i + step) % count) for i in range(count)])  33.6 us
    ppermute x12, starting transfers between devices, shifted(): lax.ppermute(x, axis, [(i, (i + step) % count) for i in range(count)])  19.9 us
    pallas_call x11, Pallas kernels, call(): pl.pallas_call(body, out_shape=outs, in_specs=[pl.BlockSpec(memory_space=...  11.7 us
    ppermute x3, waiting for transfers between devices, iteration(): lax.ppermute(send, 'atom', [(i, i ^ m) for i in range(peers)])  3.89 us
    sub x1, other arithmetic, adam_update(): master - 0.05 * (new_moment / first_fix) / (jnp.sqrt(new_second / second_...  2.97 us
    ppermute x3, starting transfers between devices, iteration(): lax.ppermute(send, 'atom', [(i, i ^ m) for i in range(peers)])  2.65 us
    unnamed x26, local copies, waits for them, and re-layouts  2.1 us
  transfers between devices with their start and end apart: 15, of which 6 were waited for; matrix products, arithmetic and copies ran while one was open for 4% of the time, Pallas kernels for 4%

profile of v2, /device:TPU:9, one launch (start us, length us, event | category | flops | bytes accessed | tf_op | source)
XLA Modules:
  0.0 82.9 jit_solution(12479568822511808119)
XLA Ops:
  0.7 1.6 %convert_element_type.16 = bf16[16,7,7,512]{3,0,2,1:T(8,128)(2,1)S(1)} convert(f32[16,7,7,512]{3,0,2,1:T(8,128)} %param.7) | non-fusion elementwise | flops 401408 | bytes 2408448 | tf_op jit(solution)/shard_map/convert_element_type | solution.py:238
  2.2 0.7 collective-permute-start
  3.0 2.5 %collective-permute-start.2 = (bf16[16,16,512]{2,1,0:T(8,128)(2,1)S(1)}, bf16[16,16,512]{2,1,0:T(8,128)(2,1)S(1)}, u32[]{:S(2)}, u32[]{:S(2)}) collective-permute-start(bf16[16,16,512]{2,1,0:T(8,128)(2,1)S(1)} %copy-done), channel_id=1, source_target_pairs={{0,2},{1,3},{2,0},{3,1},{4,6},{5,7},{6,4},{7,5},{8,10},{9,11},{10,... | collective-permute-start | bytes 786440 | tf_op jit(solution)/shard_map/ppermute | solution.py:17
  5.5 2.2 %collective-permute-start.3 = (bf16[16,16,512]{2,1,0:T(8,128)(2,1)S(1)}, bf16[16,16,512]{2,1,0:T(8,128)(2,1)S(1)}, u32[]{:S(2)}, u32[]{:S(2)}) collective-permute-start(bf16[16,16,512]{2,1,0:T(8,128)(2,1)S(1)} %copy-done), channel_id=1, source_target_pairs={{0,1},{1,2},{2,3},{3,0},{4,5},{5,6},{6,7},{7,4},{8,9},{9,10},{10,1... | collective-permute-start | bytes 786440 | tf_op jit(solution)/shard_map/ppermute | solution.py:17
  8.6 1.3 %collective-permute-start.5 = (bf16[32,256]{1,0:T(8,128)(2,1)S(1)}, bf16[32,256]{1,0:T(8,128)(2,1)S(1)}, u32[]{:S(2)}, u32[]{:S(2)}) collective-permute-start(bf16[32,256]{1,0:T(8,128)(2,1)S(1)} %bitcast.56), channel_id=1, source_target_pairs={{0,2},{1,3},{2,0},{3,1},{4,6},{5,7},{6,4},{7,5},{8,10},{9,11},{10,... | collective-permute-start | bytes 49160 | tf_op jit(solution)/shard_map/ppermute | solution.py:17
  10.0 1.3 %pad_maximum_fusion = bf16[49,32,512]{2,1,0:T(8,128)(2,1)S(1)} fusion(bf16[49,16,512]{2,1,0:T(8,128)(2,1)} %collective-permute-done, bf16[49,16,512]{2,1,0:T(8,128)(2,1)S(1)} %bitcast.51), kind=kLoop, calls=%fused_computation.5 | loop fusion | flops 3211264 | bytes 3211264 | tf_op jit(solution)/shard_map/concatenate | solution.py:242
  11.2 0.9 %shard_map.84 = (f32[32,384]{1,0:T(8,128)S(1)}, f32[32,384]{1,0:T(8,128)S(1)}) custom-call(bf16[1568,512]{1,0:T(8,128)(2,1)S(1)} %bitcast.28, bf16[256,512]{1,0:T(8,128)(2,1)S(1)} %bitcast.39), custom_call_target="tpu_custom_call" | custom-call | flops 411041792 | bytes 1966080 | tf_op jit(solution)/shard_map/pallas_call | solution.py:27
  12.2 9.9 %collective-permute-done.2 = bf16[16,16,512]{2,1,0:T(8,128)(2,1)S(1)} collective-permute-done((bf16[16,16,512]{2,1,0:T(8,128)(2,1)S(1)}, bf16[16,16,512]{2,1,0:T(8,128)(2,1)S(1)}, u32[]{:S(2)}, u32[]{:S(2)}) %collective-permute-start.2) | collective-permute-done | bytes 262176 | tf_op jit(solution)/shard_map/ppermute | solution.py:17
  22.1 7.4 %collective-permute-start.6 = (bf16[32,256]{1,0:T(8,128)(2,1)S(1)}, bf16[32,256]{1,0:T(8,128)(2,1)S(1)}, u32[]{:S(2)}, u32[]{:S(2)}) collective-permute-start(bf16[32,256]{1,0:T(8,128)(2,1)S(1)} %bitcast.55), channel_id=1, source_target_pairs={{0,3},{1,0},{2,1},{3,2},{4,7},{5,4},{6,5},{7,6},{8,11},{9,8},{10,9... | collective-permute-start | bytes 49160 | tf_op jit(solution)/shard_map/ppermute | solution.py:17
  29.5 0.9 %shard_map.85 = (f32[32,384]{1,0:T(8,128)S(1)}, f32[32,384]{1,0:T(8,128)S(1)}) custom-call(bf16[1568,512]{1,0:T(8,128)(2,1)S(1)} %bitcast.29, bf16[256,512]{1,0:T(8,128)(2,1)S(1)} %bitcast.44), custom_call_target="tpu_custom_call" | custom-call | flops 411041792 | bytes 1966080 | tf_op jit(solution)/shard_map/pallas_call | solution.py:27
  30.5 0.9 %shard_map.86 = (f32[32,384]{1,0:T(8,128)S(1)}, f32[32,384]{1,0:T(8,128)S(1)}) custom-call(bf16[1568,512]{1,0:T(8,128)(2,1)S(1)} %bitcast.30, bf16[256,512]{1,0:T(8,128)(2,1)S(1)} %bitcast.46), custom_call_target="tpu_custom_call" | custom-call | flops 411041792 | bytes 1966080 | tf_op jit(solution)/shard_map/pallas_call | solution.py:27
  31.5 0.9 %shard_map.87 = (f32[32,1536]{1,0:T(8,128)S(1)}, f32[32,512]{1,0:T(8,128)S(1)}) custom-call(bf16[1568,512]{1,0:T(8,128)(2,1)S(1)} %bitcast.31, bf16[256,512]{1,0:T(8,128)(2,1)S(1)} %bitcast.42, f32[32,384]{1,0:T(8,128)S(1)} %get-tuple-element.23.refs_2_, f32[32,384]{1,0:T(8,128)S(1)} %get-tuple-element.24.refs_3_, f32[32,384]{1,0:T(8,128)S(1)} %get-tuple-element.25.refs_4_, ...), custom_call_target="tpu_custom_call" | custom-call | flops 411041792 | bytes 2490368 | tf_op jit(solution)/shard_map/pallas_call | solution.py:27
  32.4 1.6 %collective-permute-start.7 = (f32[32,512]{1,0:T(8,128)S(1)}, f32[32,512]{1,0:T(8,128)S(1)}, u32[]{:S(2)}, u32[]{:S(2)}) collective-permute-start(f32[32,512]{1,0:T(8,128)S(1)} %get-tuple-element.30), channel_id=1, source_target_pairs={{0,4},{4,0},{1,5},{5,1},{2,6},{6,2},{3,7},{7,3},{8,12},{12,8},{9,1... | collective-permute-start | bytes 196616 | tf_op jit(solution)/shard_map/ppermute | solution.py:17
  34.1 0.9 %collective-permute-done.7.refs_1_ = f32[32,512]{1,0:T(8,128)S(1)} collective-permute-done((f32[32,512]{1,0:T(8,128)S(1)}, f32[32,512]{1,0:T(8,128)S(1)}, u32[]{:S(2)}, u32[]{:S(2)}) %collective-permute-start.7) | collective-permute-done | bytes 65568 | tf_op jit(solution)/shard_map/ppermute | solution.py:17
  35.0 0.7 shard_map.88
  35.6 2.2 %collective-permute-start.8 = (bf16[32,1536]{1,0:T(8,128)(2,1)}, bf16[32,1536]{1,0:T(8,128)(2,1)}, u32[]{:S(2)}, u32[]{:S(2)}) collective-permute-start(bf16[32,1536]{1,0:T(8,128)(2,1)} %get-tuple-element.32), channel_id=1, source_target_pairs={{0,24},{8,16},{16,8},{24,0},{1,25},{9,17},{17,9},{25,1},{2,26},{10... | collective-permute-start | bytes 294920 | tf_op jit(solution)/shard_map/ppermute | solution.py:282
  38.3 1.3 %copy.18 = bf16[1568,512]{0,1:T(8,128)(2,1)S(1)} copy(bf16[1568,512]{1,0:T(8,128)(2,1)S(1)} %bitcast.32) | data formatting | bytes 3211264 | tf_op jit(solution)/shard_map/reshape | solution.py:242
  39.6 1.2 %collective-permute-done.8.refs_2_ = bf16[32,1536]{1,0:T(8,128)(2,1)} collective-permute-done((bf16[32,1536]{1,0:T(8,128)(2,1)}, bf16[32,1536]{1,0:T(8,128)(2,1)}, u32[]{:S(2)}, u32[]{:S(2)}) %collective-permute-start.8) | collective-permute-done | bytes 98336 | tf_op jit(solution)/shard_map/ppermute | solution.py:282
  40.8 2.6 %collective-permute-done.9.refs_3_ = bf16[32,1536]{1,0:T(8,128)(2,1)} collective-permute-done((bf16[32,1536]{1,0:T(8,128)(2,1)}, bf16[32,1536]{1,0:T(8,128)(2,1)}, u32[]{:S(2)}, u32[]{:S(2)}) %collective-permute-start.9) | collective-permute-done | bytes 98336 | tf_op jit(solution)/shard_map/ppermute | solution.py:282
  43.5 1.9 %shard_map.89 = (bf16[1568,256]{1,0:T(8,128)(2,1)S(1)}, bf16[512,256]{1,0:T(8,128)(2,1)S(1)}, f32[32,1536]{1,0:T(8,128)S(1)}) custom-call(bf16[512,1568]{1,0:T(8,128)(2,1)S(1)} %bitcast.33, f32[32,1536]{1,0:T(8,128)S(1)} %get-tuple-element.31.refs_1_, bf16[32,1536]{1,0:T(8,128)(2,1)} %collective-permute-done.8.refs_2_, ...), custom_call_target="tpu_custom_call" | custom-call | flops 411041792 | bytes 3358720 | tf_op jit(solution)/shard_map/pallas_call | solution.py:27
  45.4 0.9 %shard_map.90 = (bf16[1568,256]{1,0:T(8,128)(2,1)S(1)}, f32[512,256]{1,0:T(8,128)S(1)}) custom-call(bf16[512,1568]{1,0:T(8,128)(2,1)S(1)} %bitcast.34, f32[32,1536]{1,0:T(8,128)S(1)} %get-tuple-element.33.refs_1_), custom_call_target="tpu_custom_call" | custom-call | flops 411041792 | bytes 3129344 | tf_op jit(solution)/shard_map/pallas_call | solution.py:27
  46.3 0.9 %shard_map.91 = (bf16[1568,256]{1,0:T(8,128)(2,1)S(1)}, bf16[512,256]{1,0:T(8,128)(2,1)S(1)}) custom-call(bf16[512,1568]{1,0:T(8,128)(2,1)S(1)} %bitcast.35, f32[32,1536]{1,0:T(8,128)S(1)} %get-tuple-element.33.refs_1_), custom_call_target="tpu_custom_call" | custom-call | flops 411041792 | bytes 2867200 | tf_op jit(solution)/shard_map/pallas_call | solution.py:27
  47.2 0.9 %shard_map.92 = (bf16[1568,256]{1,0:T(8,128)(2,1)S(1)}, bf16[512,256]{1,0:T(8,128)(2,1)S(1)}) custom-call(bf16[512,1568]{1,0:T(8,128)(2,1)S(1)} %bitcast.36, f32[32,1536]{1,0:T(8,128)S(1)} %get-tuple-element.33.refs_1_), custom_call_target="tpu_custom_call" | custom-call | flops 411041792 | bytes 2867200 | tf_op jit(solution)/shard_map/pallas_call | solution.py:27
  48.2 1.8 %shard_map.94 = f32[1568,512]{1,0:T(8,128)S(1)} custom-call(bf16[1568,256]{1,0:T(8,128)(2,1)S(1)} %get-tuple-element.38.refs_0_, bf16[1568,256]{1,0:T(8,128)(2,1)S(1)} %get-tuple-element.39.refs_1_, bf16[1568,256]{1,0:T(8,128)(2,1)S(1)} %get-tuple-element.40.refs_2_, bf16[1568,256]{1,0:T(8,128)(2,1)S(1)} %get-tuple-element.41.refs_3_, ...), custom_call_target="tpu_custom_call" | custom-call | flops 1644167168 | bytes 7471104 | tf_op jit(solution)/shard_map/pallas_call | solution.py:27
  50.1 0.8 collective-permute-start.14
  50.9 1.8 %collective-permute-start.11 = (bf16[512,256]{1,0:T(8,128)(2,1)S(1)}, bf16[512,256]{1,0:T(8,128)(2,1)S(1)}, u32[]{:S(2)}, u32[]{:S(2)}) collective-permute-start(bf16[512,256]{1,0:T(8,128)(2,1)S(1)} %get-tuple-element.35), channel_id=1, source_target_pairs={{0,2},{1,3},{2,0},{3,1},{4,6},{5,7},{6,4},{7,5},{8,10},{9,11},{10,... | collective-permute-start | bytes 786440 | tf_op jit(solution)/shard_map/ppermute | solution.py:17
  52.8 1.5 %collective-permute-start.13 = (bf16[512,256]{1,0:T(8,128)(2,1)S(1)}, bf16[512,256]{1,0:T(8,128)(2,1)S(1)}, u32[]{:S(2)}, u32[]{:S(2)}) collective-permute-start(bf16[512,256]{1,0:T(8,128)(2,1)S(1)} %get-tuple-element.37), channel_id=1, source_target_pairs={{0,1},{1,2},{2,3},{3,0},{4,5},{5,6},{6,7},{7,4},{8,9},{9,10},{10,1... | collective-permute-start | bytes 786440 | tf_op jit(solution)/shard_map/ppermute | solution.py:17
  54.2 15.3 %collective-permute-done.11.refs_2_ = bf16[512,256]{1,0:T(8,128)(2,1)S(1)} collective-permute-done((bf16[512,256]{1,0:T(8,128)(2,1)S(1)}, bf16[512,256]{1,0:T(8,128)(2,1)S(1)}, u32[]{:S(2)}, u32[]{:S(2)}) %collective-permute-start.11) | collective-permute-done | bytes 262176 | tf_op jit(solution)/shard_map/ppermute | solution.py:17
  69.5 7.4 %collective-permute-done.12.refs_3_ = bf16[512,256]{1,0:T(8,128)(2,1)S(1)} collective-permute-done((bf16[512,256]{1,0:T(8,128)(2,1)S(1)}, bf16[512,256]{1,0:T(8,128)(2,1)S(1)}, u32[]{:S(2)}, u32[]{:S(2)}) %collective-permute-start.12) | collective-permute-done | bytes 262176 | tf_op jit(solution)/shard_map/ppermute | solution.py:17
  77.0 0.9 %shard_map.93 = bf16[256,512]{1,0:T(8,128)(2,1)} custom-call(bf16[256,512]{1,0:T(8,128)(2,1)S(1)} %bitcast.41, f32[512,256]{1,0:T(8,128)S(1)} %get-tuple-element.34.refs_1_, bf16[512,256]{1,0:T(8,128)(2,1)S(1)} %collective-permute-done.11.refs_2_, bf16[512,256]{1,0:T(8,128)(2,1)S(1)} %collective-permute-done.12.refs_3_, ...), custom_call_target="tpu_custom_call" | custom-call | bytes 1835008 | tf_op jit(solution)/shard_map/pallas_call | solution.py:27
  78.5 1.0 %copy-done.8 = f32[16,7,7,512]{3,0,2,1:T(8,128)S(1)} copy-done((f32[16,7,7,512]{3,0,2,1:T(8,128)S(1)}, f32[16,7,7,512]{3,0,2,1:T(8,128)}, u32[]{:S(2)}) %copy-start.8) | copy-done | bytes 1605656
  79.9 3.0 %divide_subtract_fusion = (f32[16,7,7,512]{3,0,2,1:T(8,128)}, f32[16,7,7,512]{3,0,2,1:T(8,128)}, f32[16,7,7,512]{3,0,2,1:T(8,128)}) fusion(f32[16,7,7,512]{3,0,2,1:T(8,128)S(1)} %copy-done.8, f32[16,7,7,512]{3,0,2,1:T(8,128)S(1)} %bitcast.49, f32[16,7,7,512]{3,0,2,1:T(8,128)S(1)} %copy-done.9, f32[16,7,7,512]{3,0,2,1:T(8,128)S(1)} %copy-done.10), kind=kLoop, calls=%fused_computation.6 | loop fusion | flops 4816896 | bytes 11239424 | tf_op jit(solution)/shard_map/sub | solution.py:217
  (44 shorter events, 2.6 us)
Async XLA Ops:
  0.6 2.4 %copy-start = (bf16[16,16,512]{2,1,0:T(8,128)(2,1)S(1)}, bf16[16,16,512]{2,1,0:T(8,128)(2,1)}, u32[]{:S(2)}) copy-start(bf16[16,16,512]{2,1,0:T(8,128)(2,1)} %param.5) | copy-start | bytes 786436
  0.6 7.0 %copy-start.11 = (bf16[16,16,128]{2,1,0:T(8,128)(2,1)S(1)}, bf16[16,16,128]{2,1,0:T(8,128)(2,1)}, u32[]{:S(2)}) copy-start(bf16[16,16,128]{2,1,0:T(8,128)(2,1)} %param.6) | copy-start | bytes 196612
  2.2 6.4 %collective-permute-start = (bf16[49,16,512]{2,1,0:T(8,128)(2,1)S(1)}, bf16[49,16,512]{2,1,0:T(8,128)(2,1)}, u32[]{:S(2)}, u32[]{:S(2)}) collective-permute-start(bf16[49,16,512]{2,1,0:T(8,128)(2,1)S(1)} %bitcast.50), channel_id=1, source_target_pairs={{0,4},{4,0},{1,5},{5,1},{2,6},{6,2},{3,7},{7,3},{8,12},{12,8},{9,1... | collective-permute-start | bytes 2408456 | tf_op jit(solution)/shard_map/ppermute | solution.py:17
  3.0 28.5 %collective-permute-start.1 = (bf16[16,16,512]{2,1,0:T(8,128)(2,1)S(1)}, bf16[16,16,512]{2,1,0:T(8,128)(2,1)S(1)}, u32[]{:S(2)}, u32[]{:S(2)}) collective-permute-start(bf16[16,16,512]{2,1,0:T(8,128)(2,1)S(1)} %copy-done), channel_id=1, source_target_pairs={{0,3},{1,0},{2,1},{3,2},{4,7},{5,4},{6,5},{7,6},{8,11},{9,8},{10,9... | collective-permute-start | bytes 786440 | tf_op jit(solution)/shard_map/ppermute | solution.py:17
  3.0 19.1 %collective-permute-start.2 = (bf16[16,16,512]{2,1,0:T(8,128)(2,1)S(1)}, bf16[16,16,512]{2,1,0:T(8,128)(2,1)S(1)}, u32[]{:S(2)}, u32[]{:S(2)}) collective-permute-start(bf16[16,16,512]{2,1,0:T(8,128)(2,1)S(1)} %copy-done), channel_id=1, source_target_pairs={{0,2},{1,3},{2,0},{3,1},{4,6},{5,7},{6,4},{7,5},{8,10},{9,11},{10,... | collective-permute-start | bytes 786440 | tf_op jit(solution)/shard_map/ppermute | solution.py:17
  5.5 25.0 %collective-permute-start.3 = (bf16[16,16,512]{2,1,0:T(8,128)(2,1)S(1)}, bf16[16,16,512]{2,1,0:T(8,128)(2,1)S(1)}, u32[]{:S(2)}, u32[]{:S(2)}) collective-permute-start(bf16[16,16,512]{2,1,0:T(8,128)(2,1)S(1)} %copy-done), channel_id=1, source_target_pairs={{0,1},{1,2},{2,3},{3,0},{4,5},{5,6},{6,7},{7,4},{8,9},{9,10},{10,1... | collective-permute-start | bytes 786440 | tf_op jit(solution)/shard_map/ppermute | solution.py:17
  8.6 22.9 %collective-permute-start.4 = (bf16[32,256]{1,0:T(8,128)(2,1)S(1)}, bf16[32,256]{1,0:T(8,128)(2,1)S(1)}, u32[]{:S(2)}, u32[]{:S(2)}) collective-permute-start(bf16[32,256]{1,0:T(8,128)(2,1)S(1)} %bitcast.57), channel_id=1, source_target_pairs={{0,1},{1,2},{2,3},{3,0},{4,5},{5,6},{6,7},{7,4},{8,9},{9,10},{10,1... | collective-permute-start | bytes 49160 | tf_op jit(solution)/shard_map/ppermute | solution.py:17
  8.6 22.8 %collective-permute-start.5 = (bf16[32,256]{1,0:T(8,128)(2,1)S(1)}, bf16[32,256]{1,0:T(8,128)(2,1)S(1)}, u32[]{:S(2)}, u32[]{:S(2)}) collective-permute-start(bf16[32,256]{1,0:T(8,128)(2,1)S(1)} %bitcast.56), channel_id=1, source_target_pairs={{0,2},{1,3},{2,0},{3,1},{4,6},{5,7},{6,4},{7,5},{8,10},{9,11},{10,... | collective-permute-start | bytes 49160 | tf_op jit(solution)/shard_map/ppermute | solution.py:17
  22.1 9.3 %copy-start.4 = (bf16[16,16,512]{2,1,0:T(8,128)(2,1)}, bf16[16,16,512]{2,1,0:T(8,128)(2,1)S(1)}, u32[]{:S(2)}) copy-start(bf16[16,16,512]{2,1,0:T(8,128)(2,1)S(1)} %collective-permute-done.2) | copy-start | bytes 786436
  22.1 9.3 %collective-permute-start.6 = (bf16[32,256]{1,0:T(8,128)(2,1)S(1)}, bf16[32,256]{1,0:T(8,128)(2,1)S(1)}, u32[]{:S(2)}, u32[]{:S(2)}) collective-permute-start(bf16[32,256]{1,0:T(8,128)(2,1)S(1)} %bitcast.55), channel_id=1, source_target_pairs={{0,3},{1,0},{2,1},{3,2},{4,7},{5,4},{6,5},{7,6},{8,11},{9,8},{10,9... | collective-permute-start | bytes 49160 | tf_op jit(solution)/shard_map/ppermute | solution.py:17
  30.5 2.0 %copy-start.6 = (bf16[16,16,512]{2,1,0:T(8,128)(2,1)}, bf16[16,16,512]{2,1,0:T(8,128)(2,1)S(1)}, u32[]{:S(2)}) copy-start(bf16[16,16,512]{2,1,0:T(8,128)(2,1)S(1)} %collective-permute-done.3) | copy-start | bytes 786436
  31.5 6.6 %copy-start.2 = (bf16[16,16,512]{2,1,0:T(8,128)(2,1)}, bf16[16,16,512]{2,1,0:T(8,128)(2,1)S(1)}, u32[]{:S(2)}) copy-start(bf16[16,16,512]{2,1,0:T(8,128)(2,1)S(1)} %collective-permute-done.1) | copy-start | bytes 786436
  32.4 2.5 %collective-permute-start.7 = (f32[32,512]{1,0:T(8,128)S(1)}, f32[32,512]{1,0:T(8,128)S(1)}, u32[]{:S(2)}, u32[]{:S(2)}) collective-permute-start(f32[32,512]{1,0:T(8,128)S(1)} %get-tuple-element.30), channel_id=1, source_target_pairs={{0,4},{4,0},{1,5},{5,1},{2,6},{6,2},{3,7},{7,3},{8,12},{12,8},{9,1... | collective-permute-start | bytes 196616 | tf_op jit(solution)/shard_map/ppermute | solution.py:17
  35.6 5.2 %collective-permute-start.8 = (bf16[32,1536]{1,0:T(8,128)(2,1)}, bf16[32,1536]{1,0:T(8,128)(2,1)}, u32[]{:S(2)}, u32[]{:S(2)}) collective-permute-start(bf16[32,1536]{1,0:T(8,128)(2,1)} %get-tuple-element.32), channel_id=1, source_target_pairs={{0,24},{8,16},{16,8},{24,0},{1,25},{9,17},{17,9},{25,1},{2,26},{10... | collective-permute-start | bytes 294920 | tf_op jit(solution)/shard_map/ppermute | solution.py:282
  37.8 5.7 %collective-permute-start.9 = (bf16[32,1536]{1,0:T(8,128)(2,1)}, bf16[32,1536]{1,0:T(8,128)(2,1)}, u32[]{:S(2)}, u32[]{:S(2)}) collective-permute-start(bf16[32,1536]{1,0:T(8,128)(2,1)} %get-tuple-element.32), channel_id=1, source_target_pairs={{0,16},{8,24},{16,0},{24,8},{1,17},{9,25},{17,1},{25,9},{2,18},{10... | collective-permute-start | bytes 294920 | tf_op jit(solution)/shard_map/ppermute | solution.py:282
  38.0 5.5 %collective-permute-start.10 = (bf16[32,1536]{1,0:T(8,128)(2,1)}, bf16[32,1536]{1,0:T(8,128)(2,1)}, u32[]{:S(2)}, u32[]{:S(2)}) collective-permute-start(bf16[32,1536]{1,0:T(8,128)(2,1)} %get-tuple-element.32), channel_id=1, source_target_pairs={{0,8},{8,0},{16,24},{24,16},{1,9},{9,1},{17,25},{25,17},{2,10},{10... | collective-permute-start | bytes 294920 | tf_op jit(solution)/shard_map/ppermute | solution.py:282
  46.3 1.8 %copy-start.1 = (bf16[16,16,512]{2,1,0:T(8,128)(2,1)S(1)}, bf16[16,16,512]{2,1,0:T(8,128)(2,1)}, u32[]{:S(2)}) copy-start(bf16[16,16,512]{2,1,0:T(8,128)(2,1)} %param.5) | copy-start | bytes 786436
  46.3 1.8 %copy-start.3 = (bf16[16,16,512]{2,1,0:T(8,128)(2,1)S(1)}, bf16[16,16,512]{2,1,0:T(8,128)(2,1)}, u32[]{:S(2)}) copy-start(bf16[16,16,512]{2,1,0:T(8,128)(2,1)} %copy-done.2) | copy-start | bytes 786436
  46.3 1.8 %copy-start.5 = (bf16[16,16,512]{2,1,0:T(8,128)(2,1)S(1)}, bf16[16,16,512]{2,1,0:T(8,128)(2,1)}, u32[]{:S(2)}) copy-start(bf16[16,16,512]{2,1,0:T(8,128)(2,1)} %copy-done.4) | copy-start | bytes 786436
  46.3 1.8 %copy-start.7 = (bf16[16,16,512]{2,1,0:T(8,128)(2,1)S(1)}, bf16[16,16,512]{2,1,0:T(8,128)(2,1)}, u32[]{:S(2)}) copy-start(bf16[16,16,512]{2,1,0:T(8,128)(2,1)} %copy-done.6) | copy-start | bytes 786436
  50.1 27.8 %collective-permute-start.14 = (bf16[49,16,512]{2,1,0:T(8,128)(2,1)S(1)}, bf16[49,16,512]{2,1,0:T(8,128)(2,1)S(1)}, u32[]{:S(2)}, u32[]{:S(2)}) collective-permute-start(bf16[49,16,512]{2,1,0:T(8,128)(2,1)S(1)} %fusion.2), channel_id=1, source_target_pairs={{0,4},{4,0},{1,5},{5,1},{2,6},{6,2},{3,7},{7,3},{8,12},{12,8},{9,1... | collective-permute-start | bytes 2408456 | tf_op jit(solution)/shard_map/ppermute | solution.py:17
  50.9 18.6 %collective-permute-start.11 = (bf16[512,256]{1,0:T(8,128)(2,1)S(1)}, bf16[512,256]{1,0:T(8,128)(2,1)S(1)}, u32[]{:S(2)}, u32[]{:S(2)}) collective-permute-start(bf16[512,256]{1,0:T(8,128)(2,1)S(1)} %get-tuple-element.35), channel_id=1, source_target_pairs={{0,2},{1,3},{2,0},{3,1},{4,6},{5,7},{6,4},{7,5},{8,10},{9,11},{10,... | collective-permute-start | bytes 786440 | tf_op jit(solution)/shard_map/ppermute | solution.py:17
  52.8 24.2 %collective-permute-start.12 = (bf16[512,256]{1,0:T(8,128)(2,1)S(1)}, bf16[512,256]{1,0:T(8,128)(2,1)S(1)}, u32[]{:S(2)}, u32[]{:S(2)}) collective-permute-start(bf16[512,256]{1,0:T(8,128)(2,1)S(1)} %get-tuple-element.36), channel_id=1, source_target_pairs={{0,3},{1,0},{2,1},{3,2},{4,7},{5,4},{6,5},{7,6},{8,11},{9,8},{10,9... | collective-permute-start | bytes 786440 | tf_op jit(solution)/shard_map/ppermute | solution.py:17
  52.8 24.2 %collective-permute-start.13 = (bf16[512,256]{1,0:T(8,128)(2,1)S(1)}, bf16[512,256]{1,0:T(8,128)(2,1)S(1)}, u32[]{:S(2)}, u32[]{:S(2)}) collective-permute-start(bf16[512,256]{1,0:T(8,128)(2,1)S(1)} %get-tuple-element.37), channel_id=1, source_target_pairs={{0,1},{1,2},{2,3},{3,0},{4,5},{5,6},{6,7},{7,4},{8,9},{9,10},{10,1... | collective-permute-start | bytes 786440 | tf_op jit(solution)/shard_map/ppermute | solution.py:17
  77.0 1.5 %copy-start.10 = (f32[16,7,7,512]{3,0,2,1:T(8,128)S(1)}, f32[16,7,7,512]{3,0,2,1:T(8,128)}, u32[]{:S(2)}) copy-start(f32[16,7,7,512]{3,0,2,1:T(8,128)} %param.9) | copy-start | bytes 4816900
  77.9 1.5 %copy-start.8 = (f32[16,7,7,512]{3,0,2,1:T(8,128)S(1)}, f32[16,7,7,512]{3,0,2,1:T(8,128)}, u32[]{:S(2)}) copy-start(f32[16,7,7,512]{3,0,2,1:T(8,128)} %param.7) | copy-start | bytes 4816900
  77.9 2.0 %copy-start.9 = (f32[16,7,7,512]{3,0,2,1:T(8,128)S(1)}, f32[16,7,7,512]{3,0,2,1:T(8,128)}, u32[]{:S(2)}) copy-start(f32[16,7,7,512]{3,0,2,1:T(8,128)} %param.8) | copy-start | bytes 4816900

commit v3 on v2

--- a/solution.py
+++ b/solution.py
@@ -20,6 +20,15 @@
 def moved_on(x, axis, step):
     count = lax.axis_size(axis)
     return lax.ppermute(x, axis, [(i, i + step) for i in range(count) if 0 <= i + step < count])
+
+
+TWO = [(0, 2), (1, 3), (2, 0), (3, 1)]
+NEAR = [(0, 1), (1, 0), (2, 3), (3, 2)]
+INNER = [(1, 2), (2, 1)]
+
+
+def along(x, pairs):
+    return lax.ppermute(x, "col", pairs)
 
 
 def call(body, outs, args, flops=0, scratch=()):
@@ -80,36 +89,40 @@
     spill_ref[...] = spill
 
 
-def tile_flags(axis, s):
-    count = lax.axis_size(axis)
-    place = lax.rem(lax.axis_index(axis) + count - s, count)
+def tile_flags(s):
+    count = lax.axis_size("col")
+    place = lax.rem(lax.axis_index("col") + count - s, count)
     return place > 0, place < count - 1
 
 
-def late_body(taps, bands, ext, cols, pixels, order, share, *refs):
-    count = len(order) + 1
-    filters_ref, tile_ref = refs[:2]
-    mains, spills = refs[2 : 1 + count], refs[1 + count : 2 * count]
-    images = refs[2 * count : 3 * count]
-    out_ref, *edge_refs, y_ref = refs[3 * count :]
-    reach = taps // 2
-    main, spill = tile_parts(filters_ref[...], tile_ref[...], y_ref, taps, bands, ext, cols)
-    last = (set(range(count)) - set(order)).pop()
-    main_of, spill_of = {last: main}, {last: spill}
-    for place, s in enumerate(order):
-        main_of[s] = mains[place][...]
-        spill_of[s] = spills[place][...]
+def near_place():
+    return jnp.where(lax.rem(lax.axis_index("col"), 2) == 1, 1, lax.axis_size("col") - 1)
+
+
+def late_body(taps, bands, ext, cols, pixels, share, *refs):
+    filters_ref, swapped_ref, passed_ref = refs[:3]
+    mains, spills, images = refs[3:6], refs[6:9], refs[9:13]
+    out_ref, tile_ref, *edge_refs, main_of, spill_of, y_ref = refs[13:]
+    count, reach = 4, taps // 2
+    middle = (lax.axis_index("col") == 1) | (lax.axis_index("col") == 2)
+    tile_ref[...] = jnp.where(middle, swapped_ref[...], passed_ref[...])
+    near = near_place()
+    places = [0, 2, near]
+    for s, main, spill in zip(places, mains, spills):
+        main_of[s] = main[...]
+        spill_of[s] = spill[...]
+    main_of[count - near], spill_of[count - near] = tile_parts(filters_ref[...], tile_ref[...], y_ref, taps, bands, ext, cols)
     column = column_of(ext, cols)
     lane = lax.broadcasted_iota(jnp.int32, (1, 128), 1)
     for s in range(count):
-        left, right = tile_flags("col", s)
+        left, right = tile_flags(s)
         from_left = jnp.where((column < reach) & left, spill_of[(s + 1) % count], 0.0)
         from_right = jnp.where((column >= cols - reach) & right, spill_of[(s - 1) % count], 0.0)
         picture = images[s][...].astype(jnp.float32) * share
         pad = jnp.zeros((bands, ext - picture.shape[1]), jnp.float32)
         picture = roll(jnp.concatenate([picture, pad], axis=1), reach * cols)
         value = main_of[s] + from_left + from_right - picture
-        out_ref[:, s * ext : (s + 1) * ext] = value
+        out_ref[s] = value
         up = jnp.where(lane < 2 * reach * cols, value[:, :128], 0.0)
         down = value[:, pixels : pixels + 128]
         if len(edge_refs) == 1:
@@ -117,55 +130,51 @@
         else:
             edges = [up, down]
         for ref, edge in zip(edge_refs, edges):
-            ref[:, s * 128 : (s + 1) * 128] = edge
-
-
-def join_body(count, ext, pixels, turn, *refs):
+            ref[s] = edge
+
+
+def join_body(count, pixels, turn, *refs):
     part_ref, *edge_refs, out_ref, send_ref = refs
-    bands = part_ref.shape[0]
+    bands = part_ref.shape[1]
 
     def turned(x, step):
         step %= bands
         return x if step == 0 else jnp.concatenate([x[bands - step :], x[: bands - step]], axis=0)
 
     for s in range(count):
-        at = s * ext
-        pieces = [turned(ref[:, s * 128 : (s + 1) * 128], turn * sign) for ref, sign in zip(edge_refs, (-1, 1))]
+        pieces = [turned(ref[s], turn * sign) for ref, sign in zip(edge_refs, (-1, 1))]
         if len(pieces) == 1:
             first = lax.axis_index("row") == 0
             pieces = [jnp.where(first, pieces[0], 0.0), jnp.where(first, 0.0, pieces[0])]
         below, above = pieces
-        own = part_ref[:, at : at + ext]
+        own = part_ref[s]
         parts = [own[:, :128] + above, own[:, 128:pixels], own[:, pixels : pixels + 128] + below, own[:, pixels + 128 :]]
         value = jnp.concatenate([part for part in parts if part.shape[1]], axis=1)
-        out_ref[:, at : at + ext] = value
-        send_ref[:, at : at + ext] = value.astype(jnp.bfloat16)
-
-
-def resid_body(ext, rows, cols, count, reach, peers, *refs):
+        out_ref[s] = value
+        send_ref[s] = value.astype(jnp.bfloat16)
+
+
+def resid_body(ext, rows, cols, reach, peers, *refs):
     own_ref, others, out_ref = refs[0], refs[1 : 1 + peers], refs[1 + peers]
     line = lax.broadcasted_iota(jnp.int32, (1, ext), 1) // cols
     place, places = lax.axis_index("row"), lax.axis_size("row")
     real = ((line >= reach) | (place > 0)) & ((line < rows + reach) | (place < places - 1)) & (line < rows + 2 * reach)
-    for s in range(count):
-        value = own_ref[:, s * ext : (s + 1) * ext]
+    for s in range(out_ref.shape[0]):
+        value = own_ref[s]
         for other in others:
-            value = value + other[:, s * ext : (s + 1) * ext].astype(jnp.float32)
-        out_ref[:, s * ext : (s + 1) * ext] = jnp.where(real, value, 0.0).astype(jnp.bfloat16).astype(jnp.float32)
-
-
-def windows_of(taps, bands, ext, rows, cols, count, s, resid_ref, windows_ref):
+            value = value + other[s].astype(jnp.float32)
+        out_ref[s] = jnp.where(real, value, 0.0).astype(jnp.bfloat16).astype(jnp.float32)
+
+
+def windows_of(taps, bands, ext, rows, cols, s, resid_ref, windows_ref):
     reach = taps // 2
     pixels = rows * cols
+    count = resid_ref.shape[0]
     column = column_of(ext, cols)
-
-    def tile(s):
-        return resid_ref[:, s * ext : (s + 1) * ext]
-
-    left, right = tile_flags("col", s)
-    own = tile(s)
-    to_left = jnp.where(left, tile((s + 1) % count), 0.0)
-    to_right = jnp.where(right, tile((s - 1) % count), 0.0)
+    left, right = tile_flags(s)
+    own = resid_ref[s]
+    to_left = jnp.where(left, resid_ref[lax.rem(s + 1, count)], 0.0)
+    to_right = jnp.where(right, resid_ref[lax.rem(s + count - 1, count)], 0.0)
     for b in range(taps):
         step = b - reach
         if step == 0:
@@ -180,16 +189,22 @@
             windows_ref[at : at + bands, :] = part.astype(jnp.bfloat16)
 
 
-def back_body(taps, bands, ext, rows, cols, count, s, peers, *refs):
+def back_body(taps, bands, ext, rows, cols, which, peers, *refs):
+    near = near_place()
+    s = {"own": 0, "two": 2, "near": near, "far": 4 - near}[which]
     turned_ref = refs[0]
     if peers is None:
         resid_ref, (windows_ref, back_ref) = refs[1], refs[2:]
     else:
         windows_ref, back_ref, resid_ref = refs[-3:]
-        resid_body(ext, rows, cols, count, taps // 2, peers, *refs[1:-3], resid_ref)
-    windows_of(taps, bands, ext, rows, cols, count, s, resid_ref, windows_ref)
+        resid_body(ext, rows, cols, taps // 2, peers, *refs[1:-3], resid_ref)
+    windows_of(taps, bands, ext, rows, cols, s, resid_ref, windows_ref)
     back = jnp.dot(turned_ref[...], windows_ref[...], preferred_element_type=jnp.float32)
     back_ref[...] = back.astype(back_ref.dtype)
+
+
+def merge_body(back_ref, passed_ref, out_ref):
+    out_ref[...] = (back_ref[...] + passed_ref[...].astype(jnp.float32)).astype(jnp.bfloat16)
 
 
 def grad_body(count, *refs):
@@ -230,10 +245,10 @@
     ext = -(-(rows + 2 * reach) * cols // 128) * 128
     row_at, col_at = lax.axis_index("row"), lax.axis_index("col")
 
-    order = column_order(count)
-    tiles = {0: codes.reshape(pixels, atoms)}
-    for s in order:
-        tiles[s] = shifted(codes, "col", s).reshape(pixels, atoms)
+    assert count == 4
+    tile = codes.reshape(pixels, atoms)
+    two = along(codes, TWO).reshape(pixels, atoms)
+    near = along(codes, NEAR).reshape(pixels, atoms)
 
     own_filters = jnp.transpose(master, (1, 2, 0, 3)).reshape(taps * taps, own_bands, atoms).astype(jnp.bfloat16)
     filters = [own_filters]
@@ -249,31 +264,34 @@
     for s in range(count):
         images.append(pieces[s] if s == 0 else shifted(pieces[s], "col", s))
 
+    passed = along(two, [(2, 3), (1, 0)])
+    swapped = along(tile, INNER)
+
     size = struct((bands, ext), jnp.float32)
     y_scratch = [pltpu.VMEM((taps * taps * bands, pixels), jnp.float32)]
     tile_flops = 2 * taps * taps * bands * pixels * atoms
     mains, spills = [], []
-    early = [0] + order[:-1]
-    for s in early:
+    for early in [tile, two, near]:
         body = functools.partial(early_body, taps, bands, ext, cols)
-        main, spill = call(body, [size, size], [filters, tiles[s]], tile_flops, y_scratch)
+        main, spill = call(body, [size, size], [filters, early], tile_flops, y_scratch)
         mains.append(main)
         spills.append(spill)
-    edge = struct((bands, count * 128), jnp.float32)
-    part, *edges = call(
-        functools.partial(late_body, taps, bands, ext, cols, pixels, tuple(early), 1.0 / peers),
-        [struct((bands, count * ext), jnp.float32)] + [edge] * (1 if groups == 2 else 2),
-        [filters, tiles[order[-1]], *mains, *spills, *images],
+    edge = struct((count, bands, 128), jnp.float32)
+    part_shape = (count, bands, ext)
+    part, far, *edges = call(
+        functools.partial(late_body, taps, bands, ext, cols, pixels, 1.0 / peers),
+        [struct(part_shape, jnp.float32), struct(tile.shape, tile.dtype)] + [edge] * (1 if groups == 2 else 2),
+        [filters, swapped, passed, *mains, *spills, *images],
         tile_flops,
-        y_scratch,
+        [pltpu.VMEM(part_shape, jnp.float32)] * 2 + y_scratch,
     )
     if groups == 2:
         edges = [shifted(edges[0], "row", 1)]
     else:
         edges = [moved_on(edges[0], "row", -1), moved_on(edges[1], "row", 1)]
     part, send = call(
-        functools.partial(join_body, count, ext, pixels, own_bands),
-        [struct(part.shape, jnp.float32), struct(part.shape, jnp.bfloat16)],
+        functools.partial(join_body, count, pixels, own_bands),
+        [struct(part_shape, jnp.float32), struct(part_shape, jnp.bfloat16)],
         [part, *edges],
     )
     if peers <= 4:
@@ -283,28 +301,26 @@
     else:
         others = [(lax.psum(send, "atom").astype(jnp.float32) - send.astype(jnp.float32)).astype(jnp.bfloat16)]
 
-    windows, received = {}, []
-    for place, s in enumerate(order + [0]):
-        body = functools.partial(
-            back_body, taps, bands, ext, rows, cols, count, s, len(others) if place == 0 else None
-        )
-        outs = [
-            struct((taps * taps * bands, pixels), jnp.bfloat16),
-            struct((atoms, pixels), jnp.bfloat16 if s else jnp.float32),
-        ]
-        if place == 0:
-            windows[s], back, resid = call(
-                body, outs + [struct(part.shape, jnp.float32)], [turned, part, *others], tile_flops
-            )
-        else:
-            windows[s], back = call(body, outs, [turned, resid], tile_flops)
-        if s:
-            received.append(shifted(back, "col", -s))
-    own_back = back
+    def back_of(which, dtype, *args, peers=None):
+        outs = [struct((taps * taps * bands, pixels), jnp.bfloat16), struct((atoms, pixels), dtype)]
+        if peers is not None:
+            outs.append(struct(part_shape, jnp.float32))
+        body = functools.partial(back_body, taps, bands, ext, rows, cols, which, peers)
+        return call(body, outs, [turned, *args], tile_flops)
+
+    far_windows, far_back, resid = back_of("far", jnp.bfloat16, part, *others, peers=len(others))
+    home_pass = along(far_back, [(3, 2), (0, 1)])
+    home_swap = along(far_back, INNER)
+    near_windows, near_back = back_of("near", jnp.bfloat16, resid)
+    home_near = along(near_back, NEAR)
+    two_windows, two_back = back_of("two", jnp.float32, resid)
+    own_windows, own_back = back_of("own", jnp.float32, resid)
+    (two_back,) = call(merge_body, [struct((atoms, pixels), jnp.bfloat16)], [two_back, home_pass])
+    home_two = along(two_back, TWO)
     (grad,) = call(
         functools.partial(grad_body, count),
         [struct((taps * taps * bands, atoms), jnp.float32)],
-        [windows[s] for s in range(count)] + [tiles[s] for s in range(count)],
+        [own_windows, two_windows, near_windows, far_windows, tile, two, near, far],
         tile_flops * count,
     )
     grad = grad.reshape(taps * taps, groups, own_bands, atoms)
@@ -316,13 +332,9 @@
     own_grad = jnp.transpose(own_grad.reshape(taps, taps, own_bands, atoms), (2, 0, 1, 3))
     new_dictionary, new_moment, new_second = adam_update(master, moment, second, own_grad)
     (new_codes,) = call(
-        codes_body, [struct((pixels, atoms), jnp.bfloat16)], [codes.reshape(pixels, atoms), own_back, *received]
+        codes_body, [struct((pixels, atoms), jnp.bfloat16)], [tile, own_back, home_near, home_swap, home_two]
     )
     return (new_codes.reshape(rows, cols, atoms), new_dictionary, new_moment, new_second)
-
-
-def column_order(count):
-    return sorted(range(1, count), key=lambda s: (abs(count - 2 * s), s))
 
 
 def solution(mesh):

time: 83.2 us -> 78.7 us (0.946)
  the two profiles are of different devices: /device:TPU:9 before, /device:TPU:0 now
where the time goes in v3:
time: 78.7 us; the launch traced here: 78.4 us
  waiting for transfers between devices  30.6 us (39%)
  starting transfers between devices  24.7 us (31%)
  Pallas kernels  11.8 us (15%)
  other arithmetic  6.1 us (8%)
  local copies, waits for them, and re-layouts  4.08 us (5%)
  between operations  1.06 us (1%)
    ppermute x8, waiting for transfers between devices, along(): return lax.ppermute(x, 'col', pairs)  22.8 us
    ppermute x8, starting transfers between devices, along(): return lax.ppermute(x, 'col', pairs)  15 us
    pallas_call x12, Pallas kernels, call(): pl.pallas_call(body, out_shape=outs, in_specs=[pl.BlockSpec(memory_space=...  11.8 us
    ppermute x6, starting transfers between devices, shifted(): lax.ppermute(x, axis, [(i, (i + step) % count) for i in range(count)])  6.21 us
    ppermute x6, waiting for transfers between devices, shifted(): lax.ppermute(x, axis, [(i, (i + step) % count) for i in range(count)])  4.5 us
    ppermute x3, starting transfers between devices, iteration(): lax.ppermute(send, 'atom', [(i, i ^ m) for i in range(peers)])  3.49 us
    ppermute x3, waiting for transfers between devices, iteration(): lax.ppermute(send, 'atom', [(i, i ^ m) for i in range(peers)])  3.37 us
    sub x1, other arithmetic, adam_update(): master - 0.05 * (new_moment / first_fix) / (jnp.sqrt(new_second / second_...  2.97 us
  transfers between devices with their start and end apart: 17, of which 8 were waited for; matrix products, arithmetic and copies ran while one was open for 4% of the time, Pallas kernels for 5%

profile of v3, /device:TPU:0, one launch (start us, length us, event | category | flops | bytes accessed | tf_op | source)
XLA Modules:
  0.0 78.4 jit_solution(6822604746876134619)
XLA Ops:
  0.7 1.6 %convert_element_type.16 = bf16[16,7,7,512]{3,0,2,1:T(8,128)(2,1)S(1)} convert(f32[16,7,7,512]{3,0,2,1:T(8,128)} %param.7) | non-fusion elementwise | flops 401408 | bytes 2408448 | tf_op jit(solution)/shard_map/convert_element_type | solution.py:253
  2.8 3.7 %collective-permute-start.2 = (bf16[16,16,512]{2,1,0:T(8,128)(2,1)S(1)}, bf16[16,16,512]{2,1,0:T(8,128)(2,1)S(1)}, u32[]{:S(2)}, u32[]{:S(2)}) collective-permute-start(bf16[16,16,512]{2,1,0:T(8,128)(2,1)S(1)} %copy-done), channel_id=1, source_target_pairs={{0,2},{1,3},{2,0},{3,1},{4,6},{5,7},{6,4},{7,5},{8,10},{9,11},{10,... | collective-permute-start | bytes 786440 | tf_op jit(solution)/shard_map/ppermute | solution.py:31
  6.5 1.6 %collective-permute-start.4 = (bf16[16,16,512]{2,1,0:T(8,128)(2,1)S(1)}, bf16[16,16,512]{2,1,0:T(8,128)(2,1)S(1)}, u32[]{:S(2)}, u32[]{:S(2)}) collective-permute-start(bf16[16,16,512]{2,1,0:T(8,128)(2,1)S(1)} %copy-done), channel_id=1, source_target_pairs={{0,1},{1,0},{2,3},{3,2},{4,5},{5,4},{6,7},{7,6},{8,9},{9,8},{10,11... | collective-permute-start | bytes 786440 | tf_op jit(solution)/shard_map/ppermute | solution.py:31
  9.7 2.2 %collective-permute-start.5 = (bf16[32,256]{1,0:T(8,128)(2,1)S(1)}, bf16[32,256]{1,0:T(8,128)(2,1)S(1)}, u32[]{:S(2)}, u32[]{:S(2)}) collective-permute-start(bf16[32,256]{1,0:T(8,128)(2,1)S(1)} %bitcast.56), channel_id=1, source_target_pairs={{0,1},{1,2},{2,3},{3,0},{4,5},{5,6},{6,7},{7,4},{8,9},{9,10},{10,1... | collective-permute-start | bytes 49160 | tf_op jit(solution)/shard_map/ppermute | solution.py:17
  11.9 7.4 %collective-permute-done.2 = bf16[16,16,512]{2,1,0:T(8,128)(2,1)S(1)} collective-permute-done((bf16[16,16,512]{2,1,0:T(8,128)(2,1)S(1)}, bf16[16,16,512]{2,1,0:T(8,128)(2,1)S(1)}, u32[]{:S(2)}, u32[]{:S(2)}) %collective-permute-start.2) | collective-permute-done | bytes 262176 | tf_op jit(solution)/shard_map/ppermute | solution.py:31
  19.3 1.3 %collective-permute-start.3 = (bf16[256,512]{1,0:T(8,128)(2,1)S(1)}, bf16[256,512]{1,0:T(8,128)(2,1)S(1)}, u32[]{:S(2)}, u32[]{:S(2)}) collective-permute-start(bf16[256,512]{1,0:T(8,128)(2,1)S(1)} %bitcast.42), channel_id=1, source_target_pairs={{2,3},{1,0},{6,7},{5,4},{10,11},{9,8},{14,15},{13,12},{18,19},{17,... | collective-permute-start | bytes 786440 | tf_op jit(solution)/shard_map/ppermute | solution.py:31
  20.6 1.3 %pad_maximum_fusion = bf16[49,32,512]{2,1,0:T(8,128)(2,1)S(1)} fusion(bf16[49,16,512]{2,1,0:T(8,128)(2,1)} %collective-permute-done, bf16[49,16,512]{2,1,0:T(8,128)(2,1)S(1)} %bitcast.50), kind=kLoop, calls=%fused_computation.5 | loop fusion | flops 3211264 | bytes 3211264 | tf_op jit(solution)/shard_map/concatenate | solution.py:257
  21.9 0.9 %shard_map.84 = (f32[32,384]{1,0:T(8,128)S(1)}, f32[32,384]{1,0:T(8,128)S(1)}) custom-call(bf16[1568,512]{1,0:T(8,128)(2,1)S(1)} %bitcast.27, bf16[256,512]{1,0:T(8,128)(2,1)S(1)} %bitcast.39), custom_call_target="tpu_custom_call" | custom-call | flops 411041792 | bytes 1966080 | tf_op jit(solution)/shard_map/pallas_call | solution.py:36
  22.8 0.9 %shard_map.85 = (f32[32,384]{1,0:T(8,128)S(1)}, f32[32,384]{1,0:T(8,128)S(1)}) custom-call(bf16[1568,512]{1,0:T(8,128)(2,1)S(1)} %bitcast.28, bf16[256,512]{1,0:T(8,128)(2,1)S(1)} %bitcast.43), custom_call_target="tpu_custom_call" | custom-call | flops 411041792 | bytes 1966080 | tf_op jit(solution)/shard_map/pallas_call | solution.py:36
  23.8 3.3 %collective-permute-start.7 = (bf16[32,256]{1,0:T(8,128)(2,1)S(1)}, bf16[32,256]{1,0:T(8,128)(2,1)S(1)}, u32[]{:S(2)}, u32[]{:S(2)}) collective-permute-start(bf16[32,256]{1,0:T(8,128)(2,1)S(1)} %bitcast.54), channel_id=1, source_target_pairs={{0,3},{1,0},{2,1},{3,2},{4,7},{5,4},{6,5},{7,6},{8,11},{9,8},{10,9... | collective-permute-start | bytes 49160 | tf_op jit(solution)/shard_map/ppermute | solution.py:17
  27.1 0.9 %shard_map.86 = (f32[32,384]{1,0:T(8,128)S(1)}, f32[32,384]{1,0:T(8,128)S(1)}) custom-call(bf16[1568,512]{1,0:T(8,128)(2,1)S(1)} %bitcast.29, bf16[256,512]{1,0:T(8,128)(2,1)S(1)} %bitcast.45), custom_call_target="tpu_custom_call" | custom-call | flops 411041792 | bytes 1966080 | tf_op jit(solution)/shard_map/pallas_call | solution.py:36
  28.1 3.2 %collective-permute-done.7.refs_12_ = bf16[32,256]{1,0:T(8,128)(2,1)S(1)} collective-permute-done((bf16[32,256]{1,0:T(8,128)(2,1)S(1)}, bf16[32,256]{1,0:T(8,128)(2,1)S(1)}, u32[]{:S(2)}, u32[]{:S(2)}) %collective-permute-start.7) | collective-permute-done | bytes 16416 | tf_op jit(solution)/shard_map/ppermute | solution.py:17
  31.3 1.0 %shard_map.87 = (f32[4,32,384]{2,1,0:T(8,128)S(1)}, bf16[256,512]{1,0:T(8,128)(2,1)S(1)}, f32[4,32,128]{2,1,0:T(8,128)S(1)}) custom-call(bf16[1568,512]{1,0:T(8,128)(2,1)S(1)} %bitcast.30, bf16[256,512]{1,0:T(8,128)(2,1)S(1)} %collective-permute-done.1.refs_1_, bf16[256,512]{1,0:T(8,128)(2,1)S(1)} %collective-permute-done.3.refs_2_, ...), custom_call_target="tpu_custom_call" | custom-call | flops 411041792 | bytes 3014656 | tf_op jit(solution)/shard_map/pallas_call | solution.py:36
  32.4 1.2 %collective-permute-done.8.refs_1_ = f32[4,32,128]{2,1,0:T(8,128)S(1)} collective-permute-done((f32[4,32,128]{2,1,0:T(8,128)S(1)}, f32[4,32,128]{2,1,0:T(8,128)S(1)}, u32[]{:S(2)}, u32[]{:S(2)}) %collective-permute-start.8) | collective-permute-done | bytes 65568 | tf_op jit(solution)/shard_map/ppermute | solution.py:17
  34.3 2.4 %collective-permute-start.9 = (bf16[4,32,384]{2,1,0:T(8,128)(2,1)}, bf16[4,32,384]{2,1,0:T(8,128)(2,1)}, u32[]{:S(2)}, u32[]{:S(2)}) collective-permute-start(bf16[4,32,384]{2,1,0:T(8,128)(2,1)} %get-tuple-element.33), channel_id=1, source_target_pairs={{0,24},{8,16},{16,8},{24,0},{1,25},{9,17},{17,9},{25,1},{2,26},{10... | collective-permute-start | bytes 294920 | tf_op jit(solution)/shard_map/ppermute | solution.py:300
  37.8 1.3 %copy.18 = bf16[1568,512]{0,1:T(8,128)(2,1)S(1)} copy(bf16[1568,512]{1,0:T(8,128)(2,1)S(1)} %bitcast.31) | data formatting | bytes 3211264 | tf_op jit(solution)/shard_map/reshape | solution.py:257
  39.1 1.4 %collective-permute-done.9.refs_2_ = bf16[4,32,384]{2,1,0:T(8,128)(2,1)} collective-permute-done((bf16[4,32,384]{2,1,0:T(8,128)(2,1)}, bf16[4,32,384]{2,1,0:T(8,128)(2,1)}, u32[]{:S(2)}, u32[]{:S(2)}) %collective-permute-start.9) | collective-permute-done | bytes 98336 | tf_op jit(solution)/shard_map/ppermute | solution.py:300
  40.5 2.0 %collective-permute-done.10.refs_3_ = bf16[4,32,384]{2,1,0:T(8,128)(2,1)} collective-permute-done((bf16[4,32,384]{2,1,0:T(8,128)(2,1)}, bf16[4,32,384]{2,1,0:T(8,128)(2,1)}, u32[]{:S(2)}, u32[]{:S(2)}) %collective-permute-start.10) | collective-permute-done | bytes 98336 | tf_op jit(solution)/shard_map/ppermute | solution.py:300
  42.5 1.9 %shard_map.89 = (bf16[1568,256]{1,0:T(8,128)(2,1)S(1)}, bf16[512,256]{1,0:T(8,128)(2,1)S(1)}, f32[4,32,384]{2,1,0:T(8,128)S(1)}) custom-call(bf16[512,1568]{1,0:T(8,128)(2,1)S(1)} %bitcast.32, f32[4,32,384]{2,1,0:T(8,128)S(1)} %get-tuple-element.32.refs_1_, bf16[4,32,384]{2,1,0:T(8,128)(2,1)} %collective-permute-done.9.refs_2_, ...), custom_call_target="tpu_custom_call" | custom-call | flops 411041792 | bytes 3358720 | tf_op jit(solution)/shard_map/pallas_call | solution.py:36
  44.4 0.9 %shard_map.90 = (bf16[1568,256]{1,0:T(8,128)(2,1)S(1)}, f32[512,256]{1,0:T(8,128)S(1)}) custom-call(bf16[512,1568]{1,0:T(8,128)(2,1)S(1)} %bitcast.33, f32[4,32,384]{2,1,0:T(8,128)S(1)} %get-tuple-element.34.refs_1_), custom_call_target="tpu_custom_call" | custom-call | flops 411041792 | bytes 3129344 | tf_op jit(solution)/shard_map/pallas_call | solution.py:36
  45.3 0.9 %shard_map.91 = (bf16[1568,256]{1,0:T(8,128)(2,1)S(1)}, bf16[512,256]{1,0:T(8,128)(2,1)S(1)}) custom-call(bf16[512,1568]{1,0:T(8,128)(2,1)S(1)} %bitcast.34, f32[4,32,384]{2,1,0:T(8,128)S(1)} %get-tuple-element.34.refs_1_), custom_call_target="tpu_custom_call" | custom-call | flops 411041792 | bytes 2867200 | tf_op jit(solution)/shard_map/pallas_call | solution.py:36
  46.3 0.9 %shard_map.92 = (bf16[1568,256]{1,0:T(8,128)(2,1)S(1)}, f32[512,256]{1,0:T(8,128)S(1)}) custom-call(bf16[512,1568]{1,0:T(8,128)(2,1)S(1)} %bitcast.35, f32[4,32,384]{2,1,0:T(8,128)S(1)} %get-tuple-element.34.refs_1_), custom_call_target="tpu_custom_call" | custom-call | flops 411041792 | bytes 3129344 | tf_op jit(solution)/shard_map/pallas_call | solution.py:36
  47.2 1.8 %shard_map.95 = f32[1568,512]{1,0:T(8,128)S(1)} custom-call(bf16[1568,256]{1,0:T(8,128)(2,1)S(1)} %get-tuple-element.39.refs_0_, bf16[1568,256]{1,0:T(8,128)(2,1)S(1)} %get-tuple-element.40.refs_1_, bf16[1568,256]{1,0:T(8,128)(2,1)S(1)} %get-tuple-element.41.refs_2_, bf16[1568,256]{1,0:T(8,128)(2,1)S(1)} %get-tuple-element.42.refs_3_, ...), custom_call_target="tpu_custom_call" | custom-call | flops 1644167168 | bytes 7471104 | tf_op jit(solution)/shard_map/pallas_call | solution.py:36
  49.2 2.1 %collective-permute-start.14 = (bf16[512,256]{1,0:T(8,128)(2,1)S(1)}, bf16[512,256]{1,0:T(8,128)(2,1)S(1)}, u32[]{:S(2)}, u32[]{:S(2)}) collective-permute-start(bf16[512,256]{1,0:T(8,128)(2,1)S(1)} %get-tuple-element.37), channel_id=1, source_target_pairs={{3,2},{0,1},{7,6},{4,5},{11,10},{8,9},{15,14},{12,13},{19,18},{16,... | collective-permute-start | bytes 786440 | tf_op jit(solution)/shard_map/ppermute | solution.py:31
  52.0 1.9 %collective-permute-start.12 = (bf16[512,256]{1,0:T(8,128)(2,1)S(1)}, bf16[512,256]{1,0:T(8,128)(2,1)S(1)}, u32[]{:S(2)}, u32[]{:S(2)}) collective-permute-start(bf16[512,256]{1,0:T(8,128)(2,1)S(1)} %get-tuple-element.36), channel_id=1, source_target_pairs={{0,1},{1,0},{2,3},{3,2},{4,5},{5,4},{6,7},{7,6},{8,9},{9,8},{10,11... | collective-permute-start | bytes 786440 | tf_op jit(solution)/shard_map/ppermute | solution.py:31
  53.9 4.1 %collective-permute-done.14.passed_ref = bf16[512,256]{1,0:T(8,128)(2,1)S(1)} collective-permute-done((bf16[512,256]{1,0:T(8,128)(2,1)S(1)}, bf16[512,256]{1,0:T(8,128)(2,1)S(1)}, u32[]{:S(2)}, u32[]{:S(2)}) %collective-permute-start.14) | collective-permute-done | bytes 262176 | tf_op jit(solution)/shard_map/ppermute | solution.py:31
  58.0 3.2 %collective-permute-start.15 = (bf16[512,256]{1,0:T(8,128)(2,1)S(1)}, bf16[512,256]{1,0:T(8,128)(2,1)S(1)}, u32[]{:S(2)}, u32[]{:S(2)}) collective-permute-start(bf16[512,256]{1,0:T(8,128)(2,1)S(1)} %shard_map.93), channel_id=1, source_target_pairs={{0,2},{1,3},{2,0},{3,1},{4,6},{5,7},{6,4},{7,5},{8,10},{9,11},{10,... | collective-permute-start | bytes 786440 | tf_op jit(solution)/shard_map/ppermute | solution.py:31
  61.2 2.4 %collective-permute-done.12.refs_2_ = bf16[512,256]{1,0:T(8,128)(2,1)S(1)} collective-permute-done((bf16[512,256]{1,0:T(8,128)(2,1)S(1)}, bf16[512,256]{1,0:T(8,128)(2,1)S(1)}, u32[]{:S(2)}, u32[]{:S(2)}) %collective-permute-start.12) | collective-permute-done | bytes 262176 | tf_op jit(solution)/shard_map/ppermute | solution.py:31
  63.6 8.8 %collective-permute-done.15.refs_4_ = bf16[512,256]{1,0:T(8,128)(2,1)S(1)} collective-permute-done((bf16[512,256]{1,0:T(8,128)(2,1)S(1)}, bf16[512,256]{1,0:T(8,128)(2,1)S(1)}, u32[]{:S(2)}, u32[]{:S(2)}) %collective-permute-start.15) | collective-permute-done | bytes 262176 | tf_op jit(solution)/shard_map/ppermute | solution.py:31
  72.5 0.9 %shard_map.94 = bf16[256,512]{1,0:T(8,128)(2,1)} custom-call(bf16[256,512]{1,0:T(8,128)(2,1)S(1)} %bitcast.41, f32[512,256]{1,0:T(8,128)S(1)} %get-tuple-element.35.refs_1_, bf16[512,256]{1,0:T(8,128)(2,1)S(1)} %collective-permute-done.12.refs_2_, bf16[512,256]{1,0:T(8,128)(2,1)S(1)} %collective-permute-done.13.refs_3_, ...), custom_call_target="tpu_custom_call" | custom-call | bytes 1835008 | tf_op jit(solution)/shard_map/pallas_call | solution.py:36
  74.0 1.0 %copy-done.8 = f32[16,7,7,512]{3,0,2,1:T(8,128)S(1)} copy-done((f32[16,7,7,512]{3,0,2,1:T(8,128)S(1)}, f32[16,7,7,512]{3,0,2,1:T(8,128)}, u32[]{:S(2)}) %copy-start.8) | copy-done | bytes 1605656
  75.4 3.0 %divide_subtract_fusion = (f32[16,7,7,512]{3,0,2,1:T(8,128)}, f32[16,7,7,512]{3,0,2,1:T(8,128)}, f32[16,7,7,512]{3,0,2,1:T(8,128)}) fusion(f32[16,7,7,512]{3,0,2,1:T(8,128)S(1)} %copy-done.8, f32[16,7,7,512]{3,0,2,1:T(8,128)S(1)} %bitcast.48, f32[16,7,7,512]{3,0,2,1:T(8,128)S(1)} %copy-done.9, f32[16,7,7,512]{3,0,2,1:T(8,128)S(1)} %copy-done.10), kind=kLoop, calls=%fused_computation.6 | loop fusion | flops 4816896 | bytes 11239424 | tf_op jit(solution)/shard_map/sub | solution.py:232
  (49 shorter events, 6.0 us)
Async XLA Ops:
  0.6 2.2 %copy-start = (bf16[16,16,512]{2,1,0:T(8,128)(2,1)S(1)}, bf16[16,16,512]{2,1,0:T(8,128)(2,1)}, u32[]{:S(2)}) copy-start(bf16[16,16,512]{2,1,0:T(8,128)(2,1)} %param.5) | copy-start | bytes 786436
  0.6 8.1 %copy-start.11 = (bf16[16,16,128]{2,1,0:T(8,128)(2,1)S(1)}, bf16[16,16,128]{2,1,0:T(8,128)(2,1)}, u32[]{:S(2)}) copy-start(bf16[16,16,128]{2,1,0:T(8,128)(2,1)} %param.6) | copy-start | bytes 196612
  2.2 17.1 %collective-permute-start = (bf16[49,16,512]{2,1,0:T(8,128)(2,1)S(1)}, bf16[49,16,512]{2,1,0:T(8,128)(2,1)}, u32[]{:S(2)}, u32[]{:S(2)}) collective-permute-start(bf16[49,16,512]{2,1,0:T(8,128)(2,1)S(1)} %bitcast.49), channel_id=1, source_target_pairs={{0,4},{4,0},{1,5},{5,1},{2,6},{6,2},{3,7},{7,3},{8,12},{12,8},{9,1... | collective-permute-start | bytes 2408456 | tf_op jit(solution)/shard_map/ppermute | solution.py:17
  2.8 16.5 %collective-permute-start.2 = (bf16[16,16,512]{2,1,0:T(8,128)(2,1)S(1)}, bf16[16,16,512]{2,1,0:T(8,128)(2,1)S(1)}, u32[]{:S(2)}, u32[]{:S(2)}) collective-permute-start(bf16[16,16,512]{2,1,0:T(8,128)(2,1)S(1)} %copy-done), channel_id=1, source_target_pairs={{0,2},{1,3},{2,0},{3,1},{4,6},{5,7},{6,4},{7,5},{8,10},{9,11},{10,... | collective-permute-start | bytes 786440 | tf_op jit(solution)/shard_map/ppermute | solution.py:31
  6.5 17.3 %collective-permute-start.4 = (bf16[16,16,512]{2,1,0:T(8,128)(2,1)S(1)}, bf16[16,16,512]{2,1,0:T(8,128)(2,1)S(1)}, u32[]{:S(2)}, u32[]{:S(2)}) collective-permute-start(bf16[16,16,512]{2,1,0:T(8,128)(2,1)S(1)} %copy-done), channel_id=1, source_target_pairs={{0,1},{1,0},{2,3},{3,2},{4,5},{5,4},{6,7},{7,6},{8,9},{9,8},{10,11... | collective-permute-start | bytes 786440 | tf_op jit(solution)/shard_map/ppermute | solution.py:31
  8.0 23.3 %collective-permute-start.1 = (bf16[256,512]{1,0:T(8,128)(2,1)S(1)}, bf16[256,512]{1,0:T(8,128)(2,1)S(1)}, u32[]{:S(2)}, u32[]{:S(2)}) collective-permute-start(bf16[256,512]{1,0:T(8,128)(2,1)S(1)} %bitcast.38), channel_id=1, source_target_pairs={{1,2},{2,1},{5,6},{6,5},{9,10},{10,9},{13,14},{14,13},{17,18},{18,... | collective-permute-start | bytes 786440 | tf_op jit(solution)/shard_map/ppermute | solution.py:31
  9.7 18.4 %collective-permute-start.5 = (bf16[32,256]{1,0:T(8,128)(2,1)S(1)}, bf16[32,256]{1,0:T(8,128)(2,1)S(1)}, u32[]{:S(2)}, u32[]{:S(2)}) collective-permute-start(bf16[32,256]{1,0:T(8,128)(2,1)S(1)} %bitcast.56), channel_id=1, source_target_pairs={{0,1},{1,2},{2,3},{3,0},{4,5},{5,6},{6,7},{7,4},{8,9},{9,10},{10,1... | collective-permute-start | bytes 49160 | tf_op jit(solution)/shard_map/ppermute | solution.py:17
  19.3 3.5 %copy-start.2 = (bf16[16,16,512]{2,1,0:T(8,128)(2,1)}, bf16[16,16,512]{2,1,0:T(8,128)(2,1)S(1)}, u32[]{:S(2)}) copy-start(bf16[16,16,512]{2,1,0:T(8,128)(2,1)S(1)} %collective-permute-done.2) | copy-start | bytes 786436
  19.3 8.8 %collective-permute-start.6 = (bf16[32,256]{1,0:T(8,128)(2,1)S(1)}, bf16[32,256]{1,0:T(8,128)(2,1)S(1)}, u32[]{:S(2)}, u32[]{:S(2)}) collective-permute-start(bf16[32,256]{1,0:T(8,128)(2,1)S(1)} %bitcast.55), channel_id=1, source_target_pairs={{0,2},{1,3},{2,0},{3,1},{4,6},{5,7},{6,4},{7,5},{8,10},{9,11},{10,... | collective-permute-start | bytes 49160 | tf_op jit(solution)/shard_map/ppermute | solution.py:17
  19.3 12.0 %collective-permute-start.3 = (bf16[256,512]{1,0:T(8,128)(2,1)S(1)}, bf16[256,512]{1,0:T(8,128)(2,1)S(1)}, u32[]{:S(2)}, u32[]{:S(2)}) collective-permute-start(bf16[256,512]{1,0:T(8,128)(2,1)S(1)} %bitcast.42), channel_id=1, source_target_pairs={{2,3},{1,0},{6,7},{5,4},{10,11},{9,8},{14,15},{13,12},{18,19},{17,... | collective-permute-start | bytes 786440 | tf_op jit(solution)/shard_map/ppermute | solution.py:31
  23.8 8.5 %copy-start.4 = (bf16[16,16,512]{2,1,0:T(8,128)(2,1)}, bf16[16,16,512]{2,1,0:T(8,128)(2,1)S(1)}, u32[]{:S(2)}) copy-start(bf16[16,16,512]{2,1,0:T(8,128)(2,1)S(1)} %collective-permute-done.4) | copy-start | bytes 786436
  23.8 7.5 %collective-permute-start.7 = (bf16[32,256]{1,0:T(8,128)(2,1)S(1)}, bf16[32,256]{1,0:T(8,128)(2,1)S(1)}, u32[]{:S(2)}, u32[]{:S(2)}) collective-permute-start(bf16[32,256]{1,0:T(8,128)(2,1)S(1)} %bitcast.54), channel_id=1, source_target_pairs={{0,3},{1,0},{2,1},{3,2},{4,7},{5,4},{6,5},{7,6},{8,11},{9,8},{10,9... | collective-permute-start | bytes 49160 | tf_op jit(solution)/shard_map/ppermute | solution.py:17
  32.3 4.9 %copy-start.6 = (bf16[256,512]{1,0:T(8,128)(2,1)}, bf16[256,512]{1,0:T(8,128)(2,1)S(1)}, u32[]{:S(2)}) copy-start(bf16[256,512]{1,0:T(8,128)(2,1)S(1)} %get-tuple-element.43.refs_7_) | copy-start | bytes 786436
  32.3 1.3 %collective-permute-start.8 = (f32[4,32,128]{2,1,0:T(8,128)S(1)}, f32[4,32,128]{2,1,0:T(8,128)S(1)}, u32[]{:S(2)}, u32[]{:S(2)}) collective-permute-start(f32[4,32,128]{2,1,0:T(8,128)S(1)} %get-tuple-element.31), channel_id=1, source_target_pairs={{0,4},{4,0},{1,5},{5,1},{2,6},{6,2},{3,7},{7,3},{8,12},{12,8},{9,1... | collective-permute-start | bytes 196616 | tf_op jit(solution)/shard_map/ppermute | solution.py:17
  34.3 6.2 %collective-permute-start.9 = (bf16[4,32,384]{2,1,0:T(8,128)(2,1)}, bf16[4,32,384]{2,1,0:T(8,128)(2,1)}, u32[]{:S(2)}, u32[]{:S(2)}) collective-permute-start(bf16[4,32,384]{2,1,0:T(8,128)(2,1)} %get-tuple-element.33), channel_id=1, source_target_pairs={{0,24},{8,16},{16,8},{24,0},{1,25},{9,17},{17,9},{25,1},{2,26},{10... | collective-permute-start | bytes 294920 | tf_op jit(solution)/shard_map/ppermute | solution.py:300
  36.7 5.8 %collective-permute-start.10 = (bf16[4,32,384]{2,1,0:T(8,128)(2,1)}, bf16[4,32,384]{2,1,0:T(8,128)(2,1)}, u32[]{:S(2)}, u32[]{:S(2)}) collective-permute-start(bf16[4,32,384]{2,1,0:T(8,128)(2,1)} %get-tuple-element.33), channel_id=1, source_target_pairs={{0,16},{8,24},{16,0},{24,8},{1,17},{9,25},{17,1},{25,9},{2,18},{10... | collective-permute-start | bytes 294920 | tf_op jit(solution)/shard_map/ppermute | solution.py:300
  37.2 5.3 %collective-permute-start.11 = (bf16[4,32,384]{2,1,0:T(8,128)(2,1)}, bf16[4,32,384]{2,1,0:T(8,128)(2,1)}, u32[]{:S(2)}, u32[]{:S(2)}) collective-permute-start(bf16[4,32,384]{2,1,0:T(8,128)(2,1)} %get-tuple-element.33), channel_id=1, source_target_pairs={{0,8},{8,0},{16,24},{24,16},{1,9},{9,1},{17,25},{25,17},{2,10},{10... | collective-permute-start | bytes 294920 | tf_op jit(solution)/shard_map/ppermute | solution.py:300
  45.3 1.8 %copy-start.1 = (bf16[16,16,512]{2,1,0:T(8,128)(2,1)S(1)}, bf16[16,16,512]{2,1,0:T(8,128)(2,1)}, u32[]{:S(2)}) copy-start(bf16[16,16,512]{2,1,0:T(8,128)(2,1)} %param.5) | copy-start | bytes 786436
  45.3 1.8 %copy-start.3 = (bf16[16,16,512]{2,1,0:T(8,128)(2,1)S(1)}, bf16[16,16,512]{2,1,0:T(8,128)(2,1)}, u32[]{:S(2)}) copy-start(bf16[16,16,512]{2,1,0:T(8,128)(2,1)} %copy-done.2) | copy-start | bytes 786436
  45.3 1.8 %copy-start.5 = (bf16[16,16,512]{2,1,0:T(8,128)(2,1)S(1)}, bf16[16,16,512]{2,1,0:T(8,128)(2,1)}, u32[]{:S(2)}) copy-start(bf16[16,16,512]{2,1,0:T(8,128)(2,1)} %copy-done.4) | copy-start | bytes 786436
  45.3 1.8 %copy-start.7 = (bf16[256,512]{1,0:T(8,128)(2,1)S(1)}, bf16[256,512]{1,0:T(8,128)(2,1)}, u32[]{:S(2)}) copy-start(bf16[256,512]{1,0:T(8,128)(2,1)} %copy-done.6) | copy-start | bytes 786436
  49.2 24.2 %collective-permute-start.16 = (bf16[49,16,512]{2,1,0:T(8,128)(2,1)S(1)}, bf16[49,16,512]{2,1,0:T(8,128)(2,1)S(1)}, u32[]{:S(2)}, u32[]{:S(2)}) collective-permute-start(bf16[49,16,512]{2,1,0:T(8,128)(2,1)S(1)} %fusion.2), channel_id=1, source_target_pairs={{0,4},{4,0},{1,5},{5,1},{2,6},{6,2},{3,7},{7,3},{8,12},{12,8},{9,1... | collective-permute-start | bytes 2408456 | tf_op jit(solution)/shard_map/ppermute | solution.py:17
  49.2 8.8 %collective-permute-start.14 = (bf16[512,256]{1,0:T(8,128)(2,1)S(1)}, bf16[512,256]{1,0:T(8,128)(2,1)S(1)}, u32[]{:S(2)}, u32[]{:S(2)}) collective-permute-start(bf16[512,256]{1,0:T(8,128)(2,1)S(1)} %get-tuple-element.37), channel_id=1, source_target_pairs={{3,2},{0,1},{7,6},{4,5},{11,10},{8,9},{15,14},{12,13},{19,18},{16,... | collective-permute-start | bytes 786440 | tf_op jit(solution)/shard_map/ppermute | solution.py:31
  51.3 12.3 %collective-permute-start.13 = (bf16[512,256]{1,0:T(8,128)(2,1)S(1)}, bf16[512,256]{1,0:T(8,128)(2,1)S(1)}, u32[]{:S(2)}, u32[]{:S(2)}) collective-permute-start(bf16[512,256]{1,0:T(8,128)(2,1)S(1)} %get-tuple-element.37), channel_id=1, source_target_pairs={{1,2},{2,1},{5,6},{6,5},{9,10},{10,9},{13,14},{14,13},{17,18},{18,... | collective-permute-start | bytes 786440 | tf_op jit(solution)/shard_map/ppermute | solution.py:31
  52.0 11.6 %collective-permute-start.12 = (bf16[512,256]{1,0:T(8,128)(2,1)S(1)}, bf16[512,256]{1,0:T(8,128)(2,1)S(1)}, u32[]{:S(2)}, u32[]{:S(2)}) collective-permute-start(bf16[512,256]{1,0:T(8,128)(2,1)S(1)} %get-tuple-element.36), channel_id=1, source_target_pairs={{0,1},{1,0},{2,3},{3,2},{4,5},{5,4},{6,7},{7,6},{8,9},{9,8},{10,11... | collective-permute-start | bytes 786440 | tf_op jit(solution)/shard_map/ppermute | solution.py:31
  58.0 14.4 %collective-permute-start.15 = (bf16[512,256]{1,0:T(8,128)(2,1)S(1)}, bf16[512,256]{1,0:T(8,128)(2,1)S(1)}, u32[]{:S(2)}, u32[]{:S(2)}) collective-permute-start(bf16[512,256]{1,0:T(8,128)(2,1)S(1)} %shard_map.93), channel_id=1, source_target_pairs={{0,2},{1,3},{2,0},{3,1},{4,6},{5,7},{6,4},{7,5},{8,10},{9,11},{10,... | collective-permute-start | bytes 786440 | tf_op jit(solution)/shard_map/ppermute | solution.py:31
  72.5 1.5 %copy-start.10 = (f32[16,7,7,512]{3,0,2,1:T(8,128)S(1)}, f32[16,7,7,512]{3,0,2,1:T(8,128)}, u32[]{:S(2)}) copy-start(f32[16,7,7,512]{3,0,2,1:T(8,128)} %param.9) | copy-start | bytes 4816900
  73.4 1.5 %copy-start.8 = (f32[16,7,7,512]{3,0,2,1:T(8,128)S(1)}, f32[16,7,7,512]{3,0,2,1:T(8,128)}, u32[]{:S(2)}) copy-start(f32[16,7,7,512]{3,0,2,1:T(8,128)} %param.7) | copy-start | bytes 4816900
  73.4 2.0 %copy-start.9 = (f32[16,7,7,512]{3,0,2,1:T(8,128)S(1)}, f32[16,7,7,512]{3,0,2,1:T(8,128)}, u32[]{:S(2)}) copy-start(f32[16,7,7,512]{3,0,2,1:T(8,128)} %param.8) | copy-start | bytes 4816900

commit v4 on v3

v4 whole, which is shorter than its diff:
```python
import functools

import jax
import jax.numpy as jnp
from jax import lax
from jax.experimental import pallas as pl
from jax.experimental.pallas import tpu as pltpu
from jax.sharding import PartitionSpec as P


first_fix = 0.9999734386011124
second_fix = 0.09520785288629038


def shifted(x, axis, step):
    count = lax.axis_size(axis)
    return lax.ppermute(x, axis, [(i, (i + step) % count) for i in range(count)])


def moved_on(x, axis, step):
    count = lax.axis_size(axis)
    return lax.ppermute(x, axis, [(i, i + step) for i in range(count) if 0 <= i + step < count])


def call(body, outs, args, flops=0, scratch=()):
    moved = sum(a.size * a.dtype.itemsize for a in args) + sum(o.size * o.dtype.itemsize for o in outs)
    return pl.pallas_call(
        body,
        out_shape=outs,
        in_specs=[pl.BlockSpec(memory_space=pltpu.VMEM)] * len(args),
        out_specs=[pl.BlockSpec(memory_space=pltpu.VMEM)] * len(outs),
        scratch_shapes=list(scratch),
        cost_estimate=pl.CostEstimate(flops=flops, bytes_accessed=moved, transcendentals=0),
        compiler_params=pltpu.CompilerParams(vmem_limit_bytes=24 << 20),
    )(*args)


def roll(x, amount):
    amount %= x.shape[1]
    return pltpu.roll(x, amount, 1) if amount else x


def struct(shape, dtype):
    return jax.ShapeDtypeStruct(shape, dtype)


def column_of(ext, cols):
    return lax.broadcasted_iota(jnp.int32, (1, ext), 1) % cols


def tile_parts(filters, tile, y_ref, taps, bands, ext, cols):
    reach = taps // 2
    y_ref[...] = lax.dot_general(filters, tile, (((1,), (1,)), ((), ())), preferred_element_type=jnp.float32)
    pixels = tile.shape[0]
    column = column_of(ext, cols)
    main = jnp.zeros((bands, ext), jnp.float32)
    to_right = jnp.zeros((bands, ext), jnp.float32)
    to_left = jnp.zeros((bands, ext), jnp.float32)
    tail = jnp.zeros((bands, ext - pixels), jnp.float32)
    for b in range(taps):
        total = None
        for a in range(taps):
            term = jnp.concatenate([y_ref[pl.ds((a * taps + b) * bands, bands), :], tail], axis=1)
            total = term if total is None else roll(total, cols) + term
        step = reach - b
        turned = roll(total, step)
        if step > 0:
            inside = column >= step
            to_right = to_right + jnp.where(inside, 0.0, turned)
        elif step < 0:
            inside = column < cols + step
            to_left = to_left + jnp.where(inside, 0.0, turned)
        main = main + (turned if step == 0 else jnp.where(inside, turned, 0.0))
    return main, roll(to_right, -cols) + roll(to_left, cols)


def early_body(taps, bands, ext, cols, filters_ref, tile_ref, main_ref, spill_ref, y_ref):
    main, spill = tile_parts(filters_ref[...], tile_ref[...], y_ref, taps, bands, ext, cols)
    main_ref[...] = main
    spill_ref[...] = spill


def tile_flags(s):
    count = lax.axis_size("col")
    place = lax.rem(lax.axis_index("col") + count - s, count)
    return place > 0, place < count - 1


def edges_of(value, pixels, reach, cols, places):
    lane = lax.broadcasted_iota(jnp.int32, (1, 128), 1)
    up = jnp.where(lane < 2 * reach * cols, value[:, :128], 0.0)
    down = value[:, pixels : pixels + 128]
    return [jnp.where(lax.axis_index("row") == 0, down, up)] if places == 1 else [up, down]


def sum_body(taps, bands, ext, cols, pixels, share, order, *refs):
    known, count = len(order), 4
    main_of = dict(zip(order, refs[:known]))
    spill_of = dict(zip(order, refs[known : 2 * known]))
    images = refs[2 * known : 2 * known + count]
    out_ref, *edge_refs = refs[2 * known + count :]
    reach = taps // 2
    column = column_of(ext, cols)
    for s in range(count):
        left, right = tile_flags(s)
        picture = images[s][...].astype(jnp.float32) * -share
        pad = jnp.zeros((bands, ext - pixels), jnp.float32)
        value = roll(jnp.concatenate([picture, pad], axis=1), reach * cols)
        if s in order:
            value = value + main_of[s][...]
        if (s + 1) % count in order:
            value = value + jnp.where((column < reach) & left, spill_of[(s + 1) % count][...], 0.0)
        if (s - 1) % count in order:
            value = value + jnp.where((column >= cols - reach) & right, spill_of[(s - 1) % count][...], 0.0)
        out_ref[s] = value
        for ref, edge in zip(edge_refs, edges_of(value, pixels, reach, cols, len(edge_refs))):
            ref[s] = edge


def late_body(taps, bands, ext, cols, pixels, filters_ref, tile_ref, out_ref, *refs):
    *edge_refs, y_ref = refs
    values = tile_parts(filters_ref[...], tile_ref[...], y_ref, taps, bands, ext, cols)
    for at, value in enumerate(values):
        out_ref[at] = value
        for ref, edge in zip(edge_refs, edges_of(value, pixels, taps // 2, cols, len(edge_refs))):
            ref[at] = edge


def join_body(pixels, turn, edges, *refs):
    part_ref, edge_refs, out_ref, send_refs = refs[0], refs[1 : 1 + edges], refs[1 + edges], refs[2 + edges :]
    count, bands = part_ref.shape[:2]

    def turned(x, step):
        step %= bands
        return x if step == 0 else jnp.concatenate([x[bands - step :], x[: bands - step]], axis=0)

    for s in range(count):
        pieces = [turned(ref[s], turn * sign) for ref, sign in zip(edge_refs, (-1, 1))]
        if len(pieces) == 1:
            first = lax.axis_index("row") == 0
            pieces = [jnp.where(first, pieces[0], 0.0), jnp.where(first, 0.0, pieces[0])]
        below, above = pieces
        own = part_ref[s]
        parts = [own[:, :128] + above, own[:, 128:pixels], own[:, pixels : pixels + 128] + below, own[:, pixels + 128 :]]
        value = jnp.concatenate([part for part in parts if part.shape[1]], axis=1)
        out_ref[s] = value
        for send_ref in send_refs:
            send_ref[s] = value.astype(jnp.bfloat16)


def real_lines(ext, rows, cols, reach):
    line = lax.broadcasted_iota(jnp.int32, (1, ext), 1) // cols
    place, places = lax.axis_index("row"), lax.axis_size("row")
    return ((line >= reach) | (place > 0)) & ((line < rows + reach) | (place < places - 1)) & (line < rows + 2 * reach)


def added(s, refs):
    value = refs[0][s]
    for ref in refs[1:]:
        value = value + ref[s].astype(jnp.float32)
    return value


def rounded(real, value):
    return jnp.where(real, value, 0.0).astype(jnp.bfloat16).astype(jnp.float32)


def windows_of(taps, bands, ext, rows, cols, s, resid_ref, windows_ref):
    reach = taps // 2
    pixels = rows * cols
    count = resid_ref.shape[0]
    column = column_of(ext, cols)
    left, right = tile_flags(s)
    own = resid_ref[s]
    to_left = jnp.where(left, resid_ref[lax.rem(s + 1, count)], 0.0)
    to_right = jnp.where(right, resid_ref[lax.rem(s + count - 1, count)], 0.0)
    for b in range(taps):
        step = b - reach
        if step == 0:
            view = own
        elif step > 0:
            view = jnp.where(column >= step, roll(own, step), roll(to_left, step - cols))
        else:
            view = jnp.where(column < cols + step, roll(own, step), roll(to_right, step + cols))
        for a in range(taps):
            part = roll(view, -cols * (2 * reach - a))[:, :pixels]
            at = (a * taps + b) * bands
            windows_ref[at : at + bands, :] = part.astype(jnp.bfloat16)


def back_of(taps, bands, ext, rows, cols, s, turned_ref, resid_ref, windows_ref, back_ref):
    windows_of(taps, bands, ext, rows, cols, s, resid_ref, windows_ref)
    back = jnp.dot(turned_ref[...], windows_ref[...], preferred_element_type=jnp.float32)
    back_ref[...] = back.astype(back_ref.dtype)


def first_back_body(taps, bands, ext, rows, cols, s, turned_ref, *refs):
    *terms, windows_ref, back_ref, sum_ref, resid_ref = refs
    real = real_lines(ext, rows, cols, taps // 2)
    for tile in range(sum_ref.shape[0]):
        value = added(tile, terms)
        sum_ref[tile] = value
        resid_ref[tile] = rounded(real, value)
    back_of(taps, bands, ext, rows, cols, s, turned_ref, resid_ref, windows_ref, back_ref)


def second_back_body(taps, bands, ext, rows, cols, s, late, turned_ref, sum_ref, *refs):
    *terms, windows_ref, back_ref, resid_ref = refs
    count, reach = sum_ref.shape[0], taps // 2
    real = real_lines(ext, rows, cols, reach)
    column = column_of(ext, cols)
    main, spill = added(0, terms), added(1, terms)
    for tile in range(count):
        value = sum_ref[tile]
        left, right = tile_flags(tile)
        if tile == late:
            value = value + main
        if (tile + 1) % count == late:
            value = value + jnp.where((column < reach) & left, spill, 0.0)
        if (tile - 1) % count == late:
            value = value + jnp.where((column >= cols - reach) & right, spill, 0.0)
        resid_ref[tile] = rounded(real, value)
    back_of(taps, bands, ext, rows, cols, s, turned_ref, resid_ref, windows_ref, back_ref)


def turn_body(filters_ref, out_ref):
    out_ref[...] = filters_ref[...].T


def grad_body(count, *refs):
    windows, tiles, grad_ref = refs[:count], refs[count : 2 * count], refs[2 * count]
    total = None
    for s in range(count):
        term = jnp.dot(windows[s][...], tiles[s][...], preferred_element_type=jnp.float32)
        total = term if total is None else total + term
    grad_ref[...] = total


def codes_body(*refs):
    codes_ref, back_ref = refs[:2]
    others, out_ref = refs[2:-1], refs[-1]
    back = back_ref[...]
    for other in others:
        back = back + other[...].astype(jnp.float32)
    moved = codes_ref[...].astype(jnp.float32) - 0.05 * back.T
    out_ref[...] = (moved - jnp.clip(moved, -0.02, 0.02)).astype(jnp.bfloat16)


def adam_update(master, moment, second, grad):
    new_moment = 0.9 * moment + 0.1 * grad
    new_second = 0.999 * second + 0.001 * grad * grad
    new_dictionary = master - 0.05 * (new_moment / first_fix) / (
        jnp.sqrt(new_second / second_fix) + 1e-08
    )
    return (new_dictionary, new_moment, new_second)


def iteration(codes, image, master, moment, second):
    rows, cols, atoms = codes.shape
    own_bands, taps = master.shape[0], master.shape[1]
    groups, count, peers = lax.axis_size("row"), lax.axis_size("col"), lax.axis_size("atom")
    bands = groups * own_bands
    reach = taps // 2
    pixels = rows * cols
    ext = -(-(rows + 2 * reach) * cols // 128) * 128
    row_at, col_at = lax.axis_index("row"), lax.axis_index("col")

    assert count == 4
    tiles = {0: codes.reshape(pixels, atoms)}
    for s in (2, 3, 1):
        tiles[s] = shifted(codes, "col", s).reshape(pixels, atoms)

    own_filters = jnp.transpose(master, (1, 2, 0, 3)).reshape(taps * taps, own_bands, atoms).astype(jnp.bfloat16)
    filters = [own_filters]
    for s in range(1, groups):
        filters.append(shifted(own_filters, "row", s))
    filters = jnp.concatenate(filters, axis=1).reshape(taps * taps * bands, atoms)
    (turned,) = call(turn_body, [struct(filters.shape[::-1], filters.dtype)], [filters])

    picture = image.reshape(pixels, groups, count, own_bands).transpose(1, 2, 3, 0)
    picture = jnp.stack([lax.dynamic_index_in_dim(picture, (row_at + groups - s) % groups, 0, False) for s in range(groups)])
    pieces = [lax.dynamic_index_in_dim(picture, (col_at + s) % count, 1, False).reshape(bands, pixels) for s in range(count)]
    images = []
    for s in range(count):
        images.append(pieces[s] if s == 0 else shifted(pieces[s], "col", s))

    size = struct((bands, ext), jnp.float32)
    y_scratch = [pltpu.VMEM((taps * taps * bands, pixels), jnp.float32)]
    tile_flops = 2 * taps * taps * bands * pixels * atoms
    edges_out = 1 if groups == 2 else 2

    def whole_rows(part, edges):
        if groups == 2:
            edges = [shifted(edges[0], "row", 1)]
        else:
            edges = [moved_on(edges[0], "row", -1), moved_on(edges[1], "row", 1)]
        return call(
            functools.partial(join_body, pixels, own_bands, edges_out),
            [struct(part.shape, jnp.float32)] + [struct(part.shape, jnp.bfloat16)] * copies,
            [part, *edges],
        )

    copies = peers - 1 if peers <= 4 else 1

    def all_atoms(part, *sends):
        if peers > 4:
            (send,) = sends
            return [part, (lax.psum(send, "atom").astype(jnp.float32) - send.astype(jnp.float32)).astype(jnp.bfloat16)]
        terms = [part]
        for m in range(peers - 1, 0, -1):
            terms.append(lax.ppermute(sends[m - 1], "atom", [(i, i ^ m) for i in range(peers)]))
        return terms

    early = (0, 2, 3)
    mains, spills = [], []
    for s in early:
        body = functools.partial(early_body, taps, bands, ext, cols)
        main, spill = call(body, [size, size], [filters, tiles[s]], tile_flops, y_scratch)
        mains.append(main)
        spills.append(spill)
    part, *edges = call(
        functools.partial(sum_body, taps, bands, ext, cols, pixels, 1.0 / peers, early),
        [struct((count, bands, ext), jnp.float32)] + [struct((count, bands, 128), jnp.float32)] * edges_out,
        [*mains, *spills, *images],
    )
    terms = all_atoms(*whole_rows(part, edges))

    part, *edges = call(
        functools.partial(late_body, taps, bands, ext, cols, pixels),
        [struct((2, bands, ext), jnp.float32)] + [struct((2, bands, 128), jnp.float32)] * edges_out,
        [filters, tiles[1]],
        tile_flops,
        y_scratch,
    )
    late_terms = all_atoms(*whole_rows(part, edges))

    shape = (taps, bands, ext, rows, cols)
    resid = struct((count, bands, ext), jnp.float32)
    windows, backs, received = {}, {}, []
    for s in (3, 2, 1, 0):
        outs = [struct((taps * taps * bands, pixels), jnp.bfloat16), struct((atoms, pixels), jnp.bfloat16 if s else jnp.float32)]
        if s == 3:
            body = functools.partial(first_back_body, *shape, s)
            windows[s], backs[s], total, _ = call(body, outs + [resid] * 2, [turned, *terms], tile_flops)
        elif s == 2:
            body = functools.partial(second_back_body, *shape, s, 1)
            args = [turned, total, *late_terms]
            windows[s], backs[s], resid = call(body, outs + [resid], args, tile_flops)
        else:
            body = functools.partial(back_of, *shape, s)
            windows[s], backs[s] = call(body, outs, [turned, resid], tile_flops)
        if s:
            received.append(shifted(backs[s], "col", -s))
    (grad,) = call(
        functools.partial(grad_body, count),
        [struct((taps * taps * bands, atoms), jnp.float32)],
        [windows[s] for s in range(count)] + [tiles[s] for s in range(count)],
        tile_flops * count,
    )
    grad = grad.reshape(taps * taps, groups, own_bands, atoms)
    own_grad = grad[:, 0]
    for s in range(1, groups):
        piece = grad[:, s].astype(jnp.bfloat16)
        piece = shifted(piece, "row", -s)
        own_grad = own_grad + piece.astype(jnp.float32)
    own_grad = jnp.transpose(own_grad.reshape(taps, taps, own_bands, atoms), (2, 0, 1, 3))
    new_dictionary, new_moment, new_second = adam_update(master, moment, second, own_grad)
    (new_codes,) = call(codes_body, [struct((pixels, atoms), jnp.bfloat16)], [tiles[0], backs[0], *received])
    return (new_codes.reshape(rows, cols, atoms), new_dictionary, new_moment, new_second)


def solution(mesh):
    return jax.shard_map(
        iteration,
        mesh=mesh,
        in_specs=(
            P("row", "col", "atom"),
            P("row", "col", None),
            P(("row", "col"), None, None, "atom"),
            P(("row", "col"), None, None, "atom"),
            P(("row", "col"), None, None, "atom"),
        ),
        out_specs=(
            P("row", "col", "atom"),
            P(("row", "col"), None, None, "atom"),
            P(("row", "col"), None, None, "atom"),
            P(("row", "col"), None, None, "atom"),
        ),
        check_vma=False,
    )
```

time: 78.7 us -> 82.1 us (1.043)
  the two profiles are of different devices: /device:TPU:0 before, /device:TPU:9 now
where the time goes in v4:
time: 82.1 us; the launch traced here: 81.9 us
  waiting for transfers between devices  40.9 us (50%)
  starting transfers between devices  20.6 us (25%)
  Pallas kernels  10.8 us (13%)
  other arithmetic  6.11 us (7%)
  local copies, waits for them, and re-layouts  2.72 us (3%)
  between operations  0.88 us (1%)
    ppermute x13, waiting for transfers between devices, shifted(): lax.ppermute(x, axis, [(i, (i + step) % count) for i in range(count)])  39.5 us
    ppermute x13, starting transfers between devices, shifted(): lax.ppermute(x, axis, [(i, (i + step) % count) for i in range(count)])  15.1 us
    pallas_call x14, Pallas kernels, call(): pl.pallas_call(body, out_shape=outs, in_specs=[pl.BlockSpec(memory_space=...  10.8 us
    ppermute x6, starting transfers between devices, all_atoms(): lax.ppermute(sends[m - 1], 'atom', [(i, i ^ m) for i in range(peers)])  5.45 us
    sub x1, other arithmetic, adam_update(): master - 0.05 * (new_moment / first_fix) / (jnp.sqrt(new_second / second_...  2.97 us
    unnamed x12, local copies, waits for them, and re-layouts  2.05 us
  transfers between devices with their start and end apart: 19, of which 10 were waited for; matrix products, arithmetic and copies ran while one was open for 3% of the time, Pallas kernels for 8%

profile of v4, /device:TPU:9, one launch (start us, length us, event | category | flops | bytes accessed | tf_op | source)
XLA Modules:
  0.0 81.9 jit_solution(8182499974862321023)
XLA Ops:
  0.7 1.6 %convert_element_type.16 = bf16[16,7,7,512]{3,0,2,1:T(8,128)(2,1)S(1)} convert(f32[16,7,7,512]{3,0,2,1:T(8,128)} %param.7) | non-fusion elementwise | flops 401408 | bytes 2408448 | tf_op jit(solution)/shard_map/convert_element_type | solution.py:273
  3.0 2.3 %collective-permute-start.1 = (bf16[16,16,512]{2,1,0:T(8,128)(2,1)S(1)}, bf16[16,16,512]{2,1,0:T(8,128)(2,1)S(1)}, u32[]{:S(2)}, u32[]{:S(2)}) collective-permute-start(bf16[16,16,512]{2,1,0:T(8,128)(2,1)S(1)} %copy-done), channel_id=1, source_target_pairs={{0,2},{1,3},{2,0},{3,1},{4,6},{5,7},{6,4},{7,5},{8,10},{9,11},{10,... | collective-permute-start | bytes 786440 | tf_op jit(solution)/shard_map/ppermute | solution.py:17
  5.5 1.3 %collective-permute-start.10 = (bf16[16,16,512]{2,1,0:T(8,128)(2,1)S(1)}, bf16[16,16,512]{2,1,0:T(8,128)(2,1)S(1)}, u32[]{:S(2)}, u32[]{:S(2)}) collective-permute-start(bf16[16,16,512]{2,1,0:T(8,128)(2,1)S(1)} %copy-done), channel_id=1, source_target_pairs={{0,1},{1,2},{2,3},{3,0},{4,5},{5,6},{6,7},{7,4},{8,9},{9,10},{10,1... | collective-permute-start | bytes 786440 | tf_op jit(solution)/shard_map/ppermute | solution.py:17
  7.7 2.2 %collective-permute-start.4 = (bf16[32,256]{1,0:T(8,128)(2,1)S(1)}, bf16[32,256]{1,0:T(8,128)(2,1)S(1)}, u32[]{:S(2)}, u32[]{:S(2)}) collective-permute-start(bf16[32,256]{1,0:T(8,128)(2,1)S(1)} %bitcast.51), channel_id=1, source_target_pairs={{0,2},{1,3},{2,0},{3,1},{4,6},{5,7},{6,4},{7,5},{8,10},{9,11},{10,... | collective-permute-start | bytes 49160 | tf_op jit(solution)/shard_map/ppermute | solution.py:17
  10.0 1.3 %pad_maximum_fusion = bf16[49,32,512]{2,1,0:T(8,128)(2,1)S(1)} fusion(bf16[49,16,512]{2,1,0:T(8,128)(2,1)} %collective-permute-done, bf16[49,16,512]{2,1,0:T(8,128)(2,1)S(1)} %bitcast.46), kind=kLoop, calls=%fused_computation.5 | loop fusion | flops 3211264 | bytes 3211264 | tf_op jit(solution)/shard_map/concatenate | solution.py:277
  11.3 0.9 %shard_map.85 = (f32[32,384]{1,0:T(8,128)S(1)}, f32[32,384]{1,0:T(8,128)S(1)}) custom-call(bf16[1568,512]{1,0:T(8,128)(2,1)S(1)} %bitcast.27, bf16[256,512]{1,0:T(8,128)(2,1)S(1)} %bitcast.34), custom_call_target="tpu_custom_call" | custom-call | flops 411041792 | bytes 1966080 | tf_op jit(solution)/shard_map/pallas_call | solution.py:27
  12.2 10.3 %collective-permute-done.1 = bf16[16,16,512]{2,1,0:T(8,128)(2,1)S(1)} collective-permute-done((bf16[16,16,512]{2,1,0:T(8,128)(2,1)S(1)}, bf16[16,16,512]{2,1,0:T(8,128)(2,1)S(1)}, u32[]{:S(2)}, u32[]{:S(2)}) %collective-permute-start.1) | collective-permute-done | bytes 262176 | tf_op jit(solution)/shard_map/ppermute | solution.py:17
  22.5 0.9 %shard_map.86 = (f32[32,384]{1,0:T(8,128)S(1)}, f32[32,384]{1,0:T(8,128)S(1)}) custom-call(bf16[1568,512]{1,0:T(8,128)(2,1)S(1)} %bitcast.28, bf16[256,512]{1,0:T(8,128)(2,1)S(1)} %bitcast.37), custom_call_target="tpu_custom_call" | custom-call | flops 411041792 | bytes 1966080 | tf_op jit(solution)/shard_map/pallas_call | solution.py:27
  23.5 5.0 %collective-permute-done.2 = bf16[16,16,512]{2,1,0:T(8,128)(2,1)S(1)} collective-permute-done((bf16[16,16,512]{2,1,0:T(8,128)(2,1)S(1)}, bf16[16,16,512]{2,1,0:T(8,128)(2,1)S(1)}, u32[]{:S(2)}, u32[]{:S(2)}) %collective-permute-start.2) | collective-permute-done | bytes 262176 | tf_op jit(solution)/shard_map/ppermute | solution.py:17
  28.5 0.9 %shard_map.87 = (f32[32,384]{1,0:T(8,128)S(1)}, f32[32,384]{1,0:T(8,128)S(1)}) custom-call(bf16[1568,512]{1,0:T(8,128)(2,1)S(1)} %bitcast.29, bf16[256,512]{1,0:T(8,128)(2,1)S(1)} %bitcast.39), custom_call_target="tpu_custom_call" | custom-call | flops 411041792 | bytes 1966080 | tf_op jit(solution)/shard_map/pallas_call | solution.py:27
  29.7 0.9 %collective-permute-start.6 = (f32[4,32,128]{2,1,0:T(8,128)S(1)}, f32[4,32,128]{2,1,0:T(8,128)S(1)}, u32[]{:S(2)}, u32[]{:S(2)}) collective-permute-start(f32[4,32,128]{2,1,0:T(8,128)S(1)} %get-tuple-element.39), channel_id=1, source_target_pairs={{0,4},{4,0},{1,5},{5,1},{2,6},{6,2},{3,7},{7,3},{8,12},{12,8},{9,1... | collective-permute-start | bytes 196616 | tf_op jit(solution)/shard_map/ppermute | solution.py:17
  30.6 0.9 %collective-permute-done.6.refs_1_ = f32[4,32,128]{2,1,0:T(8,128)S(1)} collective-permute-done((f32[4,32,128]{2,1,0:T(8,128)S(1)}, f32[4,32,128]{2,1,0:T(8,128)S(1)}, u32[]{:S(2)}, u32[]{:S(2)}) %collective-permute-start.6) | collective-permute-done | bytes 65568 | tf_op jit(solution)/shard_map/ppermute | solution.py:17
  31.5 2.4 %collective-permute-start.7 = (bf16[4,32,384]{2,1,0:T(8,128)(2,1)S(1)}, bf16[4,32,384]{2,1,0:T(8,128)(2,1)S(1)}, u32[]{:S(2)}, u32[]{:S(2)}) collective-permute-start(bf16[4,32,384]{2,1,0:T(8,128)(2,1)S(1)} %get-tuple-element.41), channel_id=1, source_target_pairs={{0,24},{8,16},{16,8},{24,0},{1,25},{9,17},{17,9},{25,1},{2,26},{10... | collective-permute-start | bytes 294920 | tf_op jit(solution)/shard_map/ppermute | solution.py:311
  34.2 0.9 %shard_map.91 = (f32[2,32,384]{2,1,0:T(8,128)S(1)}, f32[2,32,128]{2,1,0:T(8,128)S(1)}) custom-call(bf16[1568,512]{1,0:T(8,128)(2,1)S(1)} %bitcast.30, bf16[256,512]{1,0:T(8,128)(2,1)S(1)} %bitcast.41), custom_call_target="tpu_custom_call" | custom-call | flops 411041792 | bytes 1998848 | tf_op jit(solution)/shard_map/pallas_call | solution.py:27
  35.2 1.2 %collective-permute-start.11 = (f32[2,32,128]{2,1,0:T(8,128)S(1)}, f32[2,32,128]{2,1,0:T(8,128)S(1)}, u32[]{:S(2)}, u32[]{:S(2)}) collective-permute-start(f32[2,32,128]{2,1,0:T(8,128)S(1)} %get-tuple-element.46), channel_id=1, source_target_pairs={{0,4},{4,0},{1,5},{5,1},{2,6},{6,2},{3,7},{7,3},{8,12},{12,8},{9,1... | collective-permute-start | bytes 98312 | tf_op jit(solution)/shard_map/ppermute | solution.py:17
  37.3 2.4 %collective-permute-start.12 = (bf16[2,32,384]{2,1,0:T(8,128)(2,1)S(1)}, bf16[2,32,384]{2,1,0:T(8,128)(2,1)S(1)}, u32[]{:S(2)}, u32[]{:S(2)}) collective-permute-start(bf16[2,32,384]{2,1,0:T(8,128)(2,1)S(1)} %get-tuple-element.48), channel_id=1, source_target_pairs={{0,24},{8,16},{16,8},{24,0},{1,25},{9,17},{17,9},{25,1},{2,26},{10... | collective-permute-start | bytes 147464 | tf_op jit(solution)/shard_map/ppermute | solution.py:311
  40.6 0.9 %shard_map.90 = (bf16[1568,256]{1,0:T(8,128)(2,1)S(1)}, bf16[512,256]{1,0:T(8,128)(2,1)S(1)}, f32[4,32,384]{2,1,0:T(8,128)S(1)}, f32[4,32,384]{2,1,0:T(8,128)}) custom-call(bf16[512,1568]{1,0:T(8,128)(2,1)S(1)} %shard_map.84.turned_ref, f32[4,32,384]{2,1,0:T(8,128)S(1)} %get-tuple-element.40.refs_0_, bf16[4,32,384]{2,1,0:T(8,128)(2,1)S(1)} %collective-permute-done.7.refs_1_, ...), custom_call_target="tpu_custom_call" | custom-call | flops 411041792 | bytes 3555328 | tf_op jit(solution)/shard_map/pallas_call | solution.py:27
  41.5 1.1 %collective-permute-done.13.refs_2_ = bf16[2,32,384]{2,1,0:T(8,128)(2,1)S(1)} collective-permute-done((bf16[2,32,384]{2,1,0:T(8,128)(2,1)S(1)}, bf16[2,32,384]{2,1,0:T(8,128)(2,1)S(1)}, u32[]{:S(2)}, u32[]{:S(2)}) %collective-permute-start.13) | collective-permute-done | bytes 49184 | tf_op jit(solution)/shard_map/ppermute | solution.py:311
  42.9 0.9 %shard_map.93 = (bf16[1568,256]{1,0:T(8,128)(2,1)S(1)}, bf16[512,256]{1,0:T(8,128)(2,1)S(1)}, f32[4,32,384]{2,1,0:T(8,128)S(1)}) custom-call(bf16[512,1568]{1,0:T(8,128)(2,1)S(1)} %shard_map.84.turned_ref, f32[4,32,384]{2,1,0:T(8,128)S(1)} %get-tuple-element.44.sum_ref, f32[2,32,384]{2,1,0:T(8,128)S(1)} %get-tuple-element.47.refs_0_, ...), custom_call_target="tpu_custom_call" | custom-call | flops 411041792 | bytes 3309568 | tf_op jit(solution)/shard_map/pallas_call | solution.py:27
  43.8 0.9 %shard_map.94 = (bf16[1568,256]{1,0:T(8,128)(2,1)S(1)}, f32[512,256]{1,0:T(8,128)S(1)}) custom-call(bf16[512,1568]{1,0:T(8,128)(2,1)S(1)} %shard_map.84.turned_ref, f32[4,32,384]{2,1,0:T(8,128)S(1)} %get-tuple-element.51.resid_ref), custom_call_target="tpu_custom_call" | custom-call | flops 411041792 | bytes 3129344 | tf_op jit(solution)/shard_map/pallas_call | solution.py:27
  44.7 0.9 %shard_map.95 = (bf16[1568,256]{1,0:T(8,128)(2,1)S(1)}, bf16[512,256]{1,0:T(8,128)(2,1)S(1)}) custom-call(bf16[512,1568]{1,0:T(8,128)(2,1)S(1)} %shard_map.84.turned_ref, f32[4,32,384]{2,1,0:T(8,128)S(1)} %get-tuple-element.51.resid_ref), custom_call_target="tpu_custom_call" | custom-call | flops 411041792 | bytes 2867200 | tf_op jit(solution)/shard_map/pallas_call | solution.py:27
  45.6 1.8 %shard_map.97 = f32[1568,512]{1,0:T(8,128)S(1)} custom-call(bf16[1568,256]{1,0:T(8,128)(2,1)S(1)} %get-tuple-element.56.refs_0_, bf16[1568,256]{1,0:T(8,128)(2,1)S(1)} %get-tuple-element.57.refs_1_, bf16[1568,256]{1,0:T(8,128)(2,1)S(1)} %get-tuple-element.58.refs_2_, bf16[1568,256]{1,0:T(8,128)(2,1)S(1)} %get-tuple-element.59.refs_3_, ...), custom_call_target="tpu_custom_call" | custom-call | flops 1644167168 | bytes 7471104 | tf_op jit(solution)/shard_map/pallas_call | solution.py:27
  47.5 2.1 %collective-permute-start.18 = (bf16[49,16,512]{2,1,0:T(8,128)(2,1)S(1)}, bf16[49,16,512]{2,1,0:T(8,128)(2,1)S(1)}, u32[]{:S(2)}, u32[]{:S(2)}) collective-permute-start(bf16[49,16,512]{2,1,0:T(8,128)(2,1)S(1)} %fusion.2), channel_id=1, source_target_pairs={{0,4},{4,0},{1,5},{5,1},{2,6},{6,2},{3,7},{7,3},{8,12},{12,8},{9,1... | collective-permute-start | bytes 2408456 | tf_op jit(solution)/shard_map/ppermute | solution.py:17
  49.6 1.4 %collective-permute-start.15 = (bf16[512,256]{1,0:T(8,128)(2,1)S(1)}, bf16[512,256]{1,0:T(8,128)(2,1)S(1)}, u32[]{:S(2)}, u32[]{:S(2)}) collective-permute-start(bf16[512,256]{1,0:T(8,128)(2,1)S(1)} %get-tuple-element.53), channel_id=1, source_target_pairs={{0,1},{1,2},{2,3},{3,0},{4,5},{5,6},{6,7},{7,4},{8,9},{9,10},{10,1... | collective-permute-start | bytes 786440 | tf_op jit(solution)/shard_map/ppermute | solution.py:17
  51.0 1.2 %collective-permute-start.16 = (bf16[512,256]{1,0:T(8,128)(2,1)S(1)}, bf16[512,256]{1,0:T(8,128)(2,1)S(1)}, u32[]{:S(2)}, u32[]{:S(2)}) collective-permute-start(bf16[512,256]{1,0:T(8,128)(2,1)S(1)} %get-tuple-element.54), channel_id=1, source_target_pairs={{0,2},{1,3},{2,0},{3,1},{4,6},{5,7},{6,4},{7,5},{8,10},{9,11},{10,... | collective-permute-start | bytes 786440 | tf_op jit(solution)/shard_map/ppermute | solution.py:17
  52.3 1.5 %collective-permute-start.17 = (bf16[512,256]{1,0:T(8,128)(2,1)S(1)}, bf16[512,256]{1,0:T(8,128)(2,1)S(1)}, u32[]{:S(2)}, u32[]{:S(2)}) collective-permute-start(bf16[512,256]{1,0:T(8,128)(2,1)S(1)} %get-tuple-element.55), channel_id=1, source_target_pairs={{0,3},{1,0},{2,1},{3,2},{4,7},{5,4},{6,5},{7,6},{8,11},{9,8},{10,9... | collective-permute-start | bytes 786440 | tf_op jit(solution)/shard_map/ppermute | solution.py:17
  53.7 3.7 %collective-permute-done.15.refs_2_ = bf16[512,256]{1,0:T(8,128)(2,1)S(1)} collective-permute-done((bf16[512,256]{1,0:T(8,128)(2,1)S(1)}, bf16[512,256]{1,0:T(8,128)(2,1)S(1)}, u32[]{:S(2)}, u32[]{:S(2)}) %collective-permute-start.15) | collective-permute-done | bytes 262176 | tf_op jit(solution)/shard_map/ppermute | solution.py:17
  57.5 16.0 %collective-permute-done.16.refs_3_ = bf16[512,256]{1,0:T(8,128)(2,1)S(1)} collective-permute-done((bf16[512,256]{1,0:T(8,128)(2,1)S(1)}, bf16[512,256]{1,0:T(8,128)(2,1)S(1)}, u32[]{:S(2)}, u32[]{:S(2)}) %collective-permute-start.16) | collective-permute-done | bytes 262176 | tf_op jit(solution)/shard_map/ppermute | solution.py:17
  73.5 2.5 %collective-permute-done.17.refs_4_ = bf16[512,256]{1,0:T(8,128)(2,1)S(1)} collective-permute-done((bf16[512,256]{1,0:T(8,128)(2,1)S(1)}, bf16[512,256]{1,0:T(8,128)(2,1)S(1)}, u32[]{:S(2)}, u32[]{:S(2)}) %collective-permute-start.17) | collective-permute-done | bytes 262176 | tf_op jit(solution)/shard_map/ppermute | solution.py:17
  76.0 0.9 %shard_map.96 = bf16[256,512]{1,0:T(8,128)(2,1)} custom-call(bf16[256,512]{1,0:T(8,128)(2,1)S(1)} %bitcast.36, f32[512,256]{1,0:T(8,128)S(1)} %get-tuple-element.52.refs_1_, bf16[512,256]{1,0:T(8,128)(2,1)S(1)} %collective-permute-done.15.refs_2_, bf16[512,256]{1,0:T(8,128)(2,1)S(1)} %collective-permute-done.16.refs_3_, ...), custom_call_target="tpu_custom_call" | custom-call | bytes 1835008 | tf_op jit(solution)/shard_map/pallas_call | solution.py:27
  77.5 1.0 %copy-done.1 = f32[16,7,7,512]{3,0,2,1:T(8,128)S(1)} copy-done((f32[16,7,7,512]{3,0,2,1:T(8,128)S(1)}, f32[16,7,7,512]{3,0,2,1:T(8,128)}, u32[]{:S(2)}) %copy-start.1) | copy-done | bytes 1605656
  78.9 3.0 %divide_subtract_fusion = (f32[16,7,7,512]{3,0,2,1:T(8,128)}, f32[16,7,7,512]{3,0,2,1:T(8,128)}, f32[16,7,7,512]{3,0,2,1:T(8,128)}) fusion(f32[16,7,7,512]{3,0,2,1:T(8,128)S(1)} %copy-done.1, f32[16,7,7,512]{3,0,2,1:T(8,128)S(1)} %bitcast.44, f32[16,7,7,512]{3,0,2,1:T(8,128)S(1)} %copy-done.2, f32[16,7,7,512]{3,0,2,1:T(8,128)S(1)} %copy-done.3), kind=kLoop, calls=%fused_computation.6 | loop fusion | flops 4816896 | bytes 11239424 | tf_op jit(solution)/shard_map/sub | solution.py:252
  (40 shorter events, 5.7 us)
Async XLA Ops:
  0.6 2.4 %copy-start = (bf16[16,16,512]{2,1,0:T(8,128)(2,1)S(1)}, bf16[16,16,512]{2,1,0:T(8,128)(2,1)}, u32[]{:S(2)}) copy-start(bf16[16,16,512]{2,1,0:T(8,128)(2,1)} %param.5) | copy-start | bytes 786436
  0.6 6.1 %copy-start.4 = (bf16[16,16,128]{2,1,0:T(8,128)(2,1)S(1)}, bf16[16,16,128]{2,1,0:T(8,128)(2,1)}, u32[]{:S(2)}) copy-start(bf16[16,16,128]{2,1,0:T(8,128)(2,1)} %param.6) | copy-start | bytes 196612
  2.2 5.5 %collective-permute-start = (bf16[49,16,512]{2,1,0:T(8,128)(2,1)S(1)}, bf16[49,16,512]{2,1,0:T(8,128)(2,1)}, u32[]{:S(2)}, u32[]{:S(2)}) collective-permute-start(bf16[49,16,512]{2,1,0:T(8,128)(2,1)S(1)} %bitcast.45), channel_id=1, source_target_pairs={{0,4},{4,0},{1,5},{5,1},{2,6},{6,2},{3,7},{7,3},{8,12},{12,8},{9,1... | collective-permute-start | bytes 2408456 | tf_op jit(solution)/shard_map/ppermute | solution.py:17
  3.0 19.6 %collective-permute-start.1 = (bf16[16,16,512]{2,1,0:T(8,128)(2,1)S(1)}, bf16[16,16,512]{2,1,0:T(8,128)(2,1)S(1)}, u32[]{:S(2)}, u32[]{:S(2)}) collective-permute-start(bf16[16,16,512]{2,1,0:T(8,128)(2,1)S(1)} %copy-done), channel_id=1, source_target_pairs={{0,2},{1,3},{2,0},{3,1},{4,6},{5,7},{6,4},{7,5},{8,10},{9,11},{10,... | collective-permute-start | bytes 786440 | tf_op jit(solution)/shard_map/ppermute | solution.py:17
  5.3 23.2 %collective-permute-start.2 = (bf16[16,16,512]{2,1,0:T(8,128)(2,1)S(1)}, bf16[16,16,512]{2,1,0:T(8,128)(2,1)S(1)}, u32[]{:S(2)}, u32[]{:S(2)}) collective-permute-start(bf16[16,16,512]{2,1,0:T(8,128)(2,1)S(1)} %copy-done), channel_id=1, source_target_pairs={{0,3},{1,0},{2,1},{3,2},{4,7},{5,4},{6,5},{7,6},{8,11},{9,8},{10,9... | collective-permute-start | bytes 786440 | tf_op jit(solution)/shard_map/ppermute | solution.py:17
  5.5 28.8 %collective-permute-start.10 = (bf16[16,16,512]{2,1,0:T(8,128)(2,1)S(1)}, bf16[16,16,512]{2,1,0:T(8,128)(2,1)S(1)}, u32[]{:S(2)}, u32[]{:S(2)}) collective-permute-start(bf16[16,16,512]{2,1,0:T(8,128)(2,1)S(1)} %copy-done), channel_id=1, source_target_pairs={{0,1},{1,2},{2,3},{3,0},{4,5},{5,6},{6,7},{7,4},{8,9},{9,10},{10,1... | collective-permute-start | bytes 786440 | tf_op jit(solution)/shard_map/ppermute | solution.py:17
  7.7 21.8 %collective-permute-start.3 = (bf16[32,256]{1,0:T(8,128)(2,1)S(1)}, bf16[32,256]{1,0:T(8,128)(2,1)S(1)}, u32[]{:S(2)}, u32[]{:S(2)}) collective-permute-start(bf16[32,256]{1,0:T(8,128)(2,1)S(1)} %bitcast.52), channel_id=1, source_target_pairs={{0,1},{1,2},{2,3},{3,0},{4,5},{5,6},{6,7},{7,4},{8,9},{9,10},{10,1... | collective-permute-start | bytes 49160 | tf_op jit(solution)/shard_map/ppermute | solution.py:17
  7.7 21.8 %collective-permute-start.4 = (bf16[32,256]{1,0:T(8,128)(2,1)S(1)}, bf16[32,256]{1,0:T(8,128)(2,1)S(1)}, u32[]{:S(2)}, u32[]{:S(2)}) collective-permute-start(bf16[32,256]{1,0:T(8,128)(2,1)S(1)} %bitcast.51), channel_id=1, source_target_pairs={{0,2},{1,3},{2,0},{3,1},{4,6},{5,7},{6,4},{7,5},{8,10},{9,11},{10,... | collective-permute-start | bytes 49160 | tf_op jit(solution)/shard_map/ppermute | solution.py:17
  22.5 7.0 %collective-permute-start.5 = (bf16[32,256]{1,0:T(8,128)(2,1)S(1)}, bf16[32,256]{1,0:T(8,128)(2,1)S(1)}, u32[]{:S(2)}, u32[]{:S(2)}) collective-permute-start(bf16[32,256]{1,0:T(8,128)(2,1)S(1)} %bitcast.50), channel_id=1, source_target_pairs={{0,3},{1,0},{2,1},{3,2},{4,7},{5,4},{6,5},{7,6},{8,11},{9,8},{10,9... | collective-permute-start | bytes 49160 | tf_op jit(solution)/shard_map/ppermute | solution.py:17
  29.7 1.8 %collective-permute-start.6 = (f32[4,32,128]{2,1,0:T(8,128)S(1)}, f32[4,32,128]{2,1,0:T(8,128)S(1)}, u32[]{:S(2)}, u32[]{:S(2)}) collective-permute-start(f32[4,32,128]{2,1,0:T(8,128)S(1)} %get-tuple-element.39), channel_id=1, source_target_pairs={{0,4},{4,0},{1,5},{5,1},{2,6},{6,2},{3,7},{7,3},{8,12},{12,8},{9,1... | collective-permute-start | bytes 196616 | tf_op jit(solution)/shard_map/ppermute | solution.py:17
  31.5 8.4 %collective-permute-start.7 = (bf16[4,32,384]{2,1,0:T(8,128)(2,1)S(1)}, bf16[4,32,384]{2,1,0:T(8,128)(2,1)S(1)}, u32[]{:S(2)}, u32[]{:S(2)}) collective-permute-start(bf16[4,32,384]{2,1,0:T(8,128)(2,1)S(1)} %get-tuple-element.41), channel_id=1, source_target_pairs={{0,24},{8,16},{16,8},{24,0},{1,25},{9,17},{17,9},{25,1},{2,26},{10... | collective-permute-start | bytes 294920 | tf_op jit(solution)/shard_map/ppermute | solution.py:311
  33.9 6.7 %collective-permute-start.8 = (bf16[4,32,384]{2,1,0:T(8,128)(2,1)S(1)}, bf16[4,32,384]{2,1,0:T(8,128)(2,1)S(1)}, u32[]{:S(2)}, u32[]{:S(2)}) collective-permute-start(bf16[4,32,384]{2,1,0:T(8,128)(2,1)S(1)} %get-tuple-element.42), channel_id=1, source_target_pairs={{0,16},{8,24},{16,0},{24,8},{1,17},{9,25},{17,1},{25,9},{2,18},{10... | collective-permute-start | bytes 294920 | tf_op jit(solution)/shard_map/ppermute | solution.py:311
  34.1 6.5 %collective-permute-start.9 = (bf16[4,32,384]{2,1,0:T(8,128)(2,1)S(1)}, bf16[4,32,384]{2,1,0:T(8,128)(2,1)S(1)}, u32[]{:S(2)}, u32[]{:S(2)}) collective-permute-start(bf16[4,32,384]{2,1,0:T(8,128)(2,1)S(1)} %get-tuple-element.43), channel_id=1, source_target_pairs={{0,8},{8,0},{16,24},{24,16},{1,9},{9,1},{17,25},{25,17},{2,10},{10... | collective-permute-start | bytes 294920 | tf_op jit(solution)/shard_map/ppermute | solution.py:311
  35.2 2.1 %collective-permute-start.11 = (f32[2,32,128]{2,1,0:T(8,128)S(1)}, f32[2,32,128]{2,1,0:T(8,128)S(1)}, u32[]{:S(2)}, u32[]{:S(2)}) collective-permute-start(f32[2,32,128]{2,1,0:T(8,128)S(1)} %get-tuple-element.46), channel_id=1, source_target_pairs={{0,4},{4,0},{1,5},{5,1},{2,6},{6,2},{3,7},{7,3},{8,12},{12,8},{9,1... | collective-permute-start | bytes 98312 | tf_op jit(solution)/shard_map/ppermute | solution.py:17
  37.3 4.2 %collective-permute-start.12 = (bf16[2,32,384]{2,1,0:T(8,128)(2,1)S(1)}, bf16[2,32,384]{2,1,0:T(8,128)(2,1)S(1)}, u32[]{:S(2)}, u32[]{:S(2)}) collective-permute-start(bf16[2,32,384]{2,1,0:T(8,128)(2,1)S(1)} %get-tuple-element.48), channel_id=1, source_target_pairs={{0,24},{8,16},{16,8},{24,0},{1,25},{9,17},{17,9},{25,1},{2,26},{10... | collective-permute-start | bytes 147464 | tf_op jit(solution)/shard_map/ppermute | solution.py:311
  39.7 2.9 %collective-permute-start.13 = (bf16[2,32,384]{2,1,0:T(8,128)(2,1)S(1)}, bf16[2,32,384]{2,1,0:T(8,128)(2,1)S(1)}, u32[]{:S(2)}, u32[]{:S(2)}) collective-permute-start(bf16[2,32,384]{2,1,0:T(8,128)(2,1)S(1)} %get-tuple-element.49), channel_id=1, source_target_pairs={{0,16},{8,24},{16,0},{24,8},{1,17},{9,25},{17,1},{25,9},{2,18},{10... | collective-permute-start | bytes 147464 | tf_op jit(solution)/shard_map/ppermute | solution.py:311
  39.9 2.9 %collective-permute-start.14 = (bf16[2,32,384]{2,1,0:T(8,128)(2,1)S(1)}, bf16[2,32,384]{2,1,0:T(8,128)(2,1)S(1)}, u32[]{:S(2)}, u32[]{:S(2)}) collective-permute-start(bf16[2,32,384]{2,1,0:T(8,128)(2,1)S(1)} %get-tuple-element.50), channel_id=1, source_target_pairs={{0,8},{8,0},{16,24},{24,16},{1,9},{9,1},{17,25},{25,17},{2,10},{10... | collective-permute-start | bytes 147464 | tf_op jit(solution)/shard_map/ppermute | solution.py:311
  47.5 29.4 %collective-permute-start.18 = (bf16[49,16,512]{2,1,0:T(8,128)(2,1)S(1)}, bf16[49,16,512]{2,1,0:T(8,128)(2,1)S(1)}, u32[]{:S(2)}, u32[]{:S(2)}) collective-permute-start(bf16[49,16,512]{2,1,0:T(8,128)(2,1)S(1)} %fusion.2), channel_id=1, source_target_pairs={{0,4},{4,0},{1,5},{5,1},{2,6},{6,2},{3,7},{7,3},{8,12},{12,8},{9,1... | collective-permute-start | bytes 2408456 | tf_op jit(solution)/shard_map/ppermute | solution.py:17
  49.6 7.8 %collective-permute-start.15 = (bf16[512,256]{1,0:T(8,128)(2,1)S(1)}, bf16[512,256]{1,0:T(8,128)(2,1)S(1)}, u32[]{:S(2)}, u32[]{:S(2)}) collective-permute-start(bf16[512,256]{1,0:T(8,128)(2,1)S(1)} %get-tuple-element.53), channel_id=1, source_target_pairs={{0,1},{1,2},{2,3},{3,0},{4,5},{5,6},{6,7},{7,4},{8,9},{9,10},{10,1... | collective-permute-start | bytes 786440 | tf_op jit(solution)/shard_map/ppermute | solution.py:17
  51.0 22.5 %collective-permute-start.16 = (bf16[512,256]{1,0:T(8,128)(2,1)S(1)}, bf16[512,256]{1,0:T(8,128)(2,1)S(1)}, u32[]{:S(2)}, u32[]{:S(2)}) collective-permute-start(bf16[512,256]{1,0:T(8,128)(2,1)S(1)} %get-tuple-element.54), channel_id=1, source_target_pairs={{0,2},{1,3},{2,0},{3,1},{4,6},{5,7},{6,4},{7,5},{8,10},{9,11},{10,... | collective-permute-start | bytes 786440 | tf_op jit(solution)/shard_map/ppermute | solution.py:17
  52.3 23.7 %collective-permute-start.17 = (bf16[512,256]{1,0:T(8,128)(2,1)S(1)}, bf16[512,256]{1,0:T(8,128)(2,1)S(1)}, u32[]{:S(2)}, u32[]{:S(2)}) collective-permute-start(bf16[512,256]{1,0:T(8,128)(2,1)S(1)} %get-tuple-element.55), channel_id=1, source_target_pairs={{0,3},{1,0},{2,1},{3,2},{4,7},{5,4},{6,5},{7,6},{8,11},{9,8},{10,9... | collective-permute-start | bytes 786440 | tf_op jit(solution)/shard_map/ppermute | solution.py:17
  76.0 1.5 %copy-start.3 = (f32[16,7,7,512]{3,0,2,1:T(8,128)S(1)}, f32[16,7,7,512]{3,0,2,1:T(8,128)}, u32[]{:S(2)}) copy-start(f32[16,7,7,512]{3,0,2,1:T(8,128)} %param.9) | copy-start | bytes 4816900
  76.9 1.5 %copy-start.1 = (f32[16,7,7,512]{3,0,2,1:T(8,128)S(1)}, f32[16,7,7,512]{3,0,2,1:T(8,128)}, u32[]{:S(2)}) copy-start(f32[16,7,7,512]{3,0,2,1:T(8,128)} %param.7) | copy-start | bytes 4816900
  76.9 2.0 %copy-start.2 = (f32[16,7,7,512]{3,0,2,1:T(8,128)S(1)}, f32[16,7,7,512]{3,0,2,1:T(8,128)}, u32[]{:S(2)}) copy-start(f32[16,7,7,512]{3,0,2,1:T(8,128)} %param.8) | copy-start | bytes 4816900

commit v5 on v3

--- a/solution.py
+++ b/solution.py
@@ -194,17 +194,22 @@
     s = {"own": 0, "two": 2, "near": near, "far": 4 - near}[which]
     turned_ref = refs[0]
     if peers is None:
-        resid_ref, (windows_ref, back_ref) = refs[1], refs[2:]
+        resid_ref, (windows_ref, *back_refs) = refs[1], refs[2:]
     else:
-        windows_ref, back_ref, resid_ref = refs[-3:]
+        windows_ref, *back_refs, resid_ref = refs[-3:]
         resid_body(ext, rows, cols, taps // 2, peers, *refs[1:-3], resid_ref)
     windows_of(taps, bands, ext, rows, cols, s, resid_ref, windows_ref)
     back = jnp.dot(turned_ref[...], windows_ref[...], preferred_element_type=jnp.float32)
-    back_ref[...] = back.astype(back_ref.dtype)
+    for back_ref in back_refs:
+        back_ref[...] = back.astype(back_ref.dtype)
 
 
 def merge_body(back_ref, passed_ref, out_ref):
     out_ref[...] = (back_ref[...] + passed_ref[...].astype(jnp.float32)).astype(jnp.bfloat16)
+
+
+def turn_body(filters_ref, out_ref):
+    out_ref[...] = filters_ref[...].T
 
 
 def grad_body(count, *refs):
@@ -249,13 +254,14 @@
     tile = codes.reshape(pixels, atoms)
     two = along(codes, TWO).reshape(pixels, atoms)
     near = along(codes, NEAR).reshape(pixels, atoms)
+    swapped = along(codes, INNER).reshape(pixels, atoms)
 
     own_filters = jnp.transpose(master, (1, 2, 0, 3)).reshape(taps * taps, own_bands, atoms).astype(jnp.bfloat16)
     filters = [own_filters]
     for s in range(1, groups):
         filters.append(shifted(own_filters, "row", s))
     filters = jnp.concatenate(filters, axis=1).reshape(taps * taps * bands, atoms)
-    turned = filters.T
+    (turned,) = call(turn_body, [struct(filters.shape[::-1], filters.dtype)], [filters])
 
     picture = image.reshape(pixels, groups, count, own_bands).transpose(1, 2, 3, 0)
     picture = jnp.stack([lax.dynamic_index_in_dim(picture, (row_at + groups - s) % groups, 0, False) for s in range(groups)])
@@ -265,7 +271,6 @@
         images.append(pieces[s] if s == 0 else shifted(pieces[s], "col", s))
 
     passed = along(two, [(2, 3), (1, 0)])
-    swapped = along(tile, INNER)
 
     size = struct((bands, ext), jnp.float32)
     y_scratch = [pltpu.VMEM((taps * taps * bands, pixels), jnp.float32)]
@@ -301,22 +306,23 @@
     else:
         others = [(lax.psum(send, "atom").astype(jnp.float32) - send.astype(jnp.float32)).astype(jnp.bfloat16)]
 
-    def back_of(which, dtype, *args, peers=None):
-        outs = [struct((taps * taps * bands, pixels), jnp.bfloat16), struct((atoms, pixels), dtype)]
+    def back_of(which, dtypes, *args, peers=None):
+        outs = [struct((taps * taps * bands, pixels), jnp.bfloat16)] + [struct((atoms, pixels), dtype) for dtype in dtypes]
         if peers is not None:
             outs.append(struct(part_shape, jnp.float32))
         body = functools.partial(back_body, taps, bands, ext, rows, cols, which, peers)
         return call(body, outs, [turned, *args], tile_flops)
 
-    far_windows, far_back, resid = back_of("far", jnp.bfloat16, part, *others, peers=len(others))
+    far_windows, far_back, resid = back_of("far", [jnp.bfloat16], part, *others, peers=len(others))
     home_pass = along(far_back, [(3, 2), (0, 1)])
     home_swap = along(far_back, INNER)
-    near_windows, near_back = back_of("near", jnp.bfloat16, resid)
+    two_windows, two_back, two_send = back_of("two", [jnp.float32, jnp.bfloat16], resid)
+    home_two = along(two_send, TWO[::3])
+    near_windows, near_back = back_of("near", [jnp.bfloat16], resid)
     home_near = along(near_back, NEAR)
-    two_windows, two_back = back_of("two", jnp.float32, resid)
-    own_windows, own_back = back_of("own", jnp.float32, resid)
+    own_windows, own_back = back_of("own", [jnp.float32], resid)
     (two_back,) = call(merge_body, [struct((atoms, pixels), jnp.bfloat16)], [two_back, home_pass])
-    home_two = along(two_back, TWO)
+    home_both = along(two_back, TWO[1:3])
     (grad,) = call(
         functools.partial(grad_body, count),
         [struct((taps * taps * bands, atoms), jnp.float32)],
@@ -332,7 +338,7 @@
     own_grad = jnp.transpose(own_grad.reshape(taps, taps, own_bands, atoms), (2, 0, 1, 3))
     new_dictionary, new_moment, new_second = adam_update(master, moment, second, own_grad)
     (new_codes,) = call(
-        codes_body, [struct((pixels, atoms), jnp.bfloat16)], [tile, own_back, home_near, home_swap, home_two]
+        codes_body, [struct((pixels, atoms), jnp.bfloat16)], [tile, own_back, home_near, home_swap, home_two, home_both]
     )
     return (new_codes.reshape(rows, cols, atoms), new_dictionary, new_moment, new_second)
 

time: 78.7 us -> 78.1 us (level)
  waiting for transfers between devices: 30.6 us -> 32.4 us
  local copies, waits for them, and re-layouts: 4.08 us -> 2.72 us
  Pallas kernels: 11.8 us -> 10.7 us
    ppermute x8 -> x9, starting transfers between devices: 15 us -> 17.2 us  [along(): return lax.ppermute(x, 'col', pairs)]
    ppermute x6, starting transfers between devices: 6.21 us -> 4.22 us  [shifted(): lax.ppermute(x, axis, [(i, (i + step) % count) for i in range(count)])]
    reshape x1 -> x0, local copies, waits for them, and re-layouts: 1.31 us -> none  [iteration(): jnp.concatenate(filters, axis=1).reshape(taps * taps * bands, atoms)]
    ppermute x8 -> x9, waiting for transfers between devices: 22.8 us -> 24.1 us  [along(): return lax.ppermute(x, 'col', pairs)]
    pallas_call x12 -> x13, Pallas kernels: 11.8 us -> 10.7 us  [call(): pl.pallas_call(body, out_shape=outs, in_specs=[pl.BlockSpec(memory_space=...]
    unnamed x26 -> x12, local copies, waits for them, and re-layouts: 2.1 us -> 2.05 us
  transfers between devices with their start and end apart: 17 -> 18, of which waited for: 8 -> 9; matrix products, arithmetic and copies ran while one was open for 4% -> 3% of each run, Pallas kernels for 5% -> 5%
where the time goes in v5:
time: 78.1 us; the launch traced here: 77.8 us
  waiting for transfers between devices  32.4 us (41%)
  starting transfers between devices  24.9 us (32%)
  Pallas kernels  10.7 us (14%)
  other arithmetic  6.12 us (8%)
  local copies, waits for them, and re-layouts  2.72 us (3%)
  between operations  0.9 us (1%)
    ppermute x9, waiting for transfers between devices, along(): return lax.ppermute(x, 'col', pairs)  24.1 us
    ppermute x9, starting transfers between devices, along(): return lax.ppermute(x, 'col', pairs)  17.2 us
    pallas_call x13, Pallas kernels, call(): pl.pallas_call(body, out_shape=outs, in_specs=[pl.BlockSpec(memory_space=...  10.7 us
    ppermute x6, waiting for transfers between devices, shifted(): lax.ppermute(x, axis, [(i, (i + step) % count) for i in range(count)])  4.5 us
    ppermute x6, starting transfers between devices, shifted(): lax.ppermute(x, axis, [(i, (i + step) % count) for i in range(count)])  4.22 us
    ppermute x3, waiting for transfers between devices, iteration(): lax.ppermute(send, 'atom', [(i, i ^ m) for i in range(peers)])  3.88 us
    ppermute x3, starting transfers between devices, iteration(): lax.ppermute(send, 'atom', [(i, i ^ m) for i in range(peers)])  3.55 us
    sub x1, other arithmetic, adam_update(): master - 0.05 * (new_moment / first_fix) / (jnp.sqrt(new_second / second_...  2.97 us
  transfers between devices with their start and end apart: 18, of which 9 were waited for; matrix products, arithmetic and copies ran while one was open for 3% of the time, Pallas kernels for 5%

profile of v5, /device:TPU:0, one launch (start us, length us, event | category | flops | bytes accessed | tf_op | source)
XLA Modules:
  0.0 77.8 jit_solution(17172980204513253944)
XLA Ops:
  0.7 1.6 %convert_element_type.16 = bf16[16,7,7,512]{3,0,2,1:T(8,128)(2,1)S(1)} convert(f32[16,7,7,512]{3,0,2,1:T(8,128)} %param.7) | non-fusion elementwise | flops 401408 | bytes 2408448 | tf_op jit(solution)/shard_map/convert_element_type | solution.py:259
  2.8 3.7 %collective-permute-start.2 = (bf16[16,16,512]{2,1,0:T(8,128)(2,1)S(1)}, bf16[16,16,512]{2,1,0:T(8,128)(2,1)S(1)}, u32[]{:S(2)}, u32[]{:S(2)}) collective-permute-start(bf16[16,16,512]{2,1,0:T(8,128)(2,1)S(1)} %copy-done), channel_id=1, source_target_pairs={{0,2},{1,3},{2,0},{3,1},{4,6},{5,7},{6,4},{7,5},{8,10},{9,11},{10,... | collective-permute-start | bytes 786440 | tf_op jit(solution)/shard_map/ppermute | solution.py:31
  7.1 2.9 %collective-permute-start.4 = (bf16[16,16,512]{2,1,0:T(8,128)(2,1)S(1)}, bf16[16,16,512]{2,1,0:T(8,128)(2,1)S(1)}, u32[]{:S(2)}, u32[]{:S(2)}) collective-permute-start(bf16[16,16,512]{2,1,0:T(8,128)(2,1)S(1)} %copy-done), channel_id=1, source_target_pairs={{0,1},{1,0},{2,3},{3,2},{4,5},{5,4},{6,7},{7,6},{8,9},{9,8},{10,11... | collective-permute-start | bytes 786440 | tf_op jit(solution)/shard_map/ppermute | solution.py:31
  11.1 8.2 %collective-permute-done.2 = bf16[16,16,512]{2,1,0:T(8,128)(2,1)S(1)} collective-permute-done((bf16[16,16,512]{2,1,0:T(8,128)(2,1)S(1)}, bf16[16,16,512]{2,1,0:T(8,128)(2,1)S(1)}, u32[]{:S(2)}, u32[]{:S(2)}) %collective-permute-start.2) | collective-permute-done | bytes 262176 | tf_op jit(solution)/shard_map/ppermute | solution.py:31
  19.3 1.3 %collective-permute-start.3 = (bf16[256,512]{1,0:T(8,128)(2,1)S(1)}, bf16[256,512]{1,0:T(8,128)(2,1)S(1)}, u32[]{:S(2)}, u32[]{:S(2)}) collective-permute-start(bf16[256,512]{1,0:T(8,128)(2,1)S(1)} %bitcast.37), channel_id=1, source_target_pairs={{2,3},{1,0},{6,7},{5,4},{10,11},{9,8},{14,15},{13,12},{18,19},{17,... | collective-permute-start | bytes 786440 | tf_op jit(solution)/shard_map/ppermute | solution.py:31
  20.6 1.3 %pad_maximum_fusion = bf16[49,32,512]{2,1,0:T(8,128)(2,1)S(1)} fusion(bf16[49,16,512]{2,1,0:T(8,128)(2,1)} %collective-permute-done, bf16[49,16,512]{2,1,0:T(8,128)(2,1)S(1)} %bitcast.46), kind=kLoop, calls=%fused_computation.5 | loop fusion | flops 3211264 | bytes 3211264 | tf_op jit(solution)/shard_map/concatenate | solution.py:263
  21.9 0.9 %shard_map.86 = (f32[32,384]{1,0:T(8,128)S(1)}, f32[32,384]{1,0:T(8,128)S(1)}) custom-call(bf16[1568,512]{1,0:T(8,128)(2,1)S(1)} %bitcast.27, bf16[256,512]{1,0:T(8,128)(2,1)S(1)} %bitcast.38), custom_call_target="tpu_custom_call" | custom-call | flops 411041792 | bytes 1966080 | tf_op jit(solution)/shard_map/pallas_call | solution.py:36
  22.8 0.9 %shard_map.85 = (f32[32,384]{1,0:T(8,128)S(1)}, f32[32,384]{1,0:T(8,128)S(1)}) custom-call(bf16[1568,512]{1,0:T(8,128)(2,1)S(1)} %bitcast.28, bf16[256,512]{1,0:T(8,128)(2,1)S(1)} %bitcast.34), custom_call_target="tpu_custom_call" | custom-call | flops 411041792 | bytes 1966080 | tf_op jit(solution)/shard_map/pallas_call | solution.py:36
  23.8 3.4 %collective-permute-start.7 = (bf16[32,256]{1,0:T(8,128)(2,1)S(1)}, bf16[32,256]{1,0:T(8,128)(2,1)S(1)}, u32[]{:S(2)}, u32[]{:S(2)}) collective-permute-start(bf16[32,256]{1,0:T(8,128)(2,1)S(1)} %bitcast.50), channel_id=1, source_target_pairs={{0,3},{1,0},{2,1},{3,2},{4,7},{5,4},{6,5},{7,6},{8,11},{9,8},{10,9... | collective-permute-start | bytes 49160 | tf_op jit(solution)/shard_map/ppermute | solution.py:17
  27.1 0.9 %shard_map.87 = (f32[32,384]{1,0:T(8,128)S(1)}, f32[32,384]{1,0:T(8,128)S(1)}) custom-call(bf16[1568,512]{1,0:T(8,128)(2,1)S(1)} %bitcast.29, bf16[256,512]{1,0:T(8,128)(2,1)S(1)} %bitcast.40), custom_call_target="tpu_custom_call" | custom-call | flops 411041792 | bytes 1966080 | tf_op jit(solution)/shard_map/pallas_call | solution.py:36
  28.1 3.2 %collective-permute-done.7.refs_12_ = bf16[32,256]{1,0:T(8,128)(2,1)S(1)} collective-permute-done((bf16[32,256]{1,0:T(8,128)(2,1)S(1)}, bf16[32,256]{1,0:T(8,128)(2,1)S(1)}, u32[]{:S(2)}, u32[]{:S(2)}) %collective-permute-start.7) | collective-permute-done | bytes 16416 | tf_op jit(solution)/shard_map/ppermute | solution.py:17
  31.4 1.0 %shard_map.88 = (f32[4,32,384]{2,1,0:T(8,128)S(1)}, bf16[256,512]{1,0:T(8,128)(2,1)S(1)}, f32[4,32,128]{2,1,0:T(8,128)S(1)}) custom-call(bf16[1568,512]{1,0:T(8,128)(2,1)S(1)} %bitcast.30, bf16[256,512]{1,0:T(8,128)(2,1)S(1)} %bitcast.42, bf16[256,512]{1,0:T(8,128)(2,1)S(1)} %collective-permute-done.3.refs_2_, f32[32,384]{1,0:T(8,128)S(1)} %get-tuple-element.25.refs_3_, ...), custom_call_target="tpu_custom_call" | custom-call | flops 411041792 | bytes 3014656 | tf_op jit(solution)/shard_map/pallas_call | solution.py:36
  32.4 1.2 %collective-permute-done.8.refs_1_ = f32[4,32,128]{2,1,0:T(8,128)S(1)} collective-permute-done((f32[4,32,128]{2,1,0:T(8,128)S(1)}, f32[4,32,128]{2,1,0:T(8,128)S(1)}, u32[]{:S(2)}, u32[]{:S(2)}) %collective-permute-start.8) | collective-permute-done | bytes 65568 | tf_op jit(solution)/shard_map/ppermute | solution.py:17
  33.7 2.4 %collective-permute-start.9 = (bf16[4,32,384]{2,1,0:T(8,128)(2,1)S(1)}, bf16[4,32,384]{2,1,0:T(8,128)(2,1)S(1)}, u32[]{:S(2)}, u32[]{:S(2)}) collective-permute-start(bf16[4,32,384]{2,1,0:T(8,128)(2,1)S(1)} %get-tuple-element.34), channel_id=1, source_target_pairs={{0,24},{8,16},{16,8},{24,0},{1,25},{9,17},{17,9},{25,1},{2,26},{10... | collective-permute-start | bytes 294920 | tf_op jit(solution)/shard_map/ppermute | solution.py:305
  37.7 1.9 %collective-permute-done.9.refs_2_ = bf16[4,32,384]{2,1,0:T(8,128)(2,1)S(1)} collective-permute-done((bf16[4,32,384]{2,1,0:T(8,128)(2,1)S(1)}, bf16[4,32,384]{2,1,0:T(8,128)(2,1)S(1)}, u32[]{:S(2)}, u32[]{:S(2)}) %collective-permute-start.9) | collective-permute-done | bytes 98336 | tf_op jit(solution)/shard_map/ppermute | solution.py:305
  39.6 2.0 %collective-permute-done.10.refs_3_ = bf16[4,32,384]{2,1,0:T(8,128)(2,1)S(1)} collective-permute-done((bf16[4,32,384]{2,1,0:T(8,128)(2,1)S(1)}, bf16[4,32,384]{2,1,0:T(8,128)(2,1)S(1)}, u32[]{:S(2)}, u32[]{:S(2)}) %collective-permute-start.10) | collective-permute-done | bytes 98336 | tf_op jit(solution)/shard_map/ppermute | solution.py:305
  41.6 0.9 %shard_map.90 = (bf16[1568,256]{1,0:T(8,128)(2,1)S(1)}, bf16[512,256]{1,0:T(8,128)(2,1)S(1)}, f32[4,32,384]{2,1,0:T(8,128)S(1)}) custom-call(bf16[512,1568]{1,0:T(8,128)(2,1)S(1)} %shard_map.84.refs_0_, f32[4,32,384]{2,1,0:T(8,128)S(1)} %get-tuple-element.33.refs_1_, bf16[4,32,384]{2,1,0:T(8,128)(2,1)S(1)} %collective-permute-done.9.refs_2_, ...), custom_call_target="tpu_custom_call" | custom-call | flops 411041792 | bytes 3358720 | tf_op jit(solution)/shard_map/pallas_call | solution.py:36
  42.6 0.9 %shard_map.91 = (bf16[1568,256]{1,0:T(8,128)(2,1)S(1)}, f32[512,256]{1,0:T(8,128)S(1)}) custom-call(bf16[512,1568]{1,0:T(8,128)(2,1)S(1)} %shard_map.84.refs_0_, f32[4,32,384]{2,1,0:T(8,128)S(1)} %get-tuple-element.35.refs_1_), custom_call_target="tpu_custom_call" | custom-call | flops 411041792 | bytes 3129344 | tf_op jit(solution)/shard_map/pallas_call | solution.py:36
  43.4 0.9 %shard_map.92 = (bf16[1568,256]{1,0:T(8,128)(2,1)S(1)}, bf16[512,256]{1,0:T(8,128)(2,1)S(1)}) custom-call(bf16[512,1568]{1,0:T(8,128)(2,1)S(1)} %shard_map.84.refs_0_, f32[4,32,384]{2,1,0:T(8,128)S(1)} %get-tuple-element.35.refs_1_), custom_call_target="tpu_custom_call" | custom-call | flops 411041792 | bytes 2867200 | tf_op jit(solution)/shard_map/pallas_call | solution.py:36
  44.4 0.9 %shard_map.93 = (bf16[1568,256]{1,0:T(8,128)(2,1)S(1)}, f32[512,256]{1,0:T(8,128)S(1)}, bf16[512,256]{1,0:T(8,128)(2,1)S(1)}) custom-call(bf16[512,1568]{1,0:T(8,128)(2,1)S(1)} %shard_map.84.refs_0_, f32[4,32,384]{2,1,0:T(8,128)S(1)} %get-tuple-element.35.refs_1_), custom_call_target="tpu_custom_call" | custom-call | flops 411041792 | bytes 3391488 | tf_op jit(solution)/shard_map/pallas_call | solution.py:36
  45.2 1.8 %shard_map.96 = f32[1568,512]{1,0:T(8,128)S(1)} custom-call(bf16[1568,256]{1,0:T(8,128)(2,1)S(1)} %get-tuple-element.41.refs_0_, bf16[1568,256]{1,0:T(8,128)(2,1)S(1)} %get-tuple-element.42.refs_1_, bf16[1568,256]{1,0:T(8,128)(2,1)S(1)} %get-tuple-element.43.refs_2_, bf16[1568,256]{1,0:T(8,128)(2,1)S(1)} %get-tuple-element.44.refs_3_, ...), custom_call_target="tpu_custom_call" | custom-call | flops 1644167168 | bytes 7471104 | tf_op jit(solution)/shard_map/pallas_call | solution.py:36
  47.3 2.1 %collective-permute-start.15 = (bf16[512,256]{1,0:T(8,128)(2,1)S(1)}, bf16[512,256]{1,0:T(8,128)(2,1)S(1)}, u32[]{:S(2)}, u32[]{:S(2)}) collective-permute-start(bf16[512,256]{1,0:T(8,128)(2,1)S(1)} %get-tuple-element.38), channel_id=1, source_target_pairs={{3,2},{0,1},{7,6},{4,5},{11,10},{8,9},{15,14},{12,13},{19,18},{16,... | collective-permute-start | bytes 786440 | tf_op jit(solution)/shard_map/ppermute | solution.py:31
  50.1 1.9 %collective-permute-start.12 = (bf16[512,256]{1,0:T(8,128)(2,1)S(1)}, bf16[512,256]{1,0:T(8,128)(2,1)S(1)}, u32[]{:S(2)}, u32[]{:S(2)}) collective-permute-start(bf16[512,256]{1,0:T(8,128)(2,1)S(1)} %get-tuple-element.37), channel_id=1, source_target_pairs={{0,1},{1,0},{2,3},{3,2},{4,5},{5,4},{6,7},{7,6},{8,9},{9,8},{10,11... | collective-permute-start | bytes 786440 | tf_op jit(solution)/shard_map/ppermute | solution.py:31
  51.9 2.8 %collective-permute-start.14 = (bf16[512,256]{1,0:T(8,128)(2,1)S(1)}, bf16[512,256]{1,0:T(8,128)(2,1)S(1)}, u32[]{:S(2)}, u32[]{:S(2)}) collective-permute-start(bf16[512,256]{1,0:T(8,128)(2,1)S(1)} %get-tuple-element.39), channel_id=1, source_target_pairs={{0,2},{3,1},{4,6},{7,5},{8,10},{11,9},{12,14},{15,13},{16,18},{19,... | collective-permute-start | bytes 786440 | tf_op jit(solution)/shard_map/ppermute | solution.py:31
  54.7 1.4 %collective-permute-done.15.passed_ref = bf16[512,256]{1,0:T(8,128)(2,1)S(1)} collective-permute-done((bf16[512,256]{1,0:T(8,128)(2,1)S(1)}, bf16[512,256]{1,0:T(8,128)(2,1)S(1)}, u32[]{:S(2)}, u32[]{:S(2)}) %collective-permute-start.15) | collective-permute-done | bytes 262176 | tf_op jit(solution)/shard_map/ppermute | solution.py:31
  56.1 1.3 %collective-permute-start.16 = (bf16[512,256]{1,0:T(8,128)(2,1)S(1)}, bf16[512,256]{1,0:T(8,128)(2,1)S(1)}, u32[]{:S(2)}, u32[]{:S(2)}) collective-permute-start(bf16[512,256]{1,0:T(8,128)(2,1)S(1)} %shard_map.94), channel_id=1, source_target_pairs={{1,3},{2,0},{5,7},{6,4},{9,11},{10,8},{13,15},{14,12},{17,19},{18,... | collective-permute-start | bytes 786440 | tf_op jit(solution)/shard_map/ppermute | solution.py:31
  57.4 4.3 %collective-permute-done.12.refs_2_ = bf16[512,256]{1,0:T(8,128)(2,1)S(1)} collective-permute-done((bf16[512,256]{1,0:T(8,128)(2,1)S(1)}, bf16[512,256]{1,0:T(8,128)(2,1)S(1)}, u32[]{:S(2)}, u32[]{:S(2)}) %collective-permute-start.12) | collective-permute-done | bytes 262176 | tf_op jit(solution)/shard_map/ppermute | solution.py:31
  61.7 5.2 %collective-permute-done.14.refs_4_ = bf16[512,256]{1,0:T(8,128)(2,1)S(1)} collective-permute-done((bf16[512,256]{1,0:T(8,128)(2,1)S(1)}, bf16[512,256]{1,0:T(8,128)(2,1)S(1)}, u32[]{:S(2)}, u32[]{:S(2)}) %collective-permute-start.14) | collective-permute-done | bytes 262176 | tf_op jit(solution)/shard_map/ppermute | solution.py:31
  66.8 5.0 %collective-permute-done.16.refs_5_ = bf16[512,256]{1,0:T(8,128)(2,1)S(1)} collective-permute-done((bf16[512,256]{1,0:T(8,128)(2,1)S(1)}, bf16[512,256]{1,0:T(8,128)(2,1)S(1)}, u32[]{:S(2)}, u32[]{:S(2)}) %collective-permute-start.16) | collective-permute-done | bytes 262176 | tf_op jit(solution)/shard_map/ppermute | solution.py:31
  71.9 1.0 %shard_map.95 = bf16[256,512]{1,0:T(8,128)(2,1)} custom-call(bf16[256,512]{1,0:T(8,128)(2,1)S(1)} %bitcast.36, f32[512,256]{1,0:T(8,128)S(1)} %get-tuple-element.36.refs_1_, bf16[512,256]{1,0:T(8,128)(2,1)S(1)} %collective-permute-done.12.refs_2_, bf16[512,256]{1,0:T(8,128)(2,1)S(1)} %collective-permute-done.13.refs_3_, ...), custom_call_target="tpu_custom_call" | custom-call | bytes 2097152 | tf_op jit(solution)/shard_map/pallas_call | solution.py:36
  73.4 1.0 %copy-done.1 = f32[16,7,7,512]{3,0,2,1:T(8,128)S(1)} copy-done((f32[16,7,7,512]{3,0,2,1:T(8,128)S(1)}, f32[16,7,7,512]{3,0,2,1:T(8,128)}, u32[]{:S(2)}) %copy-start.1) | copy-done | bytes 1605656
  74.8 3.0 %divide_subtract_fusion = (f32[16,7,7,512]{3,0,2,1:T(8,128)}, f32[16,7,7,512]{3,0,2,1:T(8,128)}, f32[16,7,7,512]{3,0,2,1:T(8,128)}) fusion(f32[16,7,7,512]{3,0,2,1:T(8,128)S(1)} %copy-done.1, f32[16,7,7,512]{3,0,2,1:T(8,128)S(1)} %bitcast.44, f32[16,7,7,512]{3,0,2,1:T(8,128)S(1)} %copy-done.2, f32[16,7,7,512]{3,0,2,1:T(8,128)S(1)} %copy-done.3), kind=kLoop, calls=%fused_computation.6 | loop fusion | flops 4816896 | bytes 11239424 | tf_op jit(solution)/shard_map/sub | solution.py:237
  (37 shorter events, 5.9 us)
Async XLA Ops:
  0.6 2.2 %copy-start = (bf16[16,16,512]{2,1,0:T(8,128)(2,1)S(1)}, bf16[16,16,512]{2,1,0:T(8,128)(2,1)}, u32[]{:S(2)}) copy-start(bf16[16,16,512]{2,1,0:T(8,128)(2,1)} %param.5) | copy-start | bytes 786436
  0.6 9.4 %copy-start.4 = (bf16[16,16,128]{2,1,0:T(8,128)(2,1)S(1)}, bf16[16,16,128]{2,1,0:T(8,128)(2,1)}, u32[]{:S(2)}) copy-start(bf16[16,16,128]{2,1,0:T(8,128)(2,1)} %param.6) | copy-start | bytes 196612
  2.2 17.0 %collective-permute-start = (bf16[49,16,512]{2,1,0:T(8,128)(2,1)S(1)}, bf16[49,16,512]{2,1,0:T(8,128)(2,1)}, u32[]{:S(2)}, u32[]{:S(2)}) collective-permute-start(bf16[49,16,512]{2,1,0:T(8,128)(2,1)S(1)} %bitcast.45), channel_id=1, source_target_pairs={{0,4},{4,0},{1,5},{5,1},{2,6},{6,2},{3,7},{7,3},{8,12},{12,8},{9,1... | collective-permute-start | bytes 2408456 | tf_op jit(solution)/shard_map/ppermute | solution.py:17
  2.8 16.5 %collective-permute-start.2 = (bf16[16,16,512]{2,1,0:T(8,128)(2,1)S(1)}, bf16[16,16,512]{2,1,0:T(8,128)(2,1)S(1)}, u32[]{:S(2)}, u32[]{:S(2)}) collective-permute-start(bf16[16,16,512]{2,1,0:T(8,128)(2,1)S(1)} %copy-done), channel_id=1, source_target_pairs={{0,2},{1,3},{2,0},{3,1},{4,6},{5,7},{6,4},{7,5},{8,10},{9,11},{10,... | collective-permute-start | bytes 786440 | tf_op jit(solution)/shard_map/ppermute | solution.py:31
  6.5 24.9 %collective-permute-start.1 = (bf16[16,16,512]{2,1,0:T(8,128)(2,1)S(1)}, bf16[16,16,512]{2,1,0:T(8,128)(2,1)S(1)}, u32[]{:S(2)}, u32[]{:S(2)}) collective-permute-start(bf16[16,16,512]{2,1,0:T(8,128)(2,1)S(1)} %copy-done), channel_id=1, source_target_pairs={{1,2},{2,1},{5,6},{6,5},{9,10},{10,9},{13,14},{14,13},{17,18},{18,... | collective-permute-start | bytes 786440 | tf_op jit(solution)/shard_map/ppermute | solution.py:31
  7.1 16.6 %collective-permute-start.4 = (bf16[16,16,512]{2,1,0:T(8,128)(2,1)S(1)}, bf16[16,16,512]{2,1,0:T(8,128)(2,1)S(1)}, u32[]{:S(2)}, u32[]{:S(2)}) collective-permute-start(bf16[16,16,512]{2,1,0:T(8,128)(2,1)S(1)} %copy-done), channel_id=1, source_target_pairs={{0,1},{1,0},{2,3},{3,2},{4,5},{5,4},{6,7},{7,6},{8,9},{9,8},{10,11... | collective-permute-start | bytes 786440 | tf_op jit(solution)/shard_map/ppermute | solution.py:31
  10.9 17.2 %collective-permute-start.5 = (bf16[32,256]{1,0:T(8,128)(2,1)S(1)}, bf16[32,256]{1,0:T(8,128)(2,1)S(1)}, u32[]{:S(2)}, u32[]{:S(2)}) collective-permute-start(bf16[32,256]{1,0:T(8,128)(2,1)S(1)} %bitcast.52), channel_id=1, source_target_pairs={{0,1},{1,2},{2,3},{3,0},{4,5},{5,6},{6,7},{7,4},{8,9},{9,10},{10,1... | collective-permute-start | bytes 49160 | tf_op jit(solution)/shard_map/ppermute | solution.py:17
  19.3 8.8 %collective-permute-start.6 = (bf16[32,256]{1,0:T(8,128)(2,1)S(1)}, bf16[32,256]{1,0:T(8,128)(2,1)S(1)}, u32[]{:S(2)}, u32[]{:S(2)}) collective-permute-start(bf16[32,256]{1,0:T(8,128)(2,1)S(1)} %bitcast.51), channel_id=1, source_target_pairs={{0,2},{1,3},{2,0},{3,1},{4,6},{5,7},{6,4},{7,5},{8,10},{9,11},{10,... | collective-permute-start | bytes 49160 | tf_op jit(solution)/shard_map/ppermute | solution.py:17
  19.3 12.1 %collective-permute-start.3 = (bf16[256,512]{1,0:T(8,128)(2,1)S(1)}, bf16[256,512]{1,0:T(8,128)(2,1)S(1)}, u32[]{:S(2)}, u32[]{:S(2)}) collective-permute-start(bf16[256,512]{1,0:T(8,128)(2,1)S(1)} %bitcast.37), channel_id=1, source_target_pairs={{2,3},{1,0},{6,7},{5,4},{10,11},{9,8},{14,15},{13,12},{18,19},{17,... | collective-permute-start | bytes 786440 | tf_op jit(solution)/shard_map/ppermute | solution.py:31
  23.8 7.6 %collective-permute-start.7 = (bf16[32,256]{1,0:T(8,128)(2,1)S(1)}, bf16[32,256]{1,0:T(8,128)(2,1)S(1)}, u32[]{:S(2)}, u32[]{:S(2)}) collective-permute-start(bf16[32,256]{1,0:T(8,128)(2,1)S(1)} %bitcast.50), channel_id=1, source_target_pairs={{0,3},{1,0},{2,1},{3,2},{4,7},{5,4},{6,5},{7,6},{8,11},{9,8},{10,9... | collective-permute-start | bytes 49160 | tf_op jit(solution)/shard_map/ppermute | solution.py:17
  32.3 1.3 %collective-permute-start.8 = (f32[4,32,128]{2,1,0:T(8,128)S(1)}, f32[4,32,128]{2,1,0:T(8,128)S(1)}, u32[]{:S(2)}, u32[]{:S(2)}) collective-permute-start(f32[4,32,128]{2,1,0:T(8,128)S(1)} %get-tuple-element.32), channel_id=1, source_target_pairs={{0,4},{4,0},{1,5},{5,1},{2,6},{6,2},{3,7},{7,3},{8,12},{12,8},{9,1... | collective-permute-start | bytes 196616 | tf_op jit(solution)/shard_map/ppermute | solution.py:17
  33.7 5.9 %collective-permute-start.9 = (bf16[4,32,384]{2,1,0:T(8,128)(2,1)S(1)}, bf16[4,32,384]{2,1,0:T(8,128)(2,1)S(1)}, u32[]{:S(2)}, u32[]{:S(2)}) collective-permute-start(bf16[4,32,384]{2,1,0:T(8,128)(2,1)S(1)} %get-tuple-element.34), channel_id=1, source_target_pairs={{0,24},{8,16},{16,8},{24,0},{1,25},{9,17},{17,9},{25,1},{2,26},{10... | collective-permute-start | bytes 294920 | tf_op jit(solution)/shard_map/ppermute | solution.py:305
  36.1 5.5 %collective-permute-start.10 = (bf16[4,32,384]{2,1,0:T(8,128)(2,1)S(1)}, bf16[4,32,384]{2,1,0:T(8,128)(2,1)S(1)}, u32[]{:S(2)}, u32[]{:S(2)}) collective-permute-start(bf16[4,32,384]{2,1,0:T(8,128)(2,1)S(1)} %get-tuple-element.34), channel_id=1, source_target_pairs={{0,16},{8,24},{16,0},{24,8},{1,17},{9,25},{17,1},{25,9},{2,18},{10... | collective-permute-start | bytes 294920 | tf_op jit(solution)/shard_map/ppermute | solution.py:305
  36.6 5.0 %collective-permute-start.11 = (bf16[4,32,384]{2,1,0:T(8,128)(2,1)S(1)}, bf16[4,32,384]{2,1,0:T(8,128)(2,1)S(1)}, u32[]{:S(2)}, u32[]{:S(2)}) collective-permute-start(bf16[4,32,384]{2,1,0:T(8,128)(2,1)S(1)} %get-tuple-element.34), channel_id=1, source_target_pairs={{0,8},{8,0},{16,24},{24,16},{1,9},{9,1},{17,25},{25,17},{2,10},{10... | collective-permute-start | bytes 294920 | tf_op jit(solution)/shard_map/ppermute | solution.py:305
  47.2 25.6 %collective-permute-start.17 = (bf16[49,16,512]{2,1,0:T(8,128)(2,1)S(1)}, bf16[49,16,512]{2,1,0:T(8,128)(2,1)S(1)}, u32[]{:S(2)}, u32[]{:S(2)}) collective-permute-start(bf16[49,16,512]{2,1,0:T(8,128)(2,1)S(1)} %fusion.2), channel_id=1, source_target_pairs={{0,4},{4,0},{1,5},{5,1},{2,6},{6,2},{3,7},{7,3},{8,12},{12,8},{9,1... | collective-permute-start | bytes 2408456 | tf_op jit(solution)/shard_map/ppermute | solution.py:17
  47.3 8.8 %collective-permute-start.15 = (bf16[512,256]{1,0:T(8,128)(2,1)S(1)}, bf16[512,256]{1,0:T(8,128)(2,1)S(1)}, u32[]{:S(2)}, u32[]{:S(2)}) collective-permute-start(bf16[512,256]{1,0:T(8,128)(2,1)S(1)} %get-tuple-element.38), channel_id=1, source_target_pairs={{3,2},{0,1},{7,6},{4,5},{11,10},{8,9},{15,14},{12,13},{19,18},{16,... | collective-permute-start | bytes 786440 | tf_op jit(solution)/shard_map/ppermute | solution.py:31
  49.4 12.3 %collective-permute-start.13 = (bf16[512,256]{1,0:T(8,128)(2,1)S(1)}, bf16[512,256]{1,0:T(8,128)(2,1)S(1)}, u32[]{:S(2)}, u32[]{:S(2)}) collective-permute-start(bf16[512,256]{1,0:T(8,128)(2,1)S(1)} %get-tuple-element.38), channel_id=1, source_target_pairs={{1,2},{2,1},{5,6},{6,5},{9,10},{10,9},{13,14},{14,13},{17,18},{18,... | collective-permute-start | bytes 786440 | tf_op jit(solution)/shard_map/ppermute | solution.py:31
  50.1 11.6 %collective-permute-start.12 = (bf16[512,256]{1,0:T(8,128)(2,1)S(1)}, bf16[512,256]{1,0:T(8,128)(2,1)S(1)}, u32[]{:S(2)}, u32[]{:S(2)}) collective-permute-start(bf16[512,256]{1,0:T(8,128)(2,1)S(1)} %get-tuple-element.37), channel_id=1, source_target_pairs={{0,1},{1,0},{2,3},{3,2},{4,5},{5,4},{6,7},{7,6},{8,9},{9,8},{10,11... | collective-permute-start | bytes 786440 | tf_op jit(solution)/shard_map/ppermute | solution.py:31
  51.9 14.9 %collective-permute-start.14 = (bf16[512,256]{1,0:T(8,128)(2,1)S(1)}, bf16[512,256]{1,0:T(8,128)(2,1)S(1)}, u32[]{:S(2)}, u32[]{:S(2)}) collective-permute-start(bf16[512,256]{1,0:T(8,128)(2,1)S(1)} %get-tuple-element.39), channel_id=1, source_target_pairs={{0,2},{3,1},{4,6},{7,5},{8,10},{11,9},{12,14},{15,13},{16,18},{19,... | collective-permute-start | bytes 786440 | tf_op jit(solution)/shard_map/ppermute | solution.py:31
  56.1 15.8 %collective-permute-start.16 = (bf16[512,256]{1,0:T(8,128)(2,1)S(1)}, bf16[512,256]{1,0:T(8,128)(2,1)S(1)}, u32[]{:S(2)}, u32[]{:S(2)}) collective-permute-start(bf16[512,256]{1,0:T(8,128)(2,1)S(1)} %shard_map.94), channel_id=1, source_target_pairs={{1,3},{2,0},{5,7},{6,4},{9,11},{10,8},{13,15},{14,12},{17,19},{18,... | collective-permute-start | bytes 786440 | tf_op jit(solution)/shard_map/ppermute | solution.py:31
  71.9 1.5 %copy-start.3 = (f32[16,7,7,512]{3,0,2,1:T(8,128)S(1)}, f32[16,7,7,512]{3,0,2,1:T(8,128)}, u32[]{:S(2)}) copy-start(f32[16,7,7,512]{3,0,2,1:T(8,128)} %param.9) | copy-start | bytes 4816900
  72.8 1.5 %copy-start.1 = (f32[16,7,7,512]{3,0,2,1:T(8,128)S(1)}, f32[16,7,7,512]{3,0,2,1:T(8,128)}, u32[]{:S(2)}) copy-start(f32[16,7,7,512]{3,0,2,1:T(8,128)} %param.7) | copy-start | bytes 4816900
  72.8 2.0 %copy-start.2 = (f32[16,7,7,512]{3,0,2,1:T(8,128)S(1)}, f32[16,7,7,512]{3,0,2,1:T(8,128)}, u32[]{:S(2)}) copy-start(f32[16,7,7,512]{3,0,2,1:T(8,128)} %param.8) | copy-start | bytes 4816900

commit v6 on v5

--- a/solution.py
+++ b/solution.py
@@ -221,13 +221,16 @@
     grad_ref[...] = total
 
 
-def codes_body(*refs):
-    codes_ref, back_ref = refs[:2]
-    others, out_ref = refs[2:-1], refs[-1]
-    back = back_ref[...]
-    for other in others:
+def moved_body(codes_ref, *refs):
+    *backs, out_ref = refs
+    back = backs[0][...]
+    for other in backs[1:]:
         back = back + other[...].astype(jnp.float32)
-    moved = codes_ref[...].astype(jnp.float32) - 0.05 * back.T
+    out_ref[...] = codes_ref[...].astype(jnp.float32) - 0.05 * back.T
+
+
+def codes_body(moved_ref, back_ref, out_ref):
+    moved = moved_ref[...] - 0.05 * back_ref[...].astype(jnp.float32).T
     out_ref[...] = (moved - jnp.clip(moved, -0.02, 0.02)).astype(jnp.bfloat16)
 
 
@@ -337,9 +340,10 @@
         own_grad = own_grad + piece.astype(jnp.float32)
     own_grad = jnp.transpose(own_grad.reshape(taps, taps, own_bands, atoms), (2, 0, 1, 3))
     new_dictionary, new_moment, new_second = adam_update(master, moment, second, own_grad)
-    (new_codes,) = call(
-        codes_body, [struct((pixels, atoms), jnp.bfloat16)], [tile, own_back, home_near, home_swap, home_two, home_both]
-    )
+    (moved,) = call(
+        moved_body, [struct((pixels, atoms), jnp.float32)], [tile, own_back, home_near, home_swap, home_two]
+    )
+    (new_codes,) = call(codes_body, [struct((pixels, atoms), jnp.bfloat16)], [moved, home_both])
     return (new_codes.reshape(rows, cols, atoms), new_dictionary, new_moment, new_second)
 
 

time: 78.1 us -> 78 us (level)
    pallas_call x13 -> x14, Pallas kernels: 10.7 us -> 10.8 us  [call(): pl.pallas_call(body, out_shape=outs, in_specs=[pl.BlockSpec(memory_space=...]
  transfers between devices with their start and end apart: 18 -> 18, of which waited for: 9 -> 9; matrix products, arithmetic and copies ran while one was open for 3% -> 3% of each run, Pallas kernels for 5% -> 6%
where the time goes in v6:
time: 78 us; the launch traced here: 77.7 us
  waiting for transfers between devices  32.2 us (41%)
  starting transfers between devices  24.9 us (32%)
  Pallas kernels  10.8 us (14%)
  other arithmetic  6.12 us (8%)
  local copies, waits for them, and re-layouts  2.72 us (3%)
  between operations  0.91 us (1%)
    ppermute x9, waiting for transfers between devices, along(): return lax.ppermute(x, 'col', pairs)  23.8 us
    ppermute x9, starting transfers between devices, along(): return lax.ppermute(x, 'col', pairs)  17.2 us
    pallas_call x14, Pallas kernels, call(): pl.pallas_call(body, out_shape=outs, in_specs=[pl.BlockSpec(memory_space=...  10.8 us
    ppermute x6, waiting for transfers between devices, shifted(): lax.ppermute(x, axis, [(i, (i + step) % count) for i in range(count)])  4.5 us
    ppermute x6, starting transfers between devices, shifted(): lax.ppermute(x, axis, [(i, (i + step) % count) for i in range(count)])  4.22 us
    ppermute x3, waiting for transfers between devices, iteration(): lax.ppermute(send, 'atom', [(i, i ^ m) for i in range(peers)])  3.88 us
    ppermute x3, starting transfers between devices, iteration(): lax.ppermute(send, 'atom', [(i, i ^ m) for i in range(peers)])  3.55 us
    sub x1, other arithmetic, adam_update(): master - 0.05 * (new_moment / first_fix) / (jnp.sqrt(new_second / second_...  2.97 us
  transfers between devices with their start and end apart: 18, of which 9 were waited for; matrix products, arithmetic and copies ran while one was open for 3% of the time, Pallas kernels for 6%

profile of v6, /device:TPU:0, one launch (start us, length us, event | category | flops | bytes accessed | tf_op | source)
XLA Modules:
  0.0 77.7 jit_solution(6866802834467766789)
XLA Ops:
  0.7 1.6 %convert_element_type.16 = bf16[16,7,7,512]{3,0,2,1:T(8,128)(2,1)S(1)} convert(f32[16,7,7,512]{3,0,2,1:T(8,128)} %param.7) | non-fusion elementwise | flops 401408 | bytes 2408448 | tf_op jit(solution)/shard_map/convert_element_type | solution.py:262
  2.8 3.7 %collective-permute-start.2 = (bf16[16,16,512]{2,1,0:T(8,128)(2,1)S(1)}, bf16[16,16,512]{2,1,0:T(8,128)(2,1)S(1)}, u32[]{:S(2)}, u32[]{:S(2)}) collective-permute-start(bf16[16,16,512]{2,1,0:T(8,128)(2,1)S(1)} %copy-done), channel_id=1, source_target_pairs={{0,2},{1,3},{2,0},{3,1},{4,6},{5,7},{6,4},{7,5},{8,10},{9,11},{10,... | collective-permute-start | bytes 786440 | tf_op jit(solution)/shard_map/ppermute | solution.py:31
  7.1 2.9 %collective-permute-start.4 = (bf16[16,16,512]{2,1,0:T(8,128)(2,1)S(1)}, bf16[16,16,512]{2,1,0:T(8,128)(2,1)S(1)}, u32[]{:S(2)}, u32[]{:S(2)}) collective-permute-start(bf16[16,16,512]{2,1,0:T(8,128)(2,1)S(1)} %copy-done), channel_id=1, source_target_pairs={{0,1},{1,0},{2,3},{3,2},{4,5},{5,4},{6,7},{7,6},{8,9},{9,8},{10,11... | collective-permute-start | bytes 786440 | tf_op jit(solution)/shard_map/ppermute | solution.py:31
  11.1 8.2 %collective-permute-done.2 = bf16[16,16,512]{2,1,0:T(8,128)(2,1)S(1)} collective-permute-done((bf16[16,16,512]{2,1,0:T(8,128)(2,1)S(1)}, bf16[16,16,512]{2,1,0:T(8,128)(2,1)S(1)}, u32[]{:S(2)}, u32[]{:S(2)}) %collective-permute-start.2) | collective-permute-done | bytes 262176 | tf_op jit(solution)/shard_map/ppermute | solution.py:31
  19.3 1.3 %collective-permute-start.3 = (bf16[256,512]{1,0:T(8,128)(2,1)S(1)}, bf16[256,512]{1,0:T(8,128)(2,1)S(1)}, u32[]{:S(2)}, u32[]{:S(2)}) collective-permute-start(bf16[256,512]{1,0:T(8,128)(2,1)S(1)} %bitcast.37), channel_id=1, source_target_pairs={{2,3},{1,0},{6,7},{5,4},{10,11},{9,8},{14,15},{13,12},{18,19},{17,... | collective-permute-start | bytes 786440 | tf_op jit(solution)/shard_map/ppermute | solution.py:31
  20.6 1.3 %pad_maximum_fusion = bf16[49,32,512]{2,1,0:T(8,128)(2,1)S(1)} fusion(bf16[49,16,512]{2,1,0:T(8,128)(2,1)} %collective-permute-done, bf16[49,16,512]{2,1,0:T(8,128)(2,1)S(1)} %bitcast.46), kind=kLoop, calls=%fused_computation.5 | loop fusion | flops 3211264 | bytes 3211264 | tf_op jit(solution)/shard_map/concatenate | solution.py:266
  21.9 0.9 %shard_map.86 = (f32[32,384]{1,0:T(8,128)S(1)}, f32[32,384]{1,0:T(8,128)S(1)}) custom-call(bf16[1568,512]{1,0:T(8,128)(2,1)S(1)} %bitcast.27, bf16[256,512]{1,0:T(8,128)(2,1)S(1)} %bitcast.38), custom_call_target="tpu_custom_call" | custom-call | flops 411041792 | bytes 1966080 | tf_op jit(solution)/shard_map/pallas_call | solution.py:36
  22.8 0.9 %shard_map.85 = (f32[32,384]{1,0:T(8,128)S(1)}, f32[32,384]{1,0:T(8,128)S(1)}) custom-call(bf16[1568,512]{1,0:T(8,128)(2,1)S(1)} %bitcast.28, bf16[256,512]{1,0:T(8,128)(2,1)S(1)} %bitcast.34), custom_call_target="tpu_custom_call" | custom-call | flops 411041792 | bytes 1966080 | tf_op jit(solution)/shard_map/pallas_call | solution.py:36
  23.8 3.4 %collective-permute-start.7 = (bf16[32,256]{1,0:T(8,128)(2,1)S(1)}, bf16[32,256]{1,0:T(8,128)(2,1)S(1)}, u32[]{:S(2)}, u32[]{:S(2)}) collective-permute-start(bf16[32,256]{1,0:T(8,128)(2,1)S(1)} %bitcast.50), channel_id=1, source_target_pairs={{0,3},{1,0},{2,1},{3,2},{4,7},{5,4},{6,5},{7,6},{8,11},{9,8},{10,9... | collective-permute-start | bytes 49160 | tf_op jit(solution)/shard_map/ppermute | solution.py:17
  27.1 0.9 %shard_map.87 = (f32[32,384]{1,0:T(8,128)S(1)}, f32[32,384]{1,0:T(8,128)S(1)}) custom-call(bf16[1568,512]{1,0:T(8,128)(2,1)S(1)} %bitcast.29, bf16[256,512]{1,0:T(8,128)(2,1)S(1)} %bitcast.40), custom_call_target="tpu_custom_call" | custom-call | flops 411041792 | bytes 1966080 | tf_op jit(solution)/shard_map/pallas_call | solution.py:36
  28.1 3.2 %collective-permute-done.7.refs_12_ = bf16[32,256]{1,0:T(8,128)(2,1)S(1)} collective-permute-done((bf16[32,256]{1,0:T(8,128)(2,1)S(1)}, bf16[32,256]{1,0:T(8,128)(2,1)S(1)}, u32[]{:S(2)}, u32[]{:S(2)}) %collective-permute-start.7) | collective-permute-done | bytes 16416 | tf_op jit(solution)/shard_map/ppermute | solution.py:17
  31.4 1.0 %shard_map.88 = (f32[4,32,384]{2,1,0:T(8,128)S(1)}, bf16[256,512]{1,0:T(8,128)(2,1)S(1)}, f32[4,32,128]{2,1,0:T(8,128)S(1)}) custom-call(bf16[1568,512]{1,0:T(8,128)(2,1)S(1)} %bitcast.30, bf16[256,512]{1,0:T(8,128)(2,1)S(1)} %bitcast.42, bf16[256,512]{1,0:T(8,128)(2,1)S(1)} %collective-permute-done.3.refs_2_, f32[32,384]{1,0:T(8,128)S(1)} %get-tuple-element.25.refs_3_, ...), custom_call_target="tpu_custom_call" | custom-call | flops 411041792 | bytes 3014656 | tf_op jit(solution)/shard_map/pallas_call | solution.py:36
  32.4 1.2 %collective-permute-done.8.refs_1_ = f32[4,32,128]{2,1,0:T(8,128)S(1)} collective-permute-done((f32[4,32,128]{2,1,0:T(8,128)S(1)}, f32[4,32,128]{2,1,0:T(8,128)S(1)}, u32[]{:S(2)}, u32[]{:S(2)}) %collective-permute-start.8) | collective-permute-done | bytes 65568 | tf_op jit(solution)/shard_map/ppermute | solution.py:17
  33.7 2.4 %collective-permute-start.9 = (bf16[4,32,384]{2,1,0:T(8,128)(2,1)S(1)}, bf16[4,32,384]{2,1,0:T(8,128)(2,1)S(1)}, u32[]{:S(2)}, u32[]{:S(2)}) collective-permute-start(bf16[4,32,384]{2,1,0:T(8,128)(2,1)S(1)} %get-tuple-element.34), channel_id=1, source_target_pairs={{0,24},{8,16},{16,8},{24,0},{1,25},{9,17},{17,9},{25,1},{2,26},{10... | collective-permute-start | bytes 294920 | tf_op jit(solution)/shard_map/ppermute | solution.py:308
  37.7 1.9 %collective-permute-done.9.refs_2_ = bf16[4,32,384]{2,1,0:T(8,128)(2,1)S(1)} collective-permute-done((bf16[4,32,384]{2,1,0:T(8,128)(2,1)S(1)}, bf16[4,32,384]{2,1,0:T(8,128)(2,1)S(1)}, u32[]{:S(2)}, u32[]{:S(2)}) %collective-permute-start.9) | collective-permute-done | bytes 98336 | tf_op jit(solution)/shard_map/ppermute | solution.py:308
  39.6 2.0 %collective-permute-done.10.refs_3_ = bf16[4,32,384]{2,1,0:T(8,128)(2,1)S(1)} collective-permute-done((bf16[4,32,384]{2,1,0:T(8,128)(2,1)S(1)}, bf16[4,32,384]{2,1,0:T(8,128)(2,1)S(1)}, u32[]{:S(2)}, u32[]{:S(2)}) %collective-permute-start.10) | collective-permute-done | bytes 98336 | tf_op jit(solution)/shard_map/ppermute | solution.py:308
  41.6 0.9 %shard_map.90 = (bf16[1568,256]{1,0:T(8,128)(2,1)S(1)}, bf16[512,256]{1,0:T(8,128)(2,1)S(1)}, f32[4,32,384]{2,1,0:T(8,128)S(1)}) custom-call(bf16[512,1568]{1,0:T(8,128)(2,1)S(1)} %shard_map.84.refs_0_, f32[4,32,384]{2,1,0:T(8,128)S(1)} %get-tuple-element.33.refs_1_, bf16[4,32,384]{2,1,0:T(8,128)(2,1)S(1)} %collective-permute-done.9.refs_2_, ...), custom_call_target="tpu_custom_call" | custom-call | flops 411041792 | bytes 3358720 | tf_op jit(solution)/shard_map/pallas_call | solution.py:36
  42.6 0.9 %shard_map.91 = (bf16[1568,256]{1,0:T(8,128)(2,1)S(1)}, f32[512,256]{1,0:T(8,128)S(1)}) custom-call(bf16[512,1568]{1,0:T(8,128)(2,1)S(1)} %shard_map.84.refs_0_, f32[4,32,384]{2,1,0:T(8,128)S(1)} %get-tuple-element.35.refs_1_), custom_call_target="tpu_custom_call" | custom-call | flops 411041792 | bytes 3129344 | tf_op jit(solution)/shard_map/pallas_call | solution.py:36
  43.4 0.9 %shard_map.92 = (bf16[1568,256]{1,0:T(8,128)(2,1)S(1)}, bf16[512,256]{1,0:T(8,128)(2,1)S(1)}) custom-call(bf16[512,1568]{1,0:T(8,128)(2,1)S(1)} %shard_map.84.refs_0_, f32[4,32,384]{2,1,0:T(8,128)S(1)} %get-tuple-element.35.refs_1_), custom_call_target="tpu_custom_call" | custom-call | flops 411041792 | bytes 2867200 | tf_op jit(solution)/shard_map/pallas_call | solution.py:36
  44.4 0.9 %shard_map.93 = (bf16[1568,256]{1,0:T(8,128)(2,1)S(1)}, f32[512,256]{1,0:T(8,128)S(1)}, bf16[512,256]{1,0:T(8,128)(2,1)S(1)}) custom-call(bf16[512,1568]{1,0:T(8,128)(2,1)S(1)} %shard_map.84.refs_0_, f32[4,32,384]{2,1,0:T(8,128)S(1)} %get-tuple-element.35.refs_1_), custom_call_target="tpu_custom_call" | custom-call | flops 411041792 | bytes 3391488 | tf_op jit(solution)/shard_map/pallas_call | solution.py:36
  45.2 1.8 %shard_map.97 = f32[1568,512]{1,0:T(8,128)S(1)} custom-call(bf16[1568,256]{1,0:T(8,128)(2,1)S(1)} %get-tuple-element.41.refs_0_, bf16[1568,256]{1,0:T(8,128)(2,1)S(1)} %get-tuple-element.42.refs_1_, bf16[1568,256]{1,0:T(8,128)(2,1)S(1)} %get-tuple-element.43.refs_2_, bf16[1568,256]{1,0:T(8,128)(2,1)S(1)} %get-tuple-element.44.refs_3_, ...), custom_call_target="tpu_custom_call" | custom-call | flops 1644167168 | bytes 7471104 | tf_op jit(solution)/shard_map/pallas_call | solution.py:36
  47.3 2.1 %collective-permute-start.15 = (bf16[512,256]{1,0:T(8,128)(2,1)S(1)}, bf16[512,256]{1,0:T(8,128)(2,1)S(1)}, u32[]{:S(2)}, u32[]{:S(2)}) collective-permute-start(bf16[512,256]{1,0:T(8,128)(2,1)S(1)} %get-tuple-element.38), channel_id=1, source_target_pairs={{3,2},{0,1},{7,6},{4,5},{11,10},{8,9},{15,14},{12,13},{19,18},{16,... | collective-permute-start | bytes 786440 | tf_op jit(solution)/shard_map/ppermute | solution.py:31
  50.1 1.9 %collective-permute-start.12 = (bf16[512,256]{1,0:T(8,128)(2,1)S(1)}, bf16[512,256]{1,0:T(8,128)(2,1)S(1)}, u32[]{:S(2)}, u32[]{:S(2)}) collective-permute-start(bf16[512,256]{1,0:T(8,128)(2,1)S(1)} %get-tuple-element.37), channel_id=1, source_target_pairs={{0,1},{1,0},{2,3},{3,2},{4,5},{5,4},{6,7},{7,6},{8,9},{9,8},{10,11... | collective-permute-start | bytes 786440 | tf_op jit(solution)/shard_map/ppermute | solution.py:31
  51.9 2.8 %collective-permute-start.14 = (bf16[512,256]{1,0:T(8,128)(2,1)S(1)}, bf16[512,256]{1,0:T(8,128)(2,1)S(1)}, u32[]{:S(2)}, u32[]{:S(2)}) collective-permute-start(bf16[512,256]{1,0:T(8,128)(2,1)S(1)} %get-tuple-element.39), channel_id=1, source_target_pairs={{0,2},{3,1},{4,6},{7,5},{8,10},{11,9},{12,14},{15,13},{16,18},{19,... | collective-permute-start | bytes 786440 | tf_op jit(solution)/shard_map/ppermute | solution.py:31
  54.7 1.4 %collective-permute-done.15.passed_ref = bf16[512,256]{1,0:T(8,128)(2,1)S(1)} collective-permute-done((bf16[512,256]{1,0:T(8,128)(2,1)S(1)}, bf16[512,256]{1,0:T(8,128)(2,1)S(1)}, u32[]{:S(2)}, u32[]{:S(2)}) %collective-permute-start.15) | collective-permute-done | bytes 262176 | tf_op jit(solution)/shard_map/ppermute | solution.py:31
  56.1 1.3 %collective-permute-start.16 = (bf16[512,256]{1,0:T(8,128)(2,1)S(1)}, bf16[512,256]{1,0:T(8,128)(2,1)S(1)}, u32[]{:S(2)}, u32[]{:S(2)}) collective-permute-start(bf16[512,256]{1,0:T(8,128)(2,1)S(1)} %shard_map.95), channel_id=1, source_target_pairs={{1,3},{2,0},{5,7},{6,4},{9,11},{10,8},{13,15},{14,12},{17,19},{18,... | collective-permute-start | bytes 786440 | tf_op jit(solution)/shard_map/ppermute | solution.py:31
  57.4 4.3 %collective-permute-done.12.refs_1_ = bf16[512,256]{1,0:T(8,128)(2,1)S(1)} collective-permute-done((bf16[512,256]{1,0:T(8,128)(2,1)S(1)}, bf16[512,256]{1,0:T(8,128)(2,1)S(1)}, u32[]{:S(2)}, u32[]{:S(2)}) %collective-permute-start.12) | collective-permute-done | bytes 262176 | tf_op jit(solution)/shard_map/ppermute | solution.py:31
  61.7 5.2 %collective-permute-done.14.refs_3_ = bf16[512,256]{1,0:T(8,128)(2,1)S(1)} collective-permute-done((bf16[512,256]{1,0:T(8,128)(2,1)S(1)}, bf16[512,256]{1,0:T(8,128)(2,1)S(1)}, u32[]{:S(2)}, u32[]{:S(2)}) %collective-permute-start.14) | collective-permute-done | bytes 262176 | tf_op jit(solution)/shard_map/ppermute | solution.py:31
  67.1 4.8 %collective-permute-done.16.back_ref = bf16[512,256]{1,0:T(8,128)(2,1)S(1)} collective-permute-done((bf16[512,256]{1,0:T(8,128)(2,1)S(1)}, bf16[512,256]{1,0:T(8,128)(2,1)S(1)}, u32[]{:S(2)}, u32[]{:S(2)}) %collective-permute-start.16) | collective-permute-done | bytes 262176 | tf_op jit(solution)/shard_map/ppermute | solution.py:31
  71.9 0.9 %shard_map.96 = bf16[256,512]{1,0:T(8,128)(2,1)} custom-call(f32[256,512]{1,0:T(8,128)S(1)} %shard_map.94.moved_ref, bf16[512,256]{1,0:T(8,128)(2,1)S(1)} %collective-permute-done.16.back_ref), custom_call_target="tpu_custom_call" | custom-call | bytes 1048576 | tf_op jit(solution)/shard_map/pallas_call | solution.py:36
  73.4 0.9 %copy-done.1 = f32[16,7,7,512]{3,0,2,1:T(8,128)S(1)} copy-done((f32[16,7,7,512]{3,0,2,1:T(8,128)S(1)}, f32[16,7,7,512]{3,0,2,1:T(8,128)}, u32[]{:S(2)}) %copy-start.1) | copy-done | bytes 1605656
  74.8 3.0 %divide_subtract_fusion = (f32[16,7,7,512]{3,0,2,1:T(8,128)}, f32[16,7,7,512]{3,0,2,1:T(8,128)}, f32[16,7,7,512]{3,0,2,1:T(8,128)}) fusion(f32[16,7,7,512]{3,0,2,1:T(8,128)S(1)} %copy-done.1, f32[16,7,7,512]{3,0,2,1:T(8,128)S(1)} %bitcast.44, f32[16,7,7,512]{3,0,2,1:T(8,128)S(1)} %copy-done.2, f32[16,7,7,512]{3,0,2,1:T(8,128)S(1)} %copy-done.3), kind=kLoop, calls=%fused_computation.6 | loop fusion | flops 4816896 | bytes 11239424 | tf_op jit(solution)/shard_map/sub | solution.py:240
  (38 shorter events, 6.2 us)
Async XLA Ops:
  0.6 2.2 %copy-start = (bf16[16,16,512]{2,1,0:T(8,128)(2,1)S(1)}, bf16[16,16,512]{2,1,0:T(8,128)(2,1)}, u32[]{:S(2)}) copy-start(bf16[16,16,512]{2,1,0:T(8,128)(2,1)} %param.5) | copy-start | bytes 786436
  0.6 9.4 %copy-start.4 = (bf16[16,16,128]{2,1,0:T(8,128)(2,1)S(1)}, bf16[16,16,128]{2,1,0:T(8,128)(2,1)}, u32[]{:S(2)}) copy-start(bf16[16,16,128]{2,1,0:T(8,128)(2,1)} %param.6) | copy-start | bytes 196612
  2.2 17.0 %collective-permute-start = (bf16[49,16,512]{2,1,0:T(8,128)(2,1)S(1)}, bf16[49,16,512]{2,1,0:T(8,128)(2,1)}, u32[]{:S(2)}, u32[]{:S(2)}) collective-permute-start(bf16[49,16,512]{2,1,0:T(8,128)(2,1)S(1)} %bitcast.45), channel_id=1, source_target_pairs={{0,4},{4,0},{1,5},{5,1},{2,6},{6,2},{3,7},{7,3},{8,12},{12,8},{9,1... | collective-permute-start | bytes 2408456 | tf_op jit(solution)/shard_map/ppermute | solution.py:17
  2.8 16.5 %collective-permute-start.2 = (bf16[16,16,512]{2,1,0:T(8,128)(2,1)S(1)}, bf16[16,16,512]{2,1,0:T(8,128)(2,1)S(1)}, u32[]{:S(2)}, u32[]{:S(2)}) collective-permute-start(bf16[16,16,512]{2,1,0:T(8,128)(2,1)S(1)} %copy-done), channel_id=1, source_target_pairs={{0,2},{1,3},{2,0},{3,1},{4,6},{5,7},{6,4},{7,5},{8,10},{9,11},{10,... | collective-permute-start | bytes 786440 | tf_op jit(solution)/shard_map/ppermute | solution.py:31
  6.5 24.9 %collective-permute-start.1 = (bf16[16,16,512]{2,1,0:T(8,128)(2,1)S(1)}, bf16[16,16,512]{2,1,0:T(8,128)(2,1)S(1)}, u32[]{:S(2)}, u32[]{:S(2)}) collective-permute-start(bf16[16,16,512]{2,1,0:T(8,128)(2,1)S(1)} %copy-done), channel_id=1, source_target_pairs={{1,2},{2,1},{5,6},{6,5},{9,10},{10,9},{13,14},{14,13},{17,18},{18,... | collective-permute-start | bytes 786440 | tf_op jit(solution)/shard_map/ppermute | solution.py:31
  7.1 16.6 %collective-permute-start.4 = (bf16[16,16,512]{2,1,0:T(8,128)(2,1)S(1)}, bf16[16,16,512]{2,1,0:T(8,128)(2,1)S(1)}, u32[]{:S(2)}, u32[]{:S(2)}) collective-permute-start(bf16[16,16,512]{2,1,0:T(8,128)(2,1)S(1)} %copy-done), channel_id=1, source_target_pairs={{0,1},{1,0},{2,3},{3,2},{4,5},{5,4},{6,7},{7,6},{8,9},{9,8},{10,11... | collective-permute-start | bytes 786440 | tf_op jit(solution)/shard_map/ppermute | solution.py:31
  10.9 17.2 %collective-permute-start.5 = (bf16[32,256]{1,0:T(8,128)(2,1)S(1)}, bf16[32,256]{1,0:T(8,128)(2,1)S(1)}, u32[]{:S(2)}, u32[]{:S(2)}) collective-permute-start(bf16[32,256]{1,0:T(8,128)(2,1)S(1)} %bitcast.52), channel_id=1, source_target_pairs={{0,1},{1,2},{2,3},{3,0},{4,5},{5,6},{6,7},{7,4},{8,9},{9,10},{10,1... | collective-permute-start | bytes 49160 | tf_op jit(solution)/shard_map/ppermute | solution.py:17
  19.3 8.8 %collective-permute-start.6 = (bf16[32,256]{1,0:T(8,128)(2,1)S(1)}, bf16[32,256]{1,0:T(8,128)(2,1)S(1)}, u32[]{:S(2)}, u32[]{:S(2)}) collective-permute-start(bf16[32,256]{1,0:T(8,128)(2,1)S(1)} %bitcast.51), channel_id=1, source_target_pairs={{0,2},{1,3},{2,0},{3,1},{4,6},{5,7},{6,4},{7,5},{8,10},{9,11},{10,... | collective-permute-start | bytes 49160 | tf_op jit(solution)/shard_map/ppermute | solution.py:17
  19.3 12.1 %collective-permute-start.3 = (bf16[256,512]{1,0:T(8,128)(2,1)S(1)}, bf16[256,512]{1,0:T(8,128)(2,1)S(1)}, u32[]{:S(2)}, u32[]{:S(2)}) collective-permute-start(bf16[256,512]{1,0:T(8,128)(2,1)S(1)} %bitcast.37), channel_id=1, source_target_pairs={{2,3},{1,0},{6,7},{5,4},{10,11},{9,8},{14,15},{13,12},{18,19},{17,... | collective-permute-start | bytes 786440 | tf_op jit(solution)/shard_map/ppermute | solution.py:31
  23.8 7.6 %collective-permute-start.7 = (bf16[32,256]{1,0:T(8,128)(2,1)S(1)}, bf16[32,256]{1,0:T(8,128)(2,1)S(1)}, u32[]{:S(2)}, u32[]{:S(2)}) collective-permute-start(bf16[32,256]{1,0:T(8,128)(2,1)S(1)} %bitcast.50), channel_id=1, source_target_pairs={{0,3},{1,0},{2,1},{3,2},{4,7},{5,4},{6,5},{7,6},{8,11},{9,8},{10,9... | collective-permute-start | bytes 49160 | tf_op jit(solution)/shard_map/ppermute | solution.py:17
  32.3 1.3 %collective-permute-start.8 = (f32[4,32,128]{2,1,0:T(8,128)S(1)}, f32[4,32,128]{2,1,0:T(8,128)S(1)}, u32[]{:S(2)}, u32[]{:S(2)}) collective-permute-start(f32[4,32,128]{2,1,0:T(8,128)S(1)} %get-tuple-element.32), channel_id=1, source_target_pairs={{0,4},{4,0},{1,5},{5,1},{2,6},{6,2},{3,7},{7,3},{8,12},{12,8},{9,1... | collective-permute-start | bytes 196616 | tf_op jit(solution)/shard_map/ppermute | solution.py:17
  33.7 5.9 %collective-permute-start.9 = (bf16[4,32,384]{2,1,0:T(8,128)(2,1)S(1)}, bf16[4,32,384]{2,1,0:T(8,128)(2,1)S(1)}, u32[]{:S(2)}, u32[]{:S(2)}) collective-permute-start(bf16[4,32,384]{2,1,0:T(8,128)(2,1)S(1)} %get-tuple-element.34), channel_id=1, source_target_pairs={{0,24},{8,16},{16,8},{24,0},{1,25},{9,17},{17,9},{25,1},{2,26},{10... | collective-permute-start | bytes 294920 | tf_op jit(solution)/shard_map/ppermute | solution.py:308
  36.1 5.5 %collective-permute-start.10 = (bf16[4,32,384]{2,1,0:T(8,128)(2,1)S(1)}, bf16[4,32,384]{2,1,0:T(8,128)(2,1)S(1)}, u32[]{:S(2)}, u32[]{:S(2)}) collective-permute-start(bf16[4,32,384]{2,1,0:T(8,128)(2,1)S(1)} %get-tuple-element.34), channel_id=1, source_target_pairs={{0,16},{8,24},{16,0},{24,8},{1,17},{9,25},{17,1},{25,9},{2,18},{10... | collective-permute-start | bytes 294920 | tf_op jit(solution)/shard_map/ppermute | solution.py:308
  36.6 5.0 %collective-permute-start.11 = (bf16[4,32,384]{2,1,0:T(8,128)(2,1)S(1)}, bf16[4,32,384]{2,1,0:T(8,128)(2,1)S(1)}, u32[]{:S(2)}, u32[]{:S(2)}) collective-permute-start(bf16[4,32,384]{2,1,0:T(8,128)(2,1)S(1)} %get-tuple-element.34), channel_id=1, source_target_pairs={{0,8},{8,0},{16,24},{24,16},{1,9},{9,1},{17,25},{25,17},{2,10},{10... | collective-permute-start | bytes 294920 | tf_op jit(solution)/shard_map/ppermute | solution.py:308
  47.2 25.5 %collective-permute-start.17 = (bf16[49,16,512]{2,1,0:T(8,128)(2,1)S(1)}, bf16[49,16,512]{2,1,0:T(8,128)(2,1)S(1)}, u32[]{:S(2)}, u32[]{:S(2)}) collective-permute-start(bf16[49,16,512]{2,1,0:T(8,128)(2,1)S(1)} %fusion.2), channel_id=1, source_target_pairs={{0,4},{4,0},{1,5},{5,1},{2,6},{6,2},{3,7},{7,3},{8,12},{12,8},{9,1... | collective-permute-start | bytes 2408456 | tf_op jit(solution)/shard_map/ppermute | solution.py:17
  47.3 8.8 %collective-permute-start.15 = (bf16[512,256]{1,0:T(8,128)(2,1)S(1)}, bf16[512,256]{1,0:T(8,128)(2,1)S(1)}, u32[]{:S(2)}, u32[]{:S(2)}) collective-permute-start(bf16[512,256]{1,0:T(8,128)(2,1)S(1)} %get-tuple-element.38), channel_id=1, source_target_pairs={{3,2},{0,1},{7,6},{4,5},{11,10},{8,9},{15,14},{12,13},{19,18},{16,... | collective-permute-start | bytes 786440 | tf_op jit(solution)/shard_map/ppermute | solution.py:31
  49.4 12.3 %collective-permute-start.13 = (bf16[512,256]{1,0:T(8,128)(2,1)S(1)}, bf16[512,256]{1,0:T(8,128)(2,1)S(1)}, u32[]{:S(2)}, u32[]{:S(2)}) collective-permute-start(bf16[512,256]{1,0:T(8,128)(2,1)S(1)} %get-tuple-element.38), channel_id=1, source_target_pairs={{1,2},{2,1},{5,6},{6,5},{9,10},{10,9},{13,14},{14,13},{17,18},{18,... | collective-permute-start | bytes 786440 | tf_op jit(solution)/shard_map/ppermute | solution.py:31
  50.1 11.6 %collective-permute-start.12 = (bf16[512,256]{1,0:T(8,128)(2,1)S(1)}, bf16[512,256]{1,0:T(8,128)(2,1)S(1)}, u32[]{:S(2)}, u32[]{:S(2)}) collective-permute-start(bf16[512,256]{1,0:T(8,128)(2,1)S(1)} %get-tuple-element.37), channel_id=1, source_target_pairs={{0,1},{1,0},{2,3},{3,2},{4,5},{5,4},{6,7},{7,6},{8,9},{9,8},{10,11... | collective-permute-start | bytes 786440 | tf_op jit(solution)/shard_map/ppermute | solution.py:31
  51.9 14.9 %collective-permute-start.14 = (bf16[512,256]{1,0:T(8,128)(2,1)S(1)}, bf16[512,256]{1,0:T(8,128)(2,1)S(1)}, u32[]{:S(2)}, u32[]{:S(2)}) collective-permute-start(bf16[512,256]{1,0:T(8,128)(2,1)S(1)} %get-tuple-element.39), channel_id=1, source_target_pairs={{0,2},{3,1},{4,6},{7,5},{8,10},{11,9},{12,14},{15,13},{16,18},{19,... | collective-permute-start | bytes 786440 | tf_op jit(solution)/shard_map/ppermute | solution.py:31
  56.1 15.8 %collective-permute-start.16 = (bf16[512,256]{1,0:T(8,128)(2,1)S(1)}, bf16[512,256]{1,0:T(8,128)(2,1)S(1)}, u32[]{:S(2)}, u32[]{:S(2)}) collective-permute-start(bf16[512,256]{1,0:T(8,128)(2,1)S(1)} %shard_map.95), channel_id=1, source_target_pairs={{1,3},{2,0},{5,7},{6,4},{9,11},{10,8},{13,15},{14,12},{17,19},{18,... | collective-permute-start | bytes 786440 | tf_op jit(solution)/shard_map/ppermute | solution.py:31
  71.9 1.5 %copy-start.3 = (f32[16,7,7,512]{3,0,2,1:T(8,128)S(1)}, f32[16,7,7,512]{3,0,2,1:T(8,128)}, u32[]{:S(2)}) copy-start(f32[16,7,7,512]{3,0,2,1:T(8,128)} %param.9) | copy-start | bytes 4816900
  72.7 1.5 %copy-start.1 = (f32[16,7,7,512]{3,0,2,1:T(8,128)S(1)}, f32[16,7,7,512]{3,0,2,1:T(8,128)}, u32[]{:S(2)}) copy-start(f32[16,7,7,512]{3,0,2,1:T(8,128)} %param.7) | copy-start | bytes 4816900
  72.7 2.0 %copy-start.2 = (f32[16,7,7,512]{3,0,2,1:T(8,128)S(1)}, f32[16,7,7,512]{3,0,2,1:T(8,128)}, u32[]{:S(2)}) copy-start(f32[16,7,7,512]{3,0,2,1:T(8,128)} %param.8) | copy-start | bytes 4816900

commit v7 on v6

--- a/solution.py
+++ b/solution.py
@@ -99,10 +99,17 @@
     return jnp.where(lax.rem(lax.axis_index("col"), 2) == 1, 1, lax.axis_size("col") - 1)
 
 
-def late_body(taps, bands, ext, cols, pixels, share, *refs):
+def edges_of(value, pixels, reach, cols, places):
+    lane = lax.broadcasted_iota(jnp.int32, (1, 128), 1)
+    up = jnp.where(lane < 2 * reach * cols, value[:, :128], 0.0)
+    down = value[:, pixels : pixels + 128]
+    return [jnp.where(lax.axis_index("row") == 0, down, up)] if places == 1 else [up, down]
+
+
+def late_body(taps, bands, ext, cols, pixels, *refs):
     filters_ref, swapped_ref, passed_ref = refs[:3]
-    mains, spills, images = refs[3:6], refs[6:9], refs[9:13]
-    out_ref, tile_ref, *edge_refs, main_of, spill_of, y_ref = refs[13:]
+    mains, spills = refs[3:6], refs[6:9]
+    out_ref, tile_ref, *edge_refs, main_of, spill_of, y_ref = refs[9:]
     count, reach = 4, taps // 2
     middle = (lax.axis_index("col") == 1) | (lax.axis_index("col") == 2)
     tile_ref[...] = jnp.where(middle, swapped_ref[...], passed_ref[...])
@@ -113,28 +120,28 @@
         spill_of[s] = spill[...]
     main_of[count - near], spill_of[count - near] = tile_parts(filters_ref[...], tile_ref[...], y_ref, taps, bands, ext, cols)
     column = column_of(ext, cols)
-    lane = lax.broadcasted_iota(jnp.int32, (1, 128), 1)
     for s in range(count):
         left, right = tile_flags(s)
         from_left = jnp.where((column < reach) & left, spill_of[(s + 1) % count], 0.0)
         from_right = jnp.where((column >= cols - reach) & right, spill_of[(s - 1) % count], 0.0)
-        picture = images[s][...].astype(jnp.float32) * share
-        pad = jnp.zeros((bands, ext - picture.shape[1]), jnp.float32)
-        picture = roll(jnp.concatenate([picture, pad], axis=1), reach * cols)
-        value = main_of[s] + from_left + from_right - picture
+        value = main_of[s] + from_left + from_right
         out_ref[s] = value
-        up = jnp.where(lane < 2 * reach * cols, value[:, :128], 0.0)
-        down = value[:, pixels : pixels + 128]
-        if len(edge_refs) == 1:
-            edges = [jnp.where(lax.axis_index("row") == 0, down, up)]
-        else:
-            edges = [up, down]
-        for ref, edge in zip(edge_refs, edges):
+        for ref, edge in zip(edge_refs, edges_of(value, pixels, reach, cols, len(edge_refs))):
             ref[s] = edge
 
 
-def join_body(count, pixels, turn, *refs):
-    part_ref, *edge_refs, out_ref, send_ref = refs
+def frame_body(bands, ext, cols, pixels, reach, *refs):
+    images, out_ref, edge_refs = refs[:4], refs[4], refs[5:]
+    for s, image in enumerate(images):
+        pad = jnp.zeros((bands, ext - pixels), jnp.float32)
+        value = roll(jnp.concatenate([image[...].astype(jnp.float32), pad], axis=1), reach * cols)
+        out_ref[s] = value
+        for ref, edge in zip(edge_refs, edges_of(value, pixels, reach, cols, len(edge_refs))):
+            ref[s] = edge
+
+
+def join_body(count, pixels, turn, edges, *refs):
+    part_ref, edge_refs, out_ref, send_refs = refs[0], refs[1 : 1 + edges], refs[1 + edges], refs[2 + edges :]
     bands = part_ref.shape[1]
 
     def turned(x, step):
@@ -151,11 +158,12 @@
         parts = [own[:, :128] + above, own[:, 128:pixels], own[:, pixels : pixels + 128] + below, own[:, pixels + 128 :]]
         value = jnp.concatenate([part for part in parts if part.shape[1]], axis=1)
         out_ref[s] = value
-        send_ref[s] = value.astype(jnp.bfloat16)
+        for send_ref in send_refs:
+            send_ref[s] = value.astype(jnp.bfloat16)
 
 
 def resid_body(ext, rows, cols, reach, peers, *refs):
-    own_ref, others, out_ref = refs[0], refs[1 : 1 + peers], refs[1 + peers]
+    image_ref, own_ref, others, out_ref = refs[0], refs[1], refs[2 : 2 + peers], refs[2 + peers]
     line = lax.broadcasted_iota(jnp.int32, (1, ext), 1) // cols
     place, places = lax.axis_index("row"), lax.axis_size("row")
     real = ((line >= reach) | (place > 0)) & ((line < rows + reach) | (place < places - 1)) & (line < rows + 2 * reach)
@@ -163,7 +171,7 @@
         value = own_ref[s]
         for other in others:
             value = value + other[s].astype(jnp.float32)
-        out_ref[s] = jnp.where(real, value, 0.0).astype(jnp.bfloat16).astype(jnp.float32)
+        out_ref[s] = jnp.where(real, value - image_ref[s], 0.0).astype(jnp.bfloat16).astype(jnp.float32)
 
 
 def windows_of(taps, bands, ext, rows, cols, s, resid_ref, windows_ref):
@@ -287,21 +295,26 @@
     edge = struct((count, bands, 128), jnp.float32)
     part_shape = (count, bands, ext)
     part, far, *edges = call(
-        functools.partial(late_body, taps, bands, ext, cols, pixels, 1.0 / peers),
+        functools.partial(late_body, taps, bands, ext, cols, pixels),
         [struct(part_shape, jnp.float32), struct(tile.shape, tile.dtype)] + [edge] * (1 if groups == 2 else 2),
-        [filters, swapped, passed, *mains, *spills, *images],
+        [filters, swapped, passed, *mains, *spills],
         tile_flops,
         [pltpu.VMEM(part_shape, jnp.float32)] * 2 + y_scratch,
     )
-    if groups == 2:
-        edges = [shifted(edges[0], "row", 1)]
-    else:
-        edges = [moved_on(edges[0], "row", -1), moved_on(edges[1], "row", 1)]
-    part, send = call(
-        functools.partial(join_body, count, pixels, own_bands),
-        [struct(part_shape, jnp.float32), struct(part_shape, jnp.bfloat16)],
-        [part, *edges],
-    )
+    edges_out = 1 if groups == 2 else 2
+
+    def whole_rows(part, edges, sends):
+        if groups == 2:
+            edges = [shifted(edges[0], "row", 1)]
+        else:
+            edges = [moved_on(edges[0], "row", -1), moved_on(edges[1], "row", 1)]
+        return call(
+            functools.partial(join_body, count, pixels, own_bands, edges_out),
+            [struct(part_shape, jnp.float32)] + [struct(part_shape, jnp.bfloat16)] * sends,
+            [part, *edges],
+        )
+
+    part, send = whole_rows(part, edges, 1)
     if peers <= 4:
         others = []
         for m in range(peers - 1, 0, -1):
@@ -309,6 +322,13 @@
     else:
         others = [(lax.psum(send, "atom").astype(jnp.float32) - send.astype(jnp.float32)).astype(jnp.bfloat16)]
 
+    picture, *edges = call(
+        functools.partial(frame_body, bands, ext, cols, pixels, reach),
+        [struct(part_shape, jnp.float32)] + [edge] * edges_out,
+        images,
+    )
+    (picture,) = whole_rows(picture, edges, 0)
+
     def back_of(which, dtypes, *args, peers=None):
         outs = [struct((taps * taps * bands, pixels), jnp.bfloat16)] + [struct((atoms, pixels), dtype) for dtype in dtypes]
         if peers is not None:
@@ -316,7 +336,7 @@
         body = functools.partial(back_body, taps, bands, ext, rows, cols, which, peers)
         return call(body, outs, [turned, *args], tile_flops)
 
-    far_windows, far_back, resid = back_of("far", [jnp.bfloat16], part, *others, peers=len(others))
+    far_windows, far_back, resid = back_of("far", [jnp.bfloat16], picture, part, *others, peers=len(others))
     home_pass = along(far_back, [(3, 2), (0, 1)])
     home_swap = along(far_back, INNER)
     two_windows, two_back, two_send = back_of("two", [jnp.float32, jnp.bfloat16], resid)

time: 78 us -> 81 us (1.038)
  waiting for transfers between devices: 32.2 us -> 34 us
  starting transfers between devices: 24.9 us -> 25.9 us
    ppermute x9, waiting for transfers between devices: 23.8 us -> 28.5 us  [along(): return lax.ppermute(x, 'col', pairs)]
    ppermute x3, waiting for transfers between devices: 3.88 us -> 0.01 us  [iteration(): lax.ppermute(send, 'atom', [(i, i ^ m) for i in range(peers)])]
    ppermute x6 -> x7, waiting for transfers between devices: 4.5 us -> 5.54 us  [shifted(): lax.ppermute(x, axis, [(i, (i + step) % count) for i in range(count)])]
    ppermute x6 -> x7, starting transfers between devices: 4.22 us -> 4.74 us  [shifted(): lax.ppermute(x, axis, [(i, (i + step) % count) for i in range(count)])]
    pallas_call x14 -> x16, Pallas kernels: 10.8 us -> 10.9 us  [call(): pl.pallas_call(body, out_shape=outs, in_specs=[pl.BlockSpec(memory_space=...]
  transfers between devices with their start and end apart: 18 -> 19, of which waited for: 9 -> 10; matrix products, arithmetic and copies ran while one was open for 3% -> 3% of each run, Pallas kernels for 6% -> 6%
where the time goes in v7:
time: 81 us; the launch traced here: 80.7 us
  waiting for transfers between devices  34 us (42%)
  starting transfers between devices  25.9 us (32%)
  Pallas kernels  10.9 us (13%)
  other arithmetic  6.12 us (8%)
  local copies, waits for them, and re-layouts  2.72 us (3%)
  between operations  1 us (1%)
    ppermute x9, waiting for transfers between devices, along(): return lax.ppermute(x, 'col', pairs)  28.5 us
    ppermute x9, starting transfers between devices, along(): return lax.ppermute(x, 'col', pairs)  17.6 us
    pallas_call x16, Pallas kernels, call(): pl.pallas_call(body, out_shape=outs, in_specs=[pl.BlockSpec(memory_space=...  10.9 us
    ppermute x7, waiting for transfers between devices, shifted(): lax.ppermute(x, axis, [(i, (i + step) % count) for i in range(count)])  5.54 us
    ppermute x7, starting transfers between devices, shifted(): lax.ppermute(x, axis, [(i, (i + step) % count) for i in range(count)])  4.74 us
    ppermute x3, starting transfers between devices, iteration(): lax.ppermute(send, 'atom', [(i, i ^ m) for i in range(peers)])  3.55 us
    sub x1, other arithmetic, adam_update(): master - 0.05 * (new_moment / first_fix) / (jnp.sqrt(new_second / second_...  2.97 us
    unnamed x12, local copies, waits for them, and re-layouts  2.05 us
  transfers between devices with their start and end apart: 19, of which 10 were waited for; matrix products, arithmetic and copies ran while one was open for 3% of the time, Pallas kernels for 6%

profile of v7, /device:TPU:0, one launch (start us, length us, event | category | flops | bytes accessed | tf_op | source)
XLA Modules:
  0.0 80.7 jit_solution(1008495824172709192)
XLA Ops:
  0.7 1.6 %convert_element_type.16 = bf16[16,7,7,512]{3,0,2,1:T(8,128)(2,1)S(1)} convert(f32[16,7,7,512]{3,0,2,1:T(8,128)} %param.7) | non-fusion elementwise | flops 401408 | bytes 2408448 | tf_op jit(solution)/shard_map/convert_element_type | solution.py:270
  2.8 3.7 %collective-permute-start.6 = (bf16[16,16,512]{2,1,0:T(8,128)(2,1)S(1)}, bf16[16,16,512]{2,1,0:T(8,128)(2,1)S(1)}, u32[]{:S(2)}, u32[]{:S(2)}) collective-permute-start(bf16[16,16,512]{2,1,0:T(8,128)(2,1)S(1)} %copy-done), channel_id=1, source_target_pairs={{0,2},{1,3},{2,0},{3,1},{4,6},{5,7},{6,4},{7,5},{8,10},{9,11},{10,... | collective-permute-start | bytes 786440 | tf_op jit(solution)/shard_map/ppermute | solution.py:31
  7.1 2.9 %collective-permute-start.8 = (bf16[16,16,512]{2,1,0:T(8,128)(2,1)S(1)}, bf16[16,16,512]{2,1,0:T(8,128)(2,1)S(1)}, u32[]{:S(2)}, u32[]{:S(2)}) collective-permute-start(bf16[16,16,512]{2,1,0:T(8,128)(2,1)S(1)} %copy-done), channel_id=1, source_target_pairs={{0,1},{1,0},{2,3},{3,2},{4,5},{5,4},{6,7},{7,6},{8,9},{9,8},{10,11... | collective-permute-start | bytes 786440 | tf_op jit(solution)/shard_map/ppermute | solution.py:31
  10.9 8.3 %collective-permute-done.6 = bf16[16,16,512]{2,1,0:T(8,128)(2,1)S(1)} collective-permute-done((bf16[16,16,512]{2,1,0:T(8,128)(2,1)S(1)}, bf16[16,16,512]{2,1,0:T(8,128)(2,1)S(1)}, u32[]{:S(2)}, u32[]{:S(2)}) %collective-permute-start.6) | collective-permute-done | bytes 262176 | tf_op jit(solution)/shard_map/ppermute | solution.py:31
  19.3 1.3 %collective-permute-start.7 = (bf16[256,512]{1,0:T(8,128)(2,1)S(1)}, bf16[256,512]{1,0:T(8,128)(2,1)S(1)}, u32[]{:S(2)}, u32[]{:S(2)}) collective-permute-start(bf16[256,512]{1,0:T(8,128)(2,1)S(1)} %bitcast.37), channel_id=1, source_target_pairs={{2,3},{1,0},{6,7},{5,4},{10,11},{9,8},{14,15},{13,12},{18,19},{17,... | collective-permute-start | bytes 786440 | tf_op jit(solution)/shard_map/ppermute | solution.py:31
  20.6 1.3 %pad_maximum_fusion = bf16[49,32,512]{2,1,0:T(8,128)(2,1)S(1)} fusion(bf16[49,16,512]{2,1,0:T(8,128)(2,1)} %collective-permute-done, bf16[49,16,512]{2,1,0:T(8,128)(2,1)S(1)} %bitcast.46), kind=kLoop, calls=%fused_computation.5 | loop fusion | flops 3211264 | bytes 3211264 | tf_op jit(solution)/shard_map/concatenate | solution.py:274
  21.9 0.9 %shard_map.88 = (f32[32,384]{1,0:T(8,128)S(1)}, f32[32,384]{1,0:T(8,128)S(1)}) custom-call(bf16[1568,512]{1,0:T(8,128)(2,1)S(1)} %bitcast.27, bf16[256,512]{1,0:T(8,128)(2,1)S(1)} %bitcast.38), custom_call_target="tpu_custom_call" | custom-call | flops 411041792 | bytes 1966080 | tf_op jit(solution)/shard_map/pallas_call | solution.py:36
  22.8 0.9 %shard_map.87 = (f32[32,384]{1,0:T(8,128)S(1)}, f32[32,384]{1,0:T(8,128)S(1)}) custom-call(bf16[1568,512]{1,0:T(8,128)(2,1)S(1)} %bitcast.28, bf16[256,512]{1,0:T(8,128)(2,1)S(1)} %bitcast.34), custom_call_target="tpu_custom_call" | custom-call | flops 411041792 | bytes 1966080 | tf_op jit(solution)/shard_map/pallas_call | solution.py:36
  23.8 0.9 %shard_map.89 = (f32[32,384]{1,0:T(8,128)S(1)}, f32[32,384]{1,0:T(8,128)S(1)}) custom-call(bf16[1568,512]{1,0:T(8,128)(2,1)S(1)} %bitcast.29, bf16[256,512]{1,0:T(8,128)(2,1)S(1)} %bitcast.40), custom_call_target="tpu_custom_call" | custom-call | flops 411041792 | bytes 1966080 | tf_op jit(solution)/shard_map/pallas_call | solution.py:36
  24.7 4.3 %collective-permute-done.7.refs_2_ = bf16[256,512]{1,0:T(8,128)(2,1)S(1)} collective-permute-done((bf16[256,512]{1,0:T(8,128)(2,1)S(1)}, bf16[256,512]{1,0:T(8,128)(2,1)S(1)}, u32[]{:S(2)}, u32[]{:S(2)}) %collective-permute-start.7) | collective-permute-done | bytes 262176 | tf_op jit(solution)/shard_map/ppermute | solution.py:31
  29.0 1.0 %shard_map.90 = (f32[4,32,384]{2,1,0:T(8,128)S(1)}, bf16[256,512]{1,0:T(8,128)(2,1)S(1)}, f32[4,32,128]{2,1,0:T(8,128)S(1)}) custom-call(bf16[1568,512]{1,0:T(8,128)(2,1)S(1)} %bitcast.30, bf16[256,512]{1,0:T(8,128)(2,1)S(1)} %bitcast.42, bf16[256,512]{1,0:T(8,128)(2,1)S(1)} %collective-permute-done.7.refs_2_, f32[32,384]{1,0:T(8,128)S(1)} %get-tuple-element.29.refs_3_, ...), custom_call_target="tpu_custom_call" | custom-call | flops 411041792 | bytes 2949120 | tf_op jit(solution)/shard_map/pallas_call | solution.py:36
  30.1 1.1 %collective-permute-done.9.refs_1_ = f32[4,32,128]{2,1,0:T(8,128)S(1)} collective-permute-done((f32[4,32,128]{2,1,0:T(8,128)S(1)}, f32[4,32,128]{2,1,0:T(8,128)S(1)}, u32[]{:S(2)}, u32[]{:S(2)}) %collective-permute-start.9) | collective-permute-done | bytes 65568 | tf_op jit(solution)/shard_map/ppermute | solution.py:17
  31.3 2.3 %collective-permute-start.10 = (bf16[4,32,384]{2,1,0:T(8,128)(2,1)S(1)}, bf16[4,32,384]{2,1,0:T(8,128)(2,1)S(1)}, u32[]{:S(2)}, u32[]{:S(2)}) collective-permute-start(bf16[4,32,384]{2,1,0:T(8,128)(2,1)S(1)} %get-tuple-element.38), channel_id=1, source_target_pairs={{0,24},{8,16},{16,8},{24,0},{1,25},{9,17},{17,9},{25,1},{2,26},{10... | collective-permute-start | bytes 294920 | tf_op jit(solution)/shard_map/ppermute | solution.py:321
  34.8 3.2 %collective-permute-start.2 = (bf16[32,256]{1,0:T(8,128)(2,1)S(1)}, bf16[32,256]{1,0:T(8,128)(2,1)S(1)}, u32[]{:S(2)}, u32[]{:S(2)}) collective-permute-start(bf16[32,256]{1,0:T(8,128)(2,1)S(1)} %bitcast.51), channel_id=1, source_target_pairs={{0,2},{1,3},{2,0},{3,1},{4,6},{5,7},{6,4},{7,5},{8,10},{9,11},{10,... | collective-permute-start | bytes 49160 | tf_op jit(solution)/shard_map/ppermute | solution.py:17
  38.6 1.1 %collective-permute-done.2.refs_2_ = bf16[32,256]{1,0:T(8,128)(2,1)S(1)} collective-permute-done((bf16[32,256]{1,0:T(8,128)(2,1)S(1)}, bf16[32,256]{1,0:T(8,128)(2,1)S(1)}, u32[]{:S(2)}, u32[]{:S(2)}) %collective-permute-start.2) | collective-permute-done | bytes 16416 | tf_op jit(solution)/shard_map/ppermute | solution.py:17
  39.7 2.0 %collective-permute-done.3.refs_3_ = bf16[32,256]{1,0:T(8,128)(2,1)S(1)} collective-permute-done((bf16[32,256]{1,0:T(8,128)(2,1)S(1)}, bf16[32,256]{1,0:T(8,128)(2,1)S(1)}, u32[]{:S(2)}, u32[]{:S(2)}) %collective-permute-start.3) | collective-permute-done | bytes 16416 | tf_op jit(solution)/shard_map/ppermute | solution.py:17
  41.9 1.2 %collective-permute-done.4.refs_1_ = f32[4,32,128]{2,1,0:T(8,128)S(1)} collective-permute-done((f32[4,32,128]{2,1,0:T(8,128)S(1)}, f32[4,32,128]{2,1,0:T(8,128)S(1)}, u32[]{:S(2)}, u32[]{:S(2)}) %collective-permute-start.4) | collective-permute-done | bytes 65568 | tf_op jit(solution)/shard_map/ppermute | solution.py:17
  43.7 0.9 %shard_map.92 = (bf16[1568,256]{1,0:T(8,128)(2,1)S(1)}, bf16[512,256]{1,0:T(8,128)(2,1)S(1)}, f32[4,32,384]{2,1,0:T(8,128)S(1)}) custom-call(bf16[512,1568]{1,0:T(8,128)(2,1)S(1)} %shard_map.84.refs_0_, f32[4,32,384]{2,1,0:T(8,128)S(1)} %shard_map.86.refs_1_, f32[4,32,384]{2,1,0:T(8,128)S(1)} %get-tuple-element.37.refs_2_, ...), custom_call_target="tpu_custom_call" | custom-call | flops 411041792 | bytes 3555328 | tf_op jit(solution)/shard_map/pallas_call | solution.py:36
  44.7 0.9 %shard_map.93 = (bf16[1568,256]{1,0:T(8,128)(2,1)S(1)}, f32[512,256]{1,0:T(8,128)S(1)}) custom-call(bf16[512,1568]{1,0:T(8,128)(2,1)S(1)} %shard_map.84.refs_0_, f32[4,32,384]{2,1,0:T(8,128)S(1)} %get-tuple-element.39.refs_1_), custom_call_target="tpu_custom_call" | custom-call | flops 411041792 | bytes 3129344 | tf_op jit(solution)/shard_map/pallas_call | solution.py:36
  45.6 0.9 %shard_map.94 = (bf16[1568,256]{1,0:T(8,128)(2,1)S(1)}, bf16[512,256]{1,0:T(8,128)(2,1)S(1)}) custom-call(bf16[512,1568]{1,0:T(8,128)(2,1)S(1)} %shard_map.84.refs_0_, f32[4,32,384]{2,1,0:T(8,128)S(1)} %get-tuple-element.39.refs_1_), custom_call_target="tpu_custom_call" | custom-call | flops 411041792 | bytes 2867200 | tf_op jit(solution)/shard_map/pallas_call | solution.py:36
  46.5 0.9 %shard_map.95 = (bf16[1568,256]{1,0:T(8,128)(2,1)S(1)}, f32[512,256]{1,0:T(8,128)S(1)}, bf16[512,256]{1,0:T(8,128)(2,1)S(1)}) custom-call(bf16[512,1568]{1,0:T(8,128)(2,1)S(1)} %shard_map.84.refs_0_, f32[4,32,384]{2,1,0:T(8,128)S(1)} %get-tuple-element.39.refs_1_), custom_call_target="tpu_custom_call" | custom-call | flops 411041792 | bytes 3391488 | tf_op jit(solution)/shard_map/pallas_call | solution.py:36
  47.4 1.8 %shard_map.99 = f32[1568,512]{1,0:T(8,128)S(1)} custom-call(bf16[1568,256]{1,0:T(8,128)(2,1)S(1)} %get-tuple-element.45.refs_0_, bf16[1568,256]{1,0:T(8,128)(2,1)S(1)} %get-tuple-element.46.refs_1_, bf16[1568,256]{1,0:T(8,128)(2,1)S(1)} %get-tuple-element.47.refs_2_, bf16[1568,256]{1,0:T(8,128)(2,1)S(1)} %get-tuple-element.48.refs_3_, ...), custom_call_target="tpu_custom_call" | custom-call | flops 1644167168 | bytes 7471104 | tf_op jit(solution)/shard_map/pallas_call | solution.py:36
  49.5 3.1 %collective-permute-start.16 = (bf16[512,256]{1,0:T(8,128)(2,1)S(1)}, bf16[512,256]{1,0:T(8,128)(2,1)S(1)}, u32[]{:S(2)}, u32[]{:S(2)}) collective-permute-start(bf16[512,256]{1,0:T(8,128)(2,1)S(1)} %get-tuple-element.42), channel_id=1, source_target_pairs={{3,2},{0,1},{7,6},{4,5},{11,10},{8,9},{15,14},{12,13},{19,18},{16,... | collective-permute-start | bytes 786440 | tf_op jit(solution)/shard_map/ppermute | solution.py:31
  53.3 1.0 %collective-permute-start.13 = (bf16[512,256]{1,0:T(8,128)(2,1)S(1)}, bf16[512,256]{1,0:T(8,128)(2,1)S(1)}, u32[]{:S(2)}, u32[]{:S(2)}) collective-permute-start(bf16[512,256]{1,0:T(8,128)(2,1)S(1)} %get-tuple-element.41), channel_id=1, source_target_pairs={{0,1},{1,0},{2,3},{3,2},{4,5},{5,4},{6,7},{7,6},{8,9},{9,8},{10,11... | collective-permute-start | bytes 786440 | tf_op jit(solution)/shard_map/ppermute | solution.py:31
  54.3 3.1 %collective-permute-start.15 = (bf16[512,256]{1,0:T(8,128)(2,1)S(1)}, bf16[512,256]{1,0:T(8,128)(2,1)S(1)}, u32[]{:S(2)}, u32[]{:S(2)}) collective-permute-start(bf16[512,256]{1,0:T(8,128)(2,1)S(1)} %get-tuple-element.43), channel_id=1, source_target_pairs={{0,2},{3,1},{4,6},{7,5},{8,10},{11,9},{12,14},{15,13},{16,18},{19,... | collective-permute-start | bytes 786440 | tf_op jit(solution)/shard_map/ppermute | solution.py:31
  57.4 1.9 %collective-permute-done.16.passed_ref = bf16[512,256]{1,0:T(8,128)(2,1)S(1)} collective-permute-done((bf16[512,256]{1,0:T(8,128)(2,1)S(1)}, bf16[512,256]{1,0:T(8,128)(2,1)S(1)}, u32[]{:S(2)}, u32[]{:S(2)}) %collective-permute-start.16) | collective-permute-done | bytes 262176 | tf_op jit(solution)/shard_map/ppermute | solution.py:31
  59.3 1.3 %collective-permute-start.17 = (bf16[512,256]{1,0:T(8,128)(2,1)S(1)}, bf16[512,256]{1,0:T(8,128)(2,1)S(1)}, u32[]{:S(2)}, u32[]{:S(2)}) collective-permute-start(bf16[512,256]{1,0:T(8,128)(2,1)S(1)} %shard_map.97), channel_id=1, source_target_pairs={{1,3},{2,0},{5,7},{6,4},{9,11},{10,8},{13,15},{14,12},{17,19},{18,... | collective-permute-start | bytes 786440 | tf_op jit(solution)/shard_map/ppermute | solution.py:31
  60.6 4.3 %collective-permute-done.13.refs_1_ = bf16[512,256]{1,0:T(8,128)(2,1)S(1)} collective-permute-done((bf16[512,256]{1,0:T(8,128)(2,1)S(1)}, bf16[512,256]{1,0:T(8,128)(2,1)S(1)}, u32[]{:S(2)}, u32[]{:S(2)}) %collective-permute-start.13) | collective-permute-done | bytes 262176 | tf_op jit(solution)/shard_map/ppermute | solution.py:31
  64.9 5.0 %collective-permute-done.15.refs_3_ = bf16[512,256]{1,0:T(8,128)(2,1)S(1)} collective-permute-done((bf16[512,256]{1,0:T(8,128)(2,1)S(1)}, bf16[512,256]{1,0:T(8,128)(2,1)S(1)}, u32[]{:S(2)}, u32[]{:S(2)}) %collective-permute-start.15) | collective-permute-done | bytes 262176 | tf_op jit(solution)/shard_map/ppermute | solution.py:31
  70.2 4.7 %collective-permute-done.17.back_ref = bf16[512,256]{1,0:T(8,128)(2,1)S(1)} collective-permute-done((bf16[512,256]{1,0:T(8,128)(2,1)S(1)}, bf16[512,256]{1,0:T(8,128)(2,1)S(1)}, u32[]{:S(2)}, u32[]{:S(2)}) %collective-permute-start.17) | collective-permute-done | bytes 262176 | tf_op jit(solution)/shard_map/ppermute | solution.py:31
  76.4 0.9 %copy-done.1 = f32[16,7,7,512]{3,0,2,1:T(8,128)S(1)} copy-done((f32[16,7,7,512]{3,0,2,1:T(8,128)S(1)}, f32[16,7,7,512]{3,0,2,1:T(8,128)}, u32[]{:S(2)}) %copy-start.1) | copy-done | bytes 1605656
  77.7 3.0 %divide_subtract_fusion = (f32[16,7,7,512]{3,0,2,1:T(8,128)}, f32[16,7,7,512]{3,0,2,1:T(8,128)}, f32[16,7,7,512]{3,0,2,1:T(8,128)}) fusion(f32[16,7,7,512]{3,0,2,1:T(8,128)S(1)} %copy-done.1, f32[16,7,7,512]{3,0,2,1:T(8,128)S(1)} %bitcast.44, f32[16,7,7,512]{3,0,2,1:T(8,128)S(1)} %copy-done.2, f32[16,7,7,512]{3,0,2,1:T(8,128)S(1)} %copy-done.3), kind=kLoop, calls=%fused_computation.6 | loop fusion | flops 4816896 | bytes 11239424 | tf_op jit(solution)/shard_map/sub | solution.py:248
  (42 shorter events, 8.0 us)
Async XLA Ops:
  0.6 2.2 %copy-start = (bf16[16,16,512]{2,1,0:T(8,128)(2,1)S(1)}, bf16[16,16,512]{2,1,0:T(8,128)(2,1)}, u32[]{:S(2)}) copy-start(bf16[16,16,512]{2,1,0:T(8,128)(2,1)} %param.5) | copy-start | bytes 786436
  0.6 9.4 %copy-start.4 = (bf16[16,16,128]{2,1,0:T(8,128)(2,1)S(1)}, bf16[16,16,128]{2,1,0:T(8,128)(2,1)}, u32[]{:S(2)}) copy-start(bf16[16,16,128]{2,1,0:T(8,128)(2,1)} %param.6) | copy-start | bytes 196612
  2.2 18.3 %collective-permute-start = (bf16[49,16,512]{2,1,0:T(8,128)(2,1)S(1)}, bf16[49,16,512]{2,1,0:T(8,128)(2,1)}, u32[]{:S(2)}, u32[]{:S(2)}) collective-permute-start(bf16[49,16,512]{2,1,0:T(8,128)(2,1)S(1)} %bitcast.45), channel_id=1, source_target_pairs={{0,4},{4,0},{1,5},{5,1},{2,6},{6,2},{3,7},{7,3},{8,12},{12,8},{9,1... | collective-permute-start | bytes 2408456 | tf_op jit(solution)/shard_map/ppermute | solution.py:17
  2.8 16.5 %collective-permute-start.6 = (bf16[16,16,512]{2,1,0:T(8,128)(2,1)S(1)}, bf16[16,16,512]{2,1,0:T(8,128)(2,1)S(1)}, u32[]{:S(2)}, u32[]{:S(2)}) collective-permute-start(bf16[16,16,512]{2,1,0:T(8,128)(2,1)S(1)} %copy-done), channel_id=1, source_target_pairs={{0,2},{1,3},{2,0},{3,1},{4,6},{5,7},{6,4},{7,5},{8,10},{9,11},{10,... | collective-permute-start | bytes 786440 | tf_op jit(solution)/shard_map/ppermute | solution.py:31
  6.5 18.2 %collective-permute-start.5 = (bf16[16,16,512]{2,1,0:T(8,128)(2,1)S(1)}, bf16[16,16,512]{2,1,0:T(8,128)(2,1)S(1)}, u32[]{:S(2)}, u32[]{:S(2)}) collective-permute-start(bf16[16,16,512]{2,1,0:T(8,128)(2,1)S(1)} %copy-done), channel_id=1, source_target_pairs={{1,2},{2,1},{5,6},{6,5},{9,10},{10,9},{13,14},{14,13},{17,18},{18,... | collective-permute-start | bytes 786440 | tf_op jit(solution)/shard_map/ppermute | solution.py:31
  7.1 16.6 %collective-permute-start.8 = (bf16[16,16,512]{2,1,0:T(8,128)(2,1)S(1)}, bf16[16,16,512]{2,1,0:T(8,128)(2,1)S(1)}, u32[]{:S(2)}, u32[]{:S(2)}) collective-permute-start(bf16[16,16,512]{2,1,0:T(8,128)(2,1)S(1)} %copy-done), channel_id=1, source_target_pairs={{0,1},{1,0},{2,3},{3,2},{4,5},{5,4},{6,7},{7,6},{8,9},{9,8},{10,11... | collective-permute-start | bytes 786440 | tf_op jit(solution)/shard_map/ppermute | solution.py:31
  19.3 9.7 %collective-permute-start.7 = (bf16[256,512]{1,0:T(8,128)(2,1)S(1)}, bf16[256,512]{1,0:T(8,128)(2,1)S(1)}, u32[]{:S(2)}, u32[]{:S(2)}) collective-permute-start(bf16[256,512]{1,0:T(8,128)(2,1)S(1)} %bitcast.37), channel_id=1, source_target_pairs={{2,3},{1,0},{6,7},{5,4},{10,11},{9,8},{14,15},{13,12},{18,19},{17,... | collective-permute-start | bytes 786440 | tf_op jit(solution)/shard_map/ppermute | solution.py:31
  29.9 1.3 %collective-permute-start.9 = (f32[4,32,128]{2,1,0:T(8,128)S(1)}, f32[4,32,128]{2,1,0:T(8,128)S(1)}, u32[]{:S(2)}, u32[]{:S(2)}) collective-permute-start(f32[4,32,128]{2,1,0:T(8,128)S(1)} %get-tuple-element.36), channel_id=1, source_target_pairs={{0,4},{4,0},{1,5},{5,1},{2,6},{6,2},{3,7},{7,3},{8,12},{12,8},{9,1... | collective-permute-start | bytes 196616 | tf_op jit(solution)/shard_map/ppermute | solution.py:17
  30.0 8.0 %collective-permute-start.1 = (bf16[32,256]{1,0:T(8,128)(2,1)S(1)}, bf16[32,256]{1,0:T(8,128)(2,1)S(1)}, u32[]{:S(2)}, u32[]{:S(2)}) collective-permute-start(bf16[32,256]{1,0:T(8,128)(2,1)S(1)} %bitcast.52), channel_id=1, source_target_pairs={{0,1},{1,2},{2,3},{3,0},{4,5},{5,6},{6,7},{7,4},{8,9},{9,10},{10,1... | collective-permute-start | bytes 49160 | tf_op jit(solution)/shard_map/ppermute | solution.py:17
  31.3 12.4 %collective-permute-start.10 = (bf16[4,32,384]{2,1,0:T(8,128)(2,1)S(1)}, bf16[4,32,384]{2,1,0:T(8,128)(2,1)S(1)}, u32[]{:S(2)}, u32[]{:S(2)}) collective-permute-start(bf16[4,32,384]{2,1,0:T(8,128)(2,1)S(1)} %get-tuple-element.38), channel_id=1, source_target_pairs={{0,24},{8,16},{16,8},{24,0},{1,25},{9,17},{17,9},{25,1},{2,26},{10... | collective-permute-start | bytes 294920 | tf_op jit(solution)/shard_map/ppermute | solution.py:321
  33.6 10.1 %collective-permute-start.11 = (bf16[4,32,384]{2,1,0:T(8,128)(2,1)S(1)}, bf16[4,32,384]{2,1,0:T(8,128)(2,1)S(1)}, u32[]{:S(2)}, u32[]{:S(2)}) collective-permute-start(bf16[4,32,384]{2,1,0:T(8,128)(2,1)S(1)} %get-tuple-element.38), channel_id=1, source_target_pairs={{0,16},{8,24},{16,0},{24,8},{1,17},{9,25},{17,1},{25,9},{2,18},{10... | collective-permute-start | bytes 294920 | tf_op jit(solution)/shard_map/ppermute | solution.py:321
  34.1 9.6 %collective-permute-start.12 = (bf16[4,32,384]{2,1,0:T(8,128)(2,1)S(1)}, bf16[4,32,384]{2,1,0:T(8,128)(2,1)S(1)}, u32[]{:S(2)}, u32[]{:S(2)}) collective-permute-start(bf16[4,32,384]{2,1,0:T(8,128)(2,1)S(1)} %get-tuple-element.38), channel_id=1, source_target_pairs={{0,8},{8,0},{16,24},{24,16},{1,9},{9,1},{17,25},{25,17},{2,10},{10... | collective-permute-start | bytes 294920 | tf_op jit(solution)/shard_map/ppermute | solution.py:321
  34.8 4.9 %collective-permute-start.2 = (bf16[32,256]{1,0:T(8,128)(2,1)S(1)}, bf16[32,256]{1,0:T(8,128)(2,1)S(1)}, u32[]{:S(2)}, u32[]{:S(2)}) collective-permute-start(bf16[32,256]{1,0:T(8,128)(2,1)S(1)} %bitcast.51), channel_id=1, source_target_pairs={{0,2},{1,3},{2,0},{3,1},{4,6},{5,7},{6,4},{7,5},{8,10},{9,11},{10,... | collective-permute-start | bytes 49160 | tf_op jit(solution)/shard_map/ppermute | solution.py:17
  38.0 3.7 %collective-permute-start.3 = (bf16[32,256]{1,0:T(8,128)(2,1)S(1)}, bf16[32,256]{1,0:T(8,128)(2,1)S(1)}, u32[]{:S(2)}, u32[]{:S(2)}) collective-permute-start(bf16[32,256]{1,0:T(8,128)(2,1)S(1)} %bitcast.50), channel_id=1, source_target_pairs={{0,3},{1,0},{2,1},{3,2},{4,7},{5,4},{6,5},{7,6},{8,11},{9,8},{10,9... | collective-permute-start | bytes 49160 | tf_op jit(solution)/shard_map/ppermute | solution.py:17
  41.8 1.3 %collective-permute-start.4 = (f32[4,32,128]{2,1,0:T(8,128)S(1)}, f32[4,32,128]{2,1,0:T(8,128)S(1)}, u32[]{:S(2)}, u32[]{:S(2)}) collective-permute-start(f32[4,32,128]{2,1,0:T(8,128)S(1)} %get-tuple-element.28), channel_id=1, source_target_pairs={{0,4},{4,0},{1,5},{5,1},{2,6},{6,2},{3,7},{7,3},{8,12},{12,8},{9,1... | collective-permute-start | bytes 196616 | tf_op jit(solution)/shard_map/ppermute | solution.py:17
  49.3 26.4 %collective-permute-start.18 = (bf16[49,16,512]{2,1,0:T(8,128)(2,1)S(1)}, bf16[49,16,512]{2,1,0:T(8,128)(2,1)S(1)}, u32[]{:S(2)}, u32[]{:S(2)}) collective-permute-start(bf16[49,16,512]{2,1,0:T(8,128)(2,1)S(1)} %fusion.2), channel_id=1, source_target_pairs={{0,4},{4,0},{1,5},{5,1},{2,6},{6,2},{3,7},{7,3},{8,12},{12,8},{9,1... | collective-permute-start | bytes 2408456 | tf_op jit(solution)/shard_map/ppermute | solution.py:17
  49.5 9.8 %collective-permute-start.16 = (bf16[512,256]{1,0:T(8,128)(2,1)S(1)}, bf16[512,256]{1,0:T(8,128)(2,1)S(1)}, u32[]{:S(2)}, u32[]{:S(2)}) collective-permute-start(bf16[512,256]{1,0:T(8,128)(2,1)S(1)} %get-tuple-element.42), channel_id=1, source_target_pairs={{3,2},{0,1},{7,6},{4,5},{11,10},{8,9},{15,14},{12,13},{19,18},{16,... | collective-permute-start | bytes 786440 | tf_op jit(solution)/shard_map/ppermute | solution.py:31
  52.6 12.3 %collective-permute-start.14 = (bf16[512,256]{1,0:T(8,128)(2,1)S(1)}, bf16[512,256]{1,0:T(8,128)(2,1)S(1)}, u32[]{:S(2)}, u32[]{:S(2)}) collective-permute-start(bf16[512,256]{1,0:T(8,128)(2,1)S(1)} %get-tuple-element.42), channel_id=1, source_target_pairs={{1,2},{2,1},{5,6},{6,5},{9,10},{10,9},{13,14},{14,13},{17,18},{18,... | collective-permute-start | bytes 786440 | tf_op jit(solution)/shard_map/ppermute | solution.py:31
  53.3 11.6 %collective-permute-start.13 = (bf16[512,256]{1,0:T(8,128)(2,1)S(1)}, bf16[512,256]{1,0:T(8,128)(2,1)S(1)}, u32[]{:S(2)}, u32[]{:S(2)}) collective-permute-start(bf16[512,256]{1,0:T(8,128)(2,1)S(1)} %get-tuple-element.41), channel_id=1, source_target_pairs={{0,1},{1,0},{2,3},{3,2},{4,5},{5,4},{6,7},{7,6},{8,9},{9,8},{10,11... | collective-permute-start | bytes 786440 | tf_op jit(solution)/shard_map/ppermute | solution.py:31
  54.3 15.7 %collective-permute-start.15 = (bf16[512,256]{1,0:T(8,128)(2,1)S(1)}, bf16[512,256]{1,0:T(8,128)(2,1)S(1)}, u32[]{:S(2)}, u32[]{:S(2)}) collective-permute-start(bf16[512,256]{1,0:T(8,128)(2,1)S(1)} %get-tuple-element.43), channel_id=1, source_target_pairs={{0,2},{3,1},{4,6},{7,5},{8,10},{11,9},{12,14},{15,13},{16,18},{19,... | collective-permute-start | bytes 786440 | tf_op jit(solution)/shard_map/ppermute | solution.py:31
  59.3 15.5 %collective-permute-start.17 = (bf16[512,256]{1,0:T(8,128)(2,1)S(1)}, bf16[512,256]{1,0:T(8,128)(2,1)S(1)}, u32[]{:S(2)}, u32[]{:S(2)}) collective-permute-start(bf16[512,256]{1,0:T(8,128)(2,1)S(1)} %shard_map.97), channel_id=1, source_target_pairs={{1,3},{2,0},{5,7},{6,4},{9,11},{10,8},{13,15},{14,12},{17,19},{18,... | collective-permute-start | bytes 786440 | tf_op jit(solution)/shard_map/ppermute | solution.py:31
  74.8 1.5 %copy-start.3 = (f32[16,7,7,512]{3,0,2,1:T(8,128)S(1)}, f32[16,7,7,512]{3,0,2,1:T(8,128)}, u32[]{:S(2)}) copy-start(f32[16,7,7,512]{3,0,2,1:T(8,128)} %param.9) | copy-start | bytes 4816900
  75.7 1.5 %copy-start.1 = (f32[16,7,7,512]{3,0,2,1:T(8,128)S(1)}, f32[16,7,7,512]{3,0,2,1:T(8,128)}, u32[]{:S(2)}) copy-start(f32[16,7,7,512]{3,0,2,1:T(8,128)} %param.7) | copy-start | bytes 4816900
  75.7 2.0 %copy-start.2 = (f32[16,7,7,512]{3,0,2,1:T(8,128)S(1)}, f32[16,7,7,512]{3,0,2,1:T(8,128)}, u32[]{:S(2)}) copy-start(f32[16,7,7,512]{3,0,2,1:T(8,128)} %param.8) | copy-start | bytes 4816900
